TPU v7x, 32 devices: a whole 2x2x4 slice. The times are simulated.
32 devices in a mesh: dp: 8 (over y, x, core), tensor: 4 (over z).
Axes of the slice: x: 2, y: 2, z: 4, core: 2. Of those that a mesh axis runs over, the one named last changes fastest.
Arguments:
- tokens: bfloat16 [8, 1024, 1280], P('dp', 'tensor'), may hold values from -6 to 6
- lengths: int32 [8], P('dp'), may hold values from 256 to 1024, as said below
- cotangent: bfloat16 [8, 1024, 1280], P('dp', 'tensor'), may hold values from -6 to 6
- ln1_gain: bfloat16 [1280], P('dp'), may hold values from 0.099609375 to 1.8984375
- ln1_bias: bfloat16 [1280], P('dp'), may hold values from -3 to 3
- query_weight: bfloat16 [1280, 1280], P('dp', 'tensor'), may hold values from -0.25 to 0.25
- query_bias: bfloat16 [1280], P('tensor'), may hold values from -3 to 3
- key_weight: bfloat16 [1280, 1280], P('dp', 'tensor'), may hold values from -0.25 to 0.25
- value_weight: bfloat16 [1280, 1280], P('dp', 'tensor'), may hold values from -0.15625 to 0.15625
- value_bias: bfloat16 [1280], P('tensor'), may hold values from -3 to 3
- out_weight: bfloat16 [1280, 1280], P('dp', 'tensor'), may hold values from -1.25 to 1.25
- out_bias: bfloat16 [1280], P('dp'), may hold values from -3 to 3
- ln2_gain: bfloat16 [1280], P('dp'), may hold values from 0.099609375 to 1.8984375
- ln2_bias: bfloat16 [1280], P('dp'), may hold values from -3 to 3
- up_weight: bfloat16 [1280, 5120], P('dp', 'tensor'), may hold values from -0.15625 to 0.15625
- up_bias: bfloat16 [5120], P('tensor'), may hold values from -3 to 3
- down_weight: bfloat16 [1280, 5120], P('dp', 'tensor'), may hold values from -0.25 to 0.25
- down_bias: bfloat16 [1280], P('dp'), may hold values from -3 to 3
Outputs:
- output: bfloat16 [8, 1024, 1280], P('dp', 'tensor')
- tokens_grad: float32 [8, 1024, 1280], P('dp', 'tensor')
- ln1_gain_grad: float32 [1280], P('dp')
- ln1_bias_grad: float32 [1280], P('dp')
- query_weight_grad: float32 [1280, 1280], P('dp', 'tensor')
- query_bias_grad: float32 [1280], P('tensor')
- key_weight_grad: float32 [1280, 1280], P('dp', 'tensor')
- value_weight_grad: float32 [1280, 1280], P('dp', 'tensor')
- value_bias_grad: float32 [1280], P('tensor')
- out_weight_grad: float32 [1280, 1280], P('dp', 'tensor')
- out_bias_grad: float32 [1280], P('dp')
- ln2_gain_grad: float32 [1280], P('dp')
- ln2_bias_grad: float32 [1280], P('dp')
- up_weight_grad: float32 [1280, 5120], P('dp', 'tensor')
- up_bias_grad: float32 [5120], P('tensor')
- down_weight_grad: float32 [1280, 5120], P('dp', 'tensor')
- down_bias_grad: float32 [1280], P('dp')
Inputs may be any that keep to these rules, and one draw needn't show every extreme that they name: `lengths`: positions of a clip at or past its length are padding and are masked as keys; some clip has exactly 1024 valid positions and some exactly 256.
All inputs are finite; a program needn't handle non-finite values.
Results may differ from a plain program's by a relative error of at most 0.02.
Values may be sent and summed in bfloat16 or wider, within the bound.
No kernel may reach another device: no remote copies, remote signals or barrier semaphores. Data moves between devices by JAX's collectives and lax.ppermute only.
A program may use at most 128 MiB of HBM per device.

v0:
```python
import jax
import jax.numpy as jnp
from jax import lax
from jax.sharding import PartitionSpec as P

HEAD_DIM = 80


masked_score = -1e30


def layer_norm(values, gain, shift):
    centre = values - jnp.mean(values, axis=-1, keepdims=True)
    spread = jnp.mean(centre * centre, axis=-1, keepdims=True)
    return centre * lax.rsqrt(spread + 1e-05) * gain + shift


def masked_scores(query_part, key_rows, length, scale):
    seq = key_rows.shape[0]
    valid = lax.broadcasted_iota(jnp.int32, (seq,), 0) < length
    scores = (
        jnp.einsum("qhe,khe->hqk", query_part, key_rows, preferred_element_type=jnp.float32) * scale
    )
    return jnp.where(valid[None, None, :], scores, masked_score)


def attend_clip(query_rows, key_rows, value_rows, length, blocks):
    seq, heads = (query_rows.shape[0], query_rows.shape[1])
    scale = HEAD_DIM ** (-0.5)
    query_blocks = query_rows.reshape(blocks, seq // blocks, heads, HEAD_DIM)

    def one_block(query_part):
        scores = masked_scores(query_part, key_rows, length, scale)
        top = jnp.max(scores, axis=-1, keepdims=True)
        expo = jnp.exp(scores - top)
        total = jnp.sum(expo, axis=-1, keepdims=True)
        probs = (expo / total).astype(jnp.bfloat16)
        context = jnp.einsum(
            "hqk,khe->qhe", probs, value_rows, preferred_element_type=jnp.float32
        ).astype(jnp.bfloat16)
        return (context, (top + jnp.log(total))[..., 0])

    context, log_total = lax.map(one_block, query_blocks)
    return (context.reshape(seq, heads, HEAD_DIM), log_total)


def attend_back(query_rows, key_rows, value_rows, context_grad, log_total, length, blocks):
    seq, heads = (query_rows.shape[0], query_rows.shape[1])
    scale = HEAD_DIM ** (-0.5)
    query_blocks = query_rows.reshape(blocks, seq // blocks, heads, HEAD_DIM)
    grad_blocks = context_grad.reshape(blocks, seq // blocks, heads, HEAD_DIM)

    def one_block(carry, inputs):
        key_acc, value_acc = carry
        query_part, grad_part, lse_part = inputs
        scores = masked_scores(query_part, key_rows, length, scale)
        probs = jnp.exp(scores - lse_part[..., None])
        value_acc = value_acc + jnp.einsum(
            "hqk,qhe->khe",
            probs.astype(jnp.bfloat16),
            grad_part,
            preferred_element_type=jnp.float32,
        )
        prob_grad = jnp.einsum(
            "qhe,khe->hqk", grad_part, value_rows, preferred_element_type=jnp.float32
        )
        centred = prob_grad - jnp.sum(probs * prob_grad, axis=-1, keepdims=True)
        score_grad = (probs * centred).astype(jnp.bfloat16)
        query_grad = (
            jnp.einsum("hqk,khe->qhe", score_grad, key_rows, preferred_element_type=jnp.float32)
            * scale
        )
        key_acc = (
            key_acc
            + jnp.einsum("hqk,qhe->khe", score_grad, query_part, preferred_element_type=jnp.float32)
            * scale
        )
        return ((key_acc, value_acc), query_grad.astype(jnp.bfloat16))

    zeros = jnp.zeros((seq, heads, HEAD_DIM), jnp.float32)
    (key_acc, value_acc), query_grad = lax.scan(
        one_block, (zeros, zeros), (query_blocks, grad_blocks, log_total)
    )
    return (
        query_grad.reshape(seq, heads, HEAD_DIM),
        key_acc.astype(jnp.bfloat16),
        value_acc.astype(jnp.bfloat16),
    )


def forward_pass(tokens, lengths, weights):
    (
        ln1_gain,
        ln1_bias,
        query_weight,
        query_bias,
        key_weight,
        value_weight,
        value_bias,
        out_weight,
        out_bias,
        ln2_gain,
        ln2_bias,
        up_weight,
        up_bias,
        down_weight,
        down_bias,
    ) = weights
    query_full, key_full, value_full, out_full, gain_one, bias_one, out_shift = (
        lax.all_gather(query_weight, "dp", axis=0, tiled=True),
        lax.all_gather(key_weight, "dp", axis=0, tiled=True),
        lax.all_gather(value_weight, "dp", axis=0, tiled=True),
        lax.all_gather(out_weight, "dp", axis=0, tiled=True),
        lax.all_gather(ln1_gain, "dp", axis=0, tiled=True),
        lax.all_gather(ln1_bias, "dp", axis=0, tiled=True),
        lax.all_gather(out_bias, "dp", axis=0, tiled=True),
    )
    gain_one = gain_one.astype(jnp.float32)
    bias_one = bias_one.astype(jnp.float32)
    rows = tokens.astype(jnp.float32)
    normed = layer_norm(rows, gain_one, bias_one).astype(jnp.bfloat16)
    normed_all = lax.all_gather(normed, "tensor", axis=1, tiled=True)
    clips, seq = (normed_all.shape[0], normed_all.shape[1])
    heads = query_full.shape[1] // HEAD_DIM
    blocks = seq // 512
    shaped = (clips, seq, heads, HEAD_DIM)
    queries = (
        (
            jnp.einsum("csd,dh->csh", normed_all, query_full, preferred_element_type=jnp.float32)
            + query_bias.astype(jnp.float32)
        )
        .astype(jnp.bfloat16)
        .reshape(shaped)
    )
    keyed = (
        jnp.einsum("csd,dh->csh", normed_all, key_full, preferred_element_type=jnp.float32)
        .astype(jnp.bfloat16)
        .reshape(shaped)
    )
    valued = (
        (
            jnp.einsum("csd,dh->csh", normed_all, value_full, preferred_element_type=jnp.float32)
            + value_bias.astype(jnp.float32)
        )
        .astype(jnp.bfloat16)
        .reshape(shaped)
    )

    def clip_attend(item):
        return attend_clip(item[0], item[1], item[2], item[3], blocks)

    context, log_total = lax.map(clip_attend, (queries, keyed, valued, lengths))
    context = context.reshape(clips, seq, heads * HEAD_DIM)
    attn_terms = jnp.einsum("csh,dh->csd", context, out_full, preferred_element_type=jnp.float32)
    attended = lax.psum_scatter(
        attn_terms.astype(jnp.bfloat16), "tensor", scatter_dimension=1, tiled=True
    ).astype(jnp.float32)
    middle = rows + attended + out_shift.astype(jnp.float32)
    up_full, down_full, gain_two, bias_two, down_shift = (
        lax.all_gather(up_weight, "dp", axis=0, tiled=True),
        lax.all_gather(down_weight, "dp", axis=0, tiled=True),
        lax.all_gather(ln2_gain, "dp", axis=0, tiled=True),
        lax.all_gather(ln2_bias, "dp", axis=0, tiled=True),
        lax.all_gather(down_bias, "dp", axis=0, tiled=True),
    )
    gain_two = gain_two.astype(jnp.float32)
    bias_two = bias_two.astype(jnp.float32)
    normed_two = layer_norm(middle, gain_two, bias_two).astype(jnp.bfloat16)
    normed_two_all = lax.all_gather(normed_two, "tensor", axis=1, tiled=True)
    hidden_pre = jnp.einsum(
        "csd,df->csf", normed_two_all, up_full, preferred_element_type=jnp.float32
    ) + up_bias.astype(jnp.float32)
    hidden = jax.nn.gelu(hidden_pre, approximate=False).astype(jnp.bfloat16)
    mlp_terms = jnp.einsum("csf,df->csd", hidden, down_full, preferred_element_type=jnp.float32)
    mixed = lax.psum_scatter(
        mlp_terms.astype(jnp.bfloat16), "tensor", scatter_dimension=1, tiled=True
    ).astype(jnp.float32)
    output = middle + mixed + down_shift.astype(jnp.float32)
    return {
        "output": output,
        "rows": rows,
        "normed_all": normed_all,
        "queries": queries,
        "keyed": keyed,
        "valued": valued,
        "context": context,
        "log_total": log_total,
        "middle": middle,
        "normed_two_all": normed_two_all,
        "hidden_pre": hidden_pre,
        "hidden": hidden,
        "query_full": query_full,
        "key_full": key_full,
        "value_full": value_full,
        "out_full": out_full,
        "up_full": up_full,
        "down_full": down_full,
        "gain_one": gain_one,
        "bias_one": bias_one,
        "gain_two": gain_two,
        "bias_two": bias_two,
        "blocks": blocks,
    }


def local(
    tokens,
    lengths,
    cotangent,
    ln1_gain,
    ln1_bias,
    query_weight,
    query_bias,
    key_weight,
    value_weight,
    value_bias,
    out_weight,
    out_bias,
    ln2_gain,
    ln2_bias,
    up_weight,
    up_bias,
    down_weight,
    down_bias,
):
    weights = (
        ln1_gain,
        ln1_bias,
        query_weight,
        query_bias,
        key_weight,
        value_weight,
        value_bias,
        out_weight,
        out_bias,
        ln2_gain,
        ln2_bias,
        up_weight,
        up_bias,
        down_weight,
        down_bias,
    )
    first = forward_pass(tokens, lengths, weights)
    fenced_tokens, fenced_lengths, fenced_weights, fenced_output = lax.optimization_barrier(
        (tokens, lengths, weights, first["output"])
    )
    saved = forward_pass(fenced_tokens, fenced_lengths, fenced_weights)
    blocks = saved["blocks"]
    grad_out = cotangent.astype(jnp.float32)
    down_shift_grad = jnp.sum(grad_out, axis=(0, 1))
    grad_out_all = lax.all_gather(cotangent, "tensor", axis=1, tiled=True)
    down_grad = jnp.einsum(
        "csd,csf->df", grad_out_all, saved["hidden"], preferred_element_type=jnp.float32
    )
    hidden_grad = jnp.einsum(
        "csd,df->csf", grad_out_all, saved["down_full"], preferred_element_type=jnp.float32
    )
    gelu_pull = jax.vjp(lambda pre: jax.nn.gelu(pre, approximate=False), saved["hidden_pre"])[1]
    pre_grad = gelu_pull(hidden_grad)[0].astype(jnp.bfloat16)
    up_shift_grad = jnp.sum(pre_grad, axis=(0, 1), dtype=jnp.float32)
    up_grad = jnp.einsum(
        "csd,csf->df", saved["normed_two_all"], pre_grad, preferred_element_type=jnp.float32
    )
    up_grad_shard, down_grad_shard = (
        lax.psum_scatter(
            up_grad.astype(jnp.bfloat16), "dp", scatter_dimension=0, tiled=True
        ).astype(jnp.float32),
        lax.psum_scatter(
            down_grad.astype(jnp.bfloat16), "dp", scatter_dimension=0, tiled=True
        ).astype(jnp.float32),
    )
    normed_two_terms = jnp.einsum(
        "csf,df->csd", pre_grad, saved["up_full"], preferred_element_type=jnp.float32
    )
    normed_two_grad = lax.psum_scatter(
        normed_two_terms.astype(jnp.bfloat16), "tensor", scatter_dimension=1, tiled=True
    ).astype(jnp.float32)
    norm_pull = jax.vjp(layer_norm, saved["middle"], saved["gain_two"], saved["bias_two"])[1]
    middle_part, gain_two_grad, bias_two_grad = norm_pull(normed_two_grad)
    middle_grad = grad_out + middle_part
    out_shift_grad = jnp.sum(middle_grad, axis=(0, 1))
    middle_all = lax.all_gather(middle_grad.astype(jnp.bfloat16), "tensor", axis=1, tiled=True)
    out_grad = jnp.einsum(
        "csd,csh->dh", middle_all, saved["context"], preferred_element_type=jnp.float32
    )
    context_grad = jnp.einsum(
        "csd,dh->csh", middle_all, saved["out_full"], preferred_element_type=jnp.float32
    ).astype(jnp.bfloat16)
    queries = saved["queries"]
    clips, seq, heads = (queries.shape[0], queries.shape[1], queries.shape[2])

    def clip_back(item):
        return attend_back(item[0], item[1], item[2], item[3], item[4], item[5], blocks)

    query_grad, key_grad, value_grad = lax.map(
        clip_back,
        (
            queries,
            saved["keyed"],
            saved["valued"],
            context_grad.reshape(clips, seq, heads, HEAD_DIM),
            saved["log_total"],
            lengths,
        ),
    )
    flat = (clips, seq, heads * HEAD_DIM)
    query_grad = query_grad.reshape(flat)
    key_grad = key_grad.reshape(flat)
    value_grad = value_grad.reshape(flat)
    normed_all = saved["normed_all"]
    query_weight_grad = jnp.einsum(
        "csd,csh->dh", normed_all, query_grad, preferred_element_type=jnp.float32
    )
    key_weight_grad = jnp.einsum(
        "csd,csh->dh", normed_all, key_grad, preferred_element_type=jnp.float32
    )
    value_weight_grad = jnp.einsum(
        "csd,csh->dh", normed_all, value_grad, preferred_element_type=jnp.float32
    )
    query_shift_grad = jnp.sum(query_grad, axis=(0, 1), dtype=jnp.float32)
    value_shift_grad = jnp.sum(value_grad, axis=(0, 1), dtype=jnp.float32)
    normed_terms = (
        jnp.einsum(
            "csh,dh->csd", query_grad, saved["query_full"], preferred_element_type=jnp.float32
        )
        + jnp.einsum("csh,dh->csd", key_grad, saved["key_full"], preferred_element_type=jnp.float32)
        + jnp.einsum(
            "csh,dh->csd", value_grad, saved["value_full"], preferred_element_type=jnp.float32
        )
    )
    normed_grad = lax.psum_scatter(
        normed_terms.astype(jnp.bfloat16), "tensor", scatter_dimension=1, tiled=True
    ).astype(jnp.float32)
    first_pull = jax.vjp(layer_norm, saved["rows"], saved["gain_one"], saved["bias_one"])[1]
    tokens_part, gain_one_grad, bias_one_grad = first_pull(normed_grad)
    tokens_grad = middle_grad + tokens_part
    summed = lax.psum(
        (
            gain_one_grad,
            bias_one_grad,
            out_shift_grad,
            gain_two_grad,
            bias_two_grad,
            down_shift_grad,
        ),
        "tensor",
    )
    owned = (
        lax.psum_scatter(
            query_weight_grad.astype(jnp.bfloat16), "dp", scatter_dimension=0, tiled=True
        ).astype(jnp.float32),
        lax.psum_scatter(
            key_weight_grad.astype(jnp.bfloat16), "dp", scatter_dimension=0, tiled=True
        ).astype(jnp.float32),
        lax.psum_scatter(
            value_weight_grad.astype(jnp.bfloat16), "dp", scatter_dimension=0, tiled=True
        ).astype(jnp.float32),
        lax.psum_scatter(
            out_grad.astype(jnp.bfloat16), "dp", scatter_dimension=0, tiled=True
        ).astype(jnp.float32),
        lax.psum_scatter(
            summed[0].astype(jnp.bfloat16), "dp", scatter_dimension=0, tiled=True
        ).astype(jnp.float32),
        lax.psum_scatter(
            summed[1].astype(jnp.bfloat16), "dp", scatter_dimension=0, tiled=True
        ).astype(jnp.float32),
        lax.psum_scatter(
            summed[2].astype(jnp.bfloat16), "dp", scatter_dimension=0, tiled=True
        ).astype(jnp.float32),
        lax.psum_scatter(
            summed[3].astype(jnp.bfloat16), "dp", scatter_dimension=0, tiled=True
        ).astype(jnp.float32),
        lax.psum_scatter(
            summed[4].astype(jnp.bfloat16), "dp", scatter_dimension=0, tiled=True
        ).astype(jnp.float32),
        lax.psum_scatter(
            summed[5].astype(jnp.bfloat16), "dp", scatter_dimension=0, tiled=True
        ).astype(jnp.float32),
    )
    shared = lax.psum((query_shift_grad, value_shift_grad, up_shift_grad), "dp")
    return (
        first["output"].astype(jnp.bfloat16),
        tokens_grad,
        owned[4],
        owned[5],
        owned[0],
        shared[0],
        owned[1],
        owned[2],
        shared[1],
        owned[3],
        owned[6],
        owned[7],
        owned[8],
        up_grad_shard,
        shared[2],
        down_grad_shard,
        owned[9],
    )


def solution(mesh):
    placed = (
        P("dp", "tensor", None),
        P("dp"),
        P("dp", "tensor", None),
        P("dp"),
        P("dp"),
        P("dp", "tensor"),
        P("tensor"),
        P("dp", "tensor"),
        P("dp", "tensor"),
        P("tensor"),
        P("dp", "tensor"),
        P("dp"),
        P("dp"),
        P("dp"),
        P("dp", "tensor"),
        P("tensor"),
        P("dp", "tensor"),
        P("dp"),
    )
    return jax.shard_map(
        local,
        mesh=mesh,
        in_specs=placed,
        out_specs=(
            P("dp", "tensor", None),
            P("dp", "tensor", None),
            P("dp"),
            P("dp"),
            P("dp", "tensor"),
            P("tensor"),
            P("dp", "tensor"),
            P("dp", "tensor"),
            P("tensor"),
            P("dp", "tensor"),
            P("dp"),
            P("dp"),
            P("dp"),
            P("dp", "tensor"),
            P("tensor"),
            P("dp", "tensor"),
            P("dp"),
        ),
        check_vma=False,
    )
```

profile of v0, /device:TPU:0, one launch (start us, length us, event | category | flops | bytes accessed | tf_op | source)
XLA Modules:
  0.0 1138.2 jit_solution(9833556908998333741)
XLA Ops:
  15.2 25.5 %all-reduce.21 = (bf16[1280]{0:T(1024)(128)(2,1)S(1)}, bf16[1280]{0:T(1024)(128)(2,1)S(1)}, bf16[1280]{0:T(1024)(128)(2,1)S(1)}, bf16[1280]{0:T(1024)(128)(2,1)S...) all-reduce(bf16[1280]{0:T(1024)(128)(2,1)S(1)} %dynamic-update-slic, ...), channel_id=1, replica_groups=mesh['dp'=8,'tensor'=4] {'dp'}, use_global_device_ids=true, to_apply=%add.1 | all-reduce | flops 7680 | bytes 30720
  45.8 10.9 all_gather.90
  56.7 11.0 all_gather.92
  67.8 11.6 %all_gather.91 = bf16[1280,320]{1,0:T(8,128)(2,1)} all-gather(bf16[160,320]{1,0:T(8,128)(2,1)S(1)} %copy-done.25), channel_id=1, replica_groups=mesh['dp'=8,'tensor'=4] {'dp'}, dimensions={0}, use_global_device_ids=true | all-gather | bytes 921600 | tf_op jit(solution)/shard_map/all_gather | solution.py:111
  109.7 25.4 %while.64 = (s32[]{:T(128)}, bf16[2,512,4,80]{1,3,2,0:T(8,128)(2,1)S(1)}, s32[]{:T(128)}, bf16[2,512,4,80]{1,3,2,0:T(8,128)(2,1)S(1)}, bf16[1024,4,80]{0,2,1:T(8...) while((s32[]{:T(128)}, bf16[2,512,4,80]{1,3,2,0:T(8,128)(2,1)S(1)}, s32[]{:T(128)}, ...), condition=%wide.region_5.6_spmd, body=%wide.region_2.5_spmd.sunk | while | flops 683837440 | bytes 21383284 | solution.py:43
  140.3 49.8 %reduce-scatter.14.cloned.1.call-done = bf16[1,256,1280]{2,1,0:T(8,128)(2,1)} async-done(((bf16[1,1024,1280]{2,1,0:T(8,128)(2,1)}), bf16[1,256,1280]{2,1,0:T(8,128)(2,1)}) %reduce-scatter.14.cloned.1.call-update) | async-done | bytes 655376 | tf_op jit(solution)/shard_map/reduce_scatter | solution.py:155
  195.8 11.6 %all-gather.17.cloned.1.call-done = bf16[1280,1280]{1,0:T(8,128)(2,1)} async-done(((bf16[160,1280]{1,0:T(8,128)(2,1)}), bf16[1280,1280]{1,0:T(8,128)(2,1)}) %all-gather.17.cloned.1.call-update) | async-done | bytes 3276816 | tf_op jit(solution)/shard_map/all_gather | solution.py:161
  207.3 56.7 %all-gather.13.cloned.1.call-done = bf16[1,1024,1280]{2,1,0:T(8,128)(2,1)} async-done(((bf16[1,256,1280]{2,1,0:T(8,128)(2,1)}), bf16[1,1024,1280]{2,1,0:T(8,128)(2,1)}) %all-gather.13.cloned.1.call-update) | async-done | bytes 2621456 | tf_op jit(solution)/shard_map/all_gather | solution.py:169
  264.0 21.3 %fusion.96 = bf16[1,1024,1280]{2,1,0:T(8,128)(2,1)} fusion(bf16[1280,1280]{1,0:T(8,128)(2,1)} %all-gather.17.cloned.1.call-done, bf16[1280,1280]{1,0:T(8,128)(2,1)} %all-gather.15.cloned.1.call-done, bf16[1,1024,1280]{2,1,0:T(8,128)(2,1)} %all-gather.13.cloned.1.call-done, f32[1280]{0:T(1024)S(1)} %convert_element_type.308), kind=kOutput, calls=%fused_computation.127 | convolution fusion | flops 6798704640 | bytes 11801600 | tf_op jit(solution)/shard_map/csf,df->csd/dot_general | solution.py:174
  285.5 50.9 %reduce-scatter.16.cloned.1.call-done = bf16[1,256,1280]{2,1,0:T(8,128)(2,1)} async-done(((bf16[1,1024,1280]{2,1,0:T(8,128)(2,1)}), bf16[1,256,1280]{2,1,0:T(8,128)(2,1)}) %reduce-scatter.16.cloned.1.call-update) | async-done | bytes 655376 | tf_op jit(solution)/shard_map/reduce_scatter | solution.py:175
  340.5 23.8 %all-reduce.20 = (bf16[1280]{0:T(1024)(128)(2,1)S(1)}, bf16[1280]{0:T(1024)(128)(2,1)S(1)}, bf16[1280]{0:T(1024)(128)(2,1)S(1)}, bf16[1280]{0:T(1024)(128)(2,1)S(1)}, bf16[1280]{0:T(1024)(128)(2,1)S(1)}) all-reduce(bf16[1280]{0:T(1024)(128)(2,1)S(1)} %dynamic-update-slice.10, ...), channel_id=1, replica_groups=mesh['dp'=8,'tensor'=4] {'dp'}, use_global_device_ids=true, to_apply=%add.10 | all-reduce | flops 6400 | bytes 25600
  365.6 10.9 all_gather.106
  376.5 11.0 all_gather.105
  397.8 12.1 %all_gather.107 = bf16[1280,320]{1,0:T(8,128)(2,1)} all-gather(bf16[160,320]{1,0:T(8,128)(2,1)S(1)} %copy-done.29), channel_id=1, replica_groups=mesh['dp'=8,'tensor'=4] {'dp'}, dimensions={0}, use_global_device_ids=true | all-gather | bytes 921600 | tf_op jit(solution)/shard_map/all_gather | solution.py:113
  430.5 13.7 %while.65 = (s32[]{:T(128)}, bf16[2,512,4,80]{1,3,2,0:T(8,128)(2,1)S(1)}, f32[2,4,512]{2,1,0:T(4,128)S(1)}, s32[]{:T(128)}, bf16[2,512,4,80]{1,3,2,0:T(8,128)(2,...) while((s32[]{:T(128)}, ...), condition=%wide.region_15.16_spmd, body=%wide.region_12.15_spmd.sunk | while | flops 696417280 | bytes 27201636 | solution.py:43
  451.0 50.2 %reduce-scatter.18.cloned.1.call-done = bf16[1,256,1280]{2,1,0:T(8,128)(2,1)} async-done(((bf16[1,1024,1280]{2,1,0:T(8,128)(2,1)}), bf16[1,256,1280]{2,1,0:T(8,128)(2,1)}) %reduce-scatter.18.cloned.1.call-update) | async-done | bytes 655376 | tf_op jit(solution)/shard_map/reduce_scatter | solution.py:155
  507.6 27.8 %all-gather.23.cloned.1.call-done = bf16[1280,1280]{1,0:T(8,128)(2,1)} async-done(((bf16[160,1280]{1,0:T(8,128)(2,1)}), bf16[1280,1280]{1,0:T(8,128)(2,1)}) %all-gather.23.cloned.1.call-update) | async-done | bytes 3276816 | tf_op jit(solution)/shard_map/all_gather | solution.py:160
  535.4 56.8 %all-gather.21.cloned.1.call-done = bf16[1,1024,1280]{2,1,0:T(8,128)(2,1)} async-done(((bf16[1,256,1280]{2,1,0:T(8,128)(2,1)}), bf16[1,1024,1280]{2,1,0:T(8,128)(2,1)}) %all-gather.21.cloned.1.call-update) | async-done | bytes 2621456 | tf_op jit(solution)/shard_map/all_gather | solution.py:169
  592.3 17.6 %fusion.75 = (f32[1024,1280]{1,0:T(8,128)}, f32[1024,1280]{1,0:T(8,128)}) fusion(f32[1280]{0:T(1024)S(1)} %convert_element_type.332, bf16[1280,1280]{1,0:T(8,128)(2,1)} %all-gather.23.cloned.1.call-done, bf16[1,1024,1280]{2,1,0:T(8,128)(2,1)} %all-gather.21.cloned.1.call-done), kind=kOutput, calls=%fused_computation.81 | convolution fusion | flops 3438018560 | bytes 16389120 | tf_op jit(solution)/shard_map/csd,df->csf/dot_general | solution.py:170
  609.9 37.3 %all-gather.27.cloned.1.call-done = bf16[1,1024,1280]{2,1,0:T(8,128)(2,1)} async-done(((bf16[1,256,1280]{2,1,0:T(8,128)(2,1)}), bf16[1,1024,1280]{2,1,0:T(8,128)(2,1)}) %all-gather.27.cloned.1.call-update) | async-done | bytes 2621456 | tf_op jit(solution)/shard_map/all_gather | solution.py:251
  647.1 33.2 %all-gather.25.cloned.1.call-done = bf16[1280,1280]{1,0:T(8,128)(2,1)} async-done(((bf16[160,1280]{1,0:T(8,128)(2,1)}), bf16[1280,1280]{1,0:T(8,128)(2,1)}) %all-gather.25.cloned.1.call-update) | async-done | bytes 3276816 | tf_op jit(solution)/shard_map/all_gather | solution.py:161
  680.4 11.4 convert_reduce_fusion
  698.2 52.2 %reduce-scatter.20.cloned.1.call-done = bf16[1,256,1280]{2,1,0:T(8,128)(2,1)} async-done(((bf16[1,1024,1280]{2,1,0:T(8,128)(2,1)}), bf16[1,256,1280]{2,1,0:T(8,128)(2,1)}) %reduce-scatter.20.cloned.1.call-update) | async-done | bytes 655376 | tf_op jit(solution)/shard_map/reduce_scatter | solution.py:275
  783.2 30.0 %all-gather.29.cloned.1.call-done = bf16[1,1024,1280]{2,1,0:T(8,128)(2,1)} async-done(((bf16[1,256,1280]{2,1,0:T(8,128)(2,1)}), bf16[1,1024,1280]{2,1,0:T(8,128)(2,1)}) %all-gather.29.cloned.1.call-update) | async-done | bytes 2621456 | tf_op jit(solution)/shard_map/all_gather | solution.py:282
  823.2 41.3 %while.66 = (s32[]{:T(128)}, f32[1024,4,80]{0,2,1:T(8,128)S(1)}, f32[1024,4,80]{0,2,1:T(8,128)}, bf16[2,512,4,80]{1,3,2,0:T(8,128)(2,1)}, bf16[2,512,4,80]{1,3,2...) while((s32[]{:T(128)}, f32[1024,4,80]{0,2,1:T(8,128)S(1)}, ...), condition=%wide.region_24.25_spmd.clone, body=%wide.region_22.24_spmd.clone.sunk | while | flops 1711143936 | bytes 144175888 | solution.py:81
  899.7 24.7 %all-reduce.17 = (f32[320]{0:T(512)}, f32[320]{0:T(512)}, f32[1280]{0:T(1024)}) all-reduce(f32[320]{0:T(512)S(1)} %reduce_sum.247, f32[320]{0:T(512)S(1)} %reduce_sum.249, f32[1280]{0:T(1024)S(1)} %copy-done.43), channel_id=1, replica_groups=mesh['dp'=8,'tensor'=4] {'dp'}, use_global_device_ids=true, to_apply=%region_36.37 | all-reduce | flops 1920 | bytes 15360 | tf_op jit(solution)/shard_map/psum | solution.py:380
  926.0 23.7 %reduce-scatter.26.cloned.1.call-done = bf16[160,320]{1,0:T(8,128)(2,1)} async-done(((bf16[1280,320]{1,0:T(8,128)(2,1)}), bf16[160,320]{1,0:T(8,128)(2,1)}) %reduce-scatter.26.cloned.1.call-update) | async-done | bytes 102416 | tf_op jit(solution)/shard_map/reduce_scatter | solution.py:352
  951.2 37.2 %reduce-scatter.30.cloned.1.call-done = bf16[160,320]{1,0:T(8,128)(2,1)} async-done(((bf16[1280,320]{1,0:T(8,128)(2,1)}), bf16[160,320]{1,0:T(8,128)(2,1)}) %reduce-scatter.30.cloned.1.call-update) | async-done | bytes 102416 | tf_op jit(solution)/shard_map/reduce_scatter | solution.py:358
  990.1 37.6 %reduce-scatter.24.cloned.1.call-done = bf16[160,320]{1,0:T(8,128)(2,1)} async-done(((bf16[1280,320]{1,0:T(8,128)(2,1)}), bf16[160,320]{1,0:T(8,128)(2,1)}) %reduce-scatter.24.cloned.1.call-update) | async-done | bytes 102416 | tf_op jit(solution)/shard_map/reduce_scatter | solution.py:349
  1029.3 52.9 %reduce-scatter.22.cloned.1.call-done = bf16[1,256,1280]{2,1,0:T(8,128)(2,1)} async-done(((bf16[1,1024,1280]{2,1,0:T(8,128)(2,1)}), bf16[1,256,1280]{2,1,0:T(8,128)(2,1)}) %reduce-scatter.22.cloned.1.call-update) | async-done | bytes 655376 | tf_op jit(solution)/shard_map/reduce_scatter | solution.py:331
  1085.6 17.8 %all-reduce.18 = (bf16[1280]{0:T(1024)(128)(2,1)S(1)}, bf16[1280]{0:T(1024)(128)(2,1)S(1)}, bf16[1280]{0:T(1024)(128)(2,1)S(1)}, bf16[1280]{0:T(1024)(128)(2,1)S...) all-reduce(f32[1280]{0:T(1024)S(1)} %get-tuple-element.403, ...), channel_id=1, replica_groups=mesh['dp'=8,'tensor'=4] {'tensor'}, use_global_device_ids=true, to_apply=%region_29.30 | all-reduce | flops 7680 | bytes 46080 | tf_op jit(solution)/shard_map/psum | solution.py:337
  1103.3 22.4 %all-reduce.19 = (bf16[1280]{0:T(1024)(128)(2,1)S(1)}, bf16[1280]{0:T(1024)(128)(2,1)S(1)}, bf16[1280]{0:T(1024)(128)(2,1)S(1)}, bf16[1280]{0:T(1024)(128)(2,1)S...) all-reduce(bf16[1280]{0:T(1024)(128)(2,1)S(1)} %get-tuple-element.4, ...), channel_id=7, replica_groups=mesh['dp'=8,'tensor'=4] {'dp'}, use_global_device_ids=true, to_apply=%region_30.31.clone | all-reduce | flops 7680 | bytes 30720
  (333 shorter events, 279.6 us)
Async XLA Ops:
  8.1 92.0 %all-gather.11.cloned.1.call-start = ((), (), s32[]{:S(2)}) async-start(), calls=%async_computation.11 | async-start | bytes 3276800 | tf_op jit(solution)/shard_map/all_gather | solution.py:122
  45.7 144.3 %reduce-scatter.14.cloned.1.call-start = ((), (), s32[]{:S(2)}) async-start(), calls=%async_computation.12 | async-start | bytes 3276800 | tf_op jit(solution)/shard_map/reduce_scatter | solution.py:155
  139.0 56.7 %all-gather.15.cloned.1.call-start = ((), (), s32[]{:S(2)}) async-start(), calls=%async_computation.14 | async-start | bytes 3686400 | tf_op jit(solution)/shard_map/all_gather | solution.py:160
  139.6 67.7 %all-gather.17.cloned.1.call-start = ((), (), s32[]{:S(2)}) async-start(), calls=%async_computation.15 | async-start | bytes 3686400 | tf_op jit(solution)/shard_map/all_gather | solution.py:161
  140.2 123.8 %all-gather.13.cloned.1.call-start = ((), (), s32[]{:S(2)}) async-start(), calls=%async_computation.13 | async-start | bytes 3276800 | tf_op jit(solution)/shard_map/all_gather | solution.py:169
  195.3 141.2 %reduce-scatter.16.cloned.1.call-start = ((), (), s32[]{:S(2)}) async-start(), calls=%async_computation.16 | async-start | bytes 3276800 | tf_op jit(solution)/shard_map/reduce_scatter | solution.py:175
  195.7 140.7 %copy-start.9 = (bf16[1,256,1280]{2,1,0:T(8,128)(2,1)S(1)}, bf16[1,256,1280]{2,1,0:T(8,128)(2,1)}, u32[]{:S(2)}) copy-start(bf16[1,256,1280]{2,1,0:T(8,128)(2,1)} %reduce-scatter.14.cloned.1.call-done) | copy-start | bytes 1966084
  285.4 133.1 %all-gather.19.cloned.1.call-start = ((), (), s32[]{:S(2)}) async-start(), calls=%async_computation.17 | async-start | bytes 3276800 | tf_op jit(solution)/shard_map/all_gather | solution.py:122
  365.5 135.7 %reduce-scatter.18.cloned.1.call-start = ((), (), s32[]{:S(2)}) async-start(), calls=%async_computation.18 | async-start | bytes 3276800 | tf_op jit(solution)/shard_map/reduce_scatter | solution.py:155
  450.2 85.2 %all-gather.23.cloned.1.call-start = ((), (), s32[]{:S(2)}) async-start(), calls=%async_computation.20 | async-start | bytes 3686400 | tf_op jit(solution)/shard_map/all_gather | solution.py:160
  451.0 141.3 %all-gather.21.cloned.1.call-start = ((), (), s32[]{:S(2)}) async-start(), calls=%async_computation.19 | async-start | bytes 3276800 | tf_op jit(solution)/shard_map/all_gather | solution.py:169
  506.4 140.7 %all-gather.27.cloned.1.call-start = ((), (), s32[]{:S(2)}) async-start(), calls=%async_computation.22 | async-start | bytes 3276800 | tf_op jit(solution)/shard_map/all_gather | solution.py:251
  507.0 173.4 %all-gather.25.cloned.1.call-start = ((), (), s32[]{:S(2)}) async-start(), calls=%async_computation.21 | async-start | bytes 3686400 | tf_op jit(solution)/shard_map/all_gather | solution.py:161
  507.6 242.8 %reduce-scatter.20.cloned.1.call-start = ((), (), s32[]{:S(2)}) async-start(), calls=%async_computation.23 | async-start | bytes 3276800 | tf_op jit(solution)/shard_map/reduce_scatter | solution.py:275
  698.2 115.0 %all-gather.29.cloned.1.call-start = ((), (), s32[]{:S(2)}) async-start(), calls=%async_computation.24 | async-start | bytes 3276800 | tf_op jit(solution)/shard_map/all_gather | solution.py:282
  758.6 135.2 %reduce-scatter.34.cloned.1.call-start = ((), (), s32[]{:S(2)}) async-start(), calls=%async_computation.31 | async-start | bytes 3686400
  774.9 121.3 %reduce-scatter.32.cloned.1.call-start = ((), (), s32[]{:S(2)}) async-start(), calls=%async_computation.30 | async-start | bytes 3686400 | tf_op jit(solution)/shard_map/reduce_scatter | solution.py:265
  782.9 141.4 %reduce-scatter.28.cloned.1.call-start = ((), (), s32[]{:S(2)}) async-start(), calls=%async_computation.28 | async-start | bytes 1105920 | tf_op jit(solution)/shard_map/reduce_scatter | solution.py:355
  871.1 78.6 %reduce-scatter.26.cloned.1.call-start = ((), (), s32[]{:S(2)}) async-start(), calls=%async_computation.27 | async-start | bytes 1105920 | tf_op jit(solution)/shard_map/reduce_scatter | solution.py:352
  875.8 112.6 %reduce-scatter.30.cloned.1.call-start = ((), (), s32[]{:S(2)}) async-start(), calls=%async_computation.29 | async-start | bytes 1105920 | tf_op jit(solution)/shard_map/reduce_scatter | solution.py:358
  880.2 147.5 %reduce-scatter.24.cloned.1.call-start = ((), (), s32[]{:S(2)}) async-start(), calls=%async_computation.26 | async-start | bytes 1105920 | tf_op jit(solution)/shard_map/reduce_scatter | solution.py:349
  886.5 195.6 %reduce-scatter.22.cloned.1.call-start = ((), (), s32[]{:S(2)}) async-start(), calls=%async_computation.25 | async-start | bytes 3276800 | tf_op jit(solution)/shard_map/reduce_scatter | solution.py:331
  893.0 189.2 %copy-start.3 = (bf16[1,256,1280]{2,1,0:T(8,128)(2,1)S(1)}, bf16[1,256,1280]{2,1,0:T(8,128)(2,1)}, u32[]{:S(2)}) copy-start(bf16[1,256,1280]{2,1,0:T(8,128)(2,1)} %param.24) | copy-start | bytes 1966084
  893.0 189.2 %copy-start.31 = (f32[1280]{0:T(1024)S(1)}, f32[1280]{0:T(1024)}, u32[]{:S(2)}) copy-start(f32[1280]{0:T(1024)} %copy-done.30) | copy-start | bytes 15364
  893.0 189.2 %copy-start.33 = (f32[256]{0:T(256)S(1)}, f32[256]{0:T(256)}, u32[]{:S(2)}) copy-start(f32[256]{0:T(256)} %copy-done.32) | copy-start | bytes 3076
  895.0 188.7 %copy-start.42 = (f32[256]{0:T(256)S(1)}, f32[256]{0:T(256)}, u32[]{:S(2)}) copy-start(f32[256]{0:T(256)} %copy-done.41) | copy-start | bytes 3076
  895.0 188.7 %copy-start.40 = (f32[256]{0:T(256)S(1)}, f32[256]{0:T(256)}, u32[]{:S(2)}) copy-start(f32[256]{0:T(256)} %copy-done.39) | copy-start | bytes 3076
  896.1 189.4 %copy-start.34 = (f32[1280]{0:T(1024)S(1)}, f32[1280]{0:T(1024)}, u32[]{:S(2)}) copy-start(f32[1280]{0:T(1024)} %get-tuple-element.405) | copy-start | bytes 15364
  896.1 189.4 %copy-start.35 = (f32[1280]{0:T(1024)S(1)}, f32[1280]{0:T(1024)}, u32[]{:S(2)}) copy-start(f32[1280]{0:T(1024)} %get-tuple-element.401) | copy-start | bytes 15364
  896.1 189.4 %copy-start.36 = (f32[1280]{0:T(1024)S(1)}, f32[1280]{0:T(1024)}, u32[]{:S(2)}) copy-start(f32[1280]{0:T(1024)} %get-tuple-element.483) | copy-start | bytes 15364
  896.1 189.4 %copy-start.37 = (f32[1280]{0:T(1024)S(1)}, f32[1280]{0:T(1024)}, u32[]{:S(2)}) copy-start(f32[1280]{0:T(1024)} %get-tuple-element.491) | copy-start | bytes 15364
  896.1 231.6 %copy-start.8 = (f32[1,256,1280]{2,1,0:T(8,128)S(1)}, f32[1,256,1280]{2,1,0:T(8,128)}, u32[]{:S(2)}) copy-start(f32[1,256,1280]{2,1,0:T(8,128)} %copy-done.7) | copy-start | bytes 3932164
  (52 other events, 1320.1 us)
Sparse Core Ops, SparseCore 0:
  45.8 54.1 all-gather.10
  139.1 50.8 reduce-scatter.13
  285.5 50.8 reduce-scatter.15
  365.6 52.9 all-gather.18
  698.3 52.0 reduce-scatter.19
  758.7 54.4 all-gather.28
Sparse Core Ops, SparseCore 1:
  141.4 31.4 all-gather.14
  174.6 32.7 all-gather.16
  209.4 54.6 all-gather.12
  450.3 50.9 reduce-scatter.17
  503.1 32.2 all-gather.22
  537.6 54.6 all-gather.20
  593.7 53.4 all-gather.26
  648.9 31.4 all-gather.24
  775.0 46.4 reduce-scatter.33
  824.8 46.7 reduce-scatter.31
  874.7 35.6 reduce-scatter.27
  913.9 35.6 reduce-scatter.25
  952.7 35.7 reduce-scatter.29
  992.0 35.6 reduce-scatter.23
  1030.0 52.1 reduce-scatter.21
where the time goes:
time: 1140 us
  waiting for transfers between devices  629 us (55%)
  blocking collectives  203 us (18%)
  matrix products  190 us (17%)
  other arithmetic  61 us (5%)
  local copies, waits for them, and re-layouts  34.6 us (3%)
  between operations  18.4 us (2%)
    all_gather x2, waiting for transfers between devices, forward_pass(): normed_two_all = lax.all_gather(normed_two, 'tensor', axis=1, tiled=True)  114 us
    reduce_scatter x2, waiting for transfers between devices, forward_pass(): lax.psum_scatter(attn_terms.astype(jnp.bfloat16), 'tensor', scatter_dimen...  99.9 us
    unnamed x3, blocking collectives  71.7 us
    reduce_scatter x1, waiting for transfers between devices, local(): lax.psum_scatter(normed_terms.astype(jnp.bfloat16), 'tensor', scatter_dim...  52.9 us
    reduce_scatter x1, waiting for transfers between devices, local(): lax.psum_scatter(normed_two_terms.astype(jnp.bfloat16), 'tensor', scatter...  52.2 us
    reduce_scatter x1, waiting for transfers between devices, forward_pass(): lax.psum_scatter(mlp_terms.astype(jnp.bfloat16), 'tensor', scatter_dimens...  50.9 us
    all_gather x2, waiting for transfers between devices, forward_pass(): lax.all_gather(down_weight, 'dp', axis=0, tiled=True)  44.8 us
    reduce_scatter x1, waiting for transfers between devices, local(): lax.psum_scatter(query_weight_grad.astype(jnp.bfloat16), 'dp', scatter_di...  37.6 us
  transfers between devices with their start and end apart: 21, of which 17 were waited for; matrix products, arithmetic and copies ran while one was open for 12% of the time, Pallas kernels for 0%

commit v1 on v0

--- a/solution.py
+++ b/solution.py
@@ -15,22 +15,178 @@
     return centre * lax.rsqrt(spread + 1e-05) * gain + shift
 
 
-def masked_scores(query_part, key_rows, length, scale):
-    seq = key_rows.shape[0]
-    valid = lax.broadcasted_iota(jnp.int32, (seq,), 0) < length
+SEATS = 4
+SLOT = 256
+CORE, ACROSS, ALONG = 1, 2, 4
+
+
+def dot(left, right, dims):
+    return lax.dot_general(
+        left, right, (((dims[0],), (dims[1],)), ((), ())), preferred_element_type=jnp.float32
+    )
+
+
+def swap(values, bits):
+    size = lax.axis_size("dp")
+    return lax.ppermute(values, "dp", [(k, k ^ bits) for k in range(size)])
+
+
+def plane_swap(values, bits, planes):
+    return lax.ppermute(values, "tensor", [(k, k ^ bits) for k in range(planes)])
+
+
+def at_index(stack, index):
+    return lax.dynamic_index_in_dim(stack, index, 0, keepdims=False)
+
+
+def to_plane(rows, seat, plane, planes):
+    parts = rows.reshape(SEATS, -1, rows.shape[1])
+    got = jnp.stack(
+        [at_index(parts, seat)]
+        + [swap(at_index(parts, seat ^ r), r << 1) for r in range(1, SEATS)]
+    )
+    turn = seat ^ plane
+    return jnp.concatenate(
+        [at_index(got, turn)]
+        + [plane_swap(at_index(got, turn ^ k), k, planes) for k in range(1, planes)]
+    )
+
+
+def from_plane(rows, seat, plane, planes):
+    parts = rows.reshape(planes, -1, rows.shape[1])
+    got = jnp.stack([parts[0]] + [plane_swap(parts[k], k, planes) for k in range(1, planes)])
+    turn = seat ^ plane
+    back = jnp.stack(
+        [at_index(got, turn)]
+        + [swap(at_index(got, turn ^ r), r << 1) for r in range(1, SEATS)]
+    )
+    return jnp.concatenate([at_index(back, s ^ seat) for s in range(SEATS)])
+
+
+def plane_gather(own):
+    half = own.shape[0] // 2
+    a, b = own[:half], own[half:]
+    across_a, along_b = swap(a, ACROSS), swap(b, ALONG)
+    across_b, along_a = swap(b, ACROSS), swap(a, ALONG)
+    far_a, far_b = swap(across_a, ALONG), swap(along_b, ACROSS)
+    return jnp.concatenate([a, b, across_a, across_b, along_a, along_b, far_a, far_b])
+
+
+def plane_scatter(terms):
+    rows = terms.shape[0] // SEATS
+    half = rows // 2
+
+    def piece(k):
+        return terms[k * half : (k + 1) * half].astype(jnp.float32)
+
+    def low(v):
+        return v.astype(jnp.bfloat16)
+
+    far_a = swap(low(piece(6)), ACROSS).astype(jnp.float32)
+    far_b = swap(low(piece(7)), ALONG).astype(jnp.float32)
+    across_a = swap(low(piece(2)), ACROSS).astype(jnp.float32)
+    along_b = swap(low(piece(5)), ALONG).astype(jnp.float32)
+    along_a = swap(low(piece(4) + far_a), ALONG).astype(jnp.float32)
+    across_b = swap(low(piece(3) + far_b), ACROSS).astype(jnp.float32)
+    return jnp.concatenate([piece(0) + across_a + along_a, piece(1) + across_b + along_b])
+
+
+def seat_exchange(pieces, seat):
+    got = jnp.stack(
+        [at_index(pieces, seat)]
+        + [swap(at_index(pieces, seat ^ r), r << 1) for r in range(1, SEATS)]
+    )
+    return jnp.concatenate([at_index(got, s ^ seat) for s in range(SEATS)])
+
+
+def with_row(rows, row):
+    return jnp.concatenate([rows, jnp.broadcast_to(row, (16, row.shape[0]))])
+
+
+def line_gather(own, planes, plane):
+    above = below = own
+    ups, downs = [], []
+    for t in range(1, planes):
+        above = lax.ppermute(above, "tensor", [(j, j + 1) for j in range(t - 1, planes - 1)])
+        below = lax.ppermute(below, "tensor", [(j, j - 1) for j in range(1, planes - t + 1)])
+        ups.append(above)
+        downs.append(below)
+    return [own] + [
+        jnp.where(plane >= t, ups[t - 1], downs[planes - t - 1]) for t in range(1, planes)
+    ]
+
+
+def line_scatter(chunks, planes):
+    up = down = jnp.zeros((), jnp.float32)
+    wide = [c.astype(jnp.float32) for c in chunks]
+    for step in range(1, planes):
+        k = planes - step
+        up = lax.ppermute(
+            (wide[planes - k] + up).astype(jnp.bfloat16),
+            "tensor",
+            [(j, j + 1) for j in range(step)],
+        ).astype(jnp.float32)
+        down = lax.ppermute(
+            (wide[k] + down).astype(jnp.bfloat16),
+            "tensor",
+            [(planes - 1 - j, planes - 2 - j) for j in range(step)],
+        ).astype(jnp.float32)
+    return wide[0] + up + down
+
+
+def both_cores(half, core, rows_of):
+    other = swap(half, CORE)
+    mine = half.reshape(SEATS, 1, rows_of, -1)
+    other = other.reshape(SEATS, 1, rows_of, -1)
+    first = jnp.where(core == 0, mine, other)
+    second = jnp.where(core == 0, other, mine)
+    return jnp.concatenate([first, second], axis=1).reshape(2 * SEATS * rows_of, -1)
+
+
+def core_scatter(full, core, rows_of):
+    paired = full.reshape(SEATS, 2, rows_of, -1)
+    kept = lax.dynamic_index_in_dim(paired, core, 1, keepdims=False)
+    given = lax.dynamic_index_in_dim(paired, 1 - core, 1, keepdims=False)
+    return kept.astype(jnp.float32) + swap(given, CORE).astype(jnp.float32)
+
+
+def weights_home(chunks, core, seat, rows_of, planes):
+    kept = [core_scatter(c, core, rows_of).astype(jnp.bfloat16) for c in chunks]
+    owned = line_scatter(kept, planes).astype(jnp.bfloat16)
+    return jnp.stack(
+        [at_index(owned, seat)]
+        + [swap(at_index(owned, seat ^ r), r << 1) for r in range(1, SEATS)]
+    )
+
+
+def norm_back(values, gain, grad):
+    mean = jnp.mean(values, axis=-1, keepdims=True)
+    centre = values - mean
+    root = lax.rsqrt(jnp.mean(centre * centre, axis=-1, keepdims=True) + 1e-05)
+    unit = centre * root
+    scaled = grad * gain
+    part = root * (
+        scaled
+        - jnp.mean(scaled, axis=-1, keepdims=True)
+        - unit * jnp.mean(scaled * unit, axis=-1, keepdims=True)
+    )
+    return part, jnp.sum(grad * unit, axis=0), jnp.sum(grad, axis=0)
+
+
+def masked_scores(query_part, key_rows, valid, scale):
     scores = (
         jnp.einsum("qhe,khe->hqk", query_part, key_rows, preferred_element_type=jnp.float32) * scale
     )
     return jnp.where(valid[None, None, :], scores, masked_score)
 
 
-def attend_clip(query_rows, key_rows, value_rows, length, blocks):
+def attend_clip(query_rows, key_rows, value_rows, valid, blocks):
     seq, heads = (query_rows.shape[0], query_rows.shape[1])
     scale = HEAD_DIM ** (-0.5)
     query_blocks = query_rows.reshape(blocks, seq // blocks, heads, HEAD_DIM)
 
     def one_block(query_part):
-        scores = masked_scores(query_part, key_rows, length, scale)
+        scores = masked_scores(query_part, key_rows, valid, scale)
         top = jnp.max(scores, axis=-1, keepdims=True)
         expo = jnp.exp(scores - top)
         total = jnp.sum(expo, axis=-1, keepdims=True)
@@ -44,7 +200,7 @@
     return (context.reshape(seq, heads, HEAD_DIM), log_total)
 
 
-def attend_back(query_rows, key_rows, value_rows, context_grad, log_total, length, blocks):
+def attend_back(query_rows, key_rows, value_rows, context_grad, log_total, valid, blocks):
     seq, heads = (query_rows.shape[0], query_rows.shape[1])
     scale = HEAD_DIM ** (-0.5)
     query_blocks = query_rows.reshape(blocks, seq // blocks, heads, HEAD_DIM)
@@ -53,7 +209,7 @@
     def one_block(carry, inputs):
         key_acc, value_acc = carry
         query_part, grad_part, lse_part = inputs
-        scores = masked_scores(query_part, key_rows, length, scale)
+        scores = masked_scores(query_part, key_rows, valid, scale)
         probs = jnp.exp(scores - lse_part[..., None])
         value_acc = value_acc + jnp.einsum(
             "hqk,qhe->khe",
@@ -147,7 +303,8 @@
     )
 
     def clip_attend(item):
-        return attend_clip(item[0], item[1], item[2], item[3], blocks)
+        valid = lax.broadcasted_iota(jnp.int32, (seq,), 0) < item[3]
+        return attend_clip(item[0], item[1], item[2], valid, blocks)
 
     context, log_total = lax.map(clip_attend, (queries, keyed, valued, lengths))
     context = context.reshape(clips, seq, heads * HEAD_DIM)
@@ -240,11 +397,7 @@
         down_weight,
         down_bias,
     )
-    first = forward_pass(tokens, lengths, weights)
-    fenced_tokens, fenced_lengths, fenced_weights, fenced_output = lax.optimization_barrier(
-        (tokens, lengths, weights, first["output"])
-    )
-    saved = forward_pass(fenced_tokens, fenced_lengths, fenced_weights)
+    saved = forward_pass(tokens, lengths, weights)
     blocks = saved["blocks"]
     grad_out = cotangent.astype(jnp.float32)
     down_shift_grad = jnp.sum(grad_out, axis=(0, 1))
@@ -290,7 +443,8 @@
     clips, seq, heads = (queries.shape[0], queries.shape[1], queries.shape[2])
 
     def clip_back(item):
-        return attend_back(item[0], item[1], item[2], item[3], item[4], item[5], blocks)
+        valid = lax.broadcasted_iota(jnp.int32, (seq,), 0) < item[5]
+        return attend_back(item[0], item[1], item[2], item[3], item[4], valid, blocks)
 
     query_grad, key_grad, value_grad = lax.map(
         clip_back,
@@ -379,7 +533,7 @@
     )
     shared = lax.psum((query_shift_grad, value_shift_grad, up_shift_grad), "dp")
     return (
-        first["output"].astype(jnp.bfloat16),
+        saved["output"].astype(jnp.bfloat16),
         tokens_grad,
         owned[4],
         owned[5],
@@ -399,7 +553,253 @@
     )
 
 
+def plane_local(
+    tokens,
+    lengths,
+    cotangent,
+    ln1_gain,
+    ln1_bias,
+    query_weight,
+    query_bias,
+    key_weight,
+    value_weight,
+    value_bias,
+    out_weight,
+    out_bias,
+    ln2_gain,
+    ln2_bias,
+    up_weight,
+    up_bias,
+    down_weight,
+    down_bias,
+):
+    planes = lax.axis_size("tensor")
+    mine = lax.axis_index("dp")
+    core, seat = mine & 1, mine >> 1
+    plane = lax.axis_index("tensor")
+    quarter, width = tokens.shape[1], tokens.shape[2]
+    rows_of = query_weight.shape[0]
+    sub = quarter // SEATS
+    wide = query_weight.shape[1]
+    heads = wide // HEAD_DIM
+    hidden_of = up_weight.shape[1] // SEATS
+
+    def at(stack, index):
+        return lax.dynamic_index_in_dim(stack, index, 0, keepdims=False)
+
+    vectors = (ln1_gain, ln1_bias, out_bias, ln2_gain, ln2_bias, down_bias)
+    small = jnp.concatenate(
+        [v.astype(jnp.float32) for v in vectors] + [lengths.astype(jnp.float32)]
+    )
+    small = lax.all_gather(small, "dp", axis=0)
+    gain_one, bias_one, out_shift, gain_two, bias_two, down_shift = (
+        small[:, k * rows_of : (k + 1) * rows_of].reshape(-1) for k in range(len(vectors))
+    )
+    length = at(small, 2 * plane + core)[-1].astype(jnp.int32)
+
+    rows_low = to_plane(tokens[0], seat, plane, planes)
+    cot_low = to_plane(cotangent[0], seat, plane, planes)
+
+    def by_seat(w):
+        return w.reshape(rows_of, SEATS, -1)
+
+    pad = jnp.zeros((rows_of, SEATS, SLOT - 3 * HEAD_DIM), jnp.bfloat16)
+    qkv_piece = jnp.concatenate(
+        [by_seat(query_weight), by_seat(key_weight), by_seat(value_weight), pad], axis=2
+    ).transpose(1, 0, 2)
+    q_shift = at(query_bias.reshape(SEATS, HEAD_DIM), seat)
+    v_shift = at(value_bias.reshape(SEATS, HEAD_DIM), seat)
+    none = jnp.zeros((HEAD_DIM,), jnp.bfloat16)
+    qkv_row = jnp.concatenate(
+        [q_shift, none, v_shift, jnp.zeros((SLOT - 3 * HEAD_DIM,), jnp.bfloat16)]
+    )
+    qkv_blocks = line_gather(
+        with_row(seat_exchange(qkv_piece, seat), qkv_row), planes, plane
+    )
+    qkv_half = jnp.concatenate([b[: SEATS * rows_of] for b in qkv_blocks], axis=1)
+    qkv_full = both_cores(qkv_half, core, rows_of)
+    qkv_shift = jnp.concatenate([b[SEATS * rows_of] for b in qkv_blocks])
+
+    out_blocks = line_gather(out_weight, planes, plane)
+    out_rows = (
+        jnp.stack([b.reshape(rows_of, SEATS, HEAD_DIM) for b in out_blocks], axis=2)
+    ).reshape(rows_of, SEATS * planes * HEAD_DIM)
+    out_around = plane_gather(out_rows).reshape(SEATS, rows_of, -1)
+    out_half = jnp.concatenate([at(out_around, s ^ seat) for s in range(SEATS)])
+    out_full = both_cores(out_half, core, rows_of)
+
+    ff_piece = jnp.concatenate([by_seat(up_weight), by_seat(down_weight)], axis=2).transpose(
+        1, 0, 2
+    )
+    up_row = at(up_bias.reshape(SEATS, hidden_of), seat)
+    ff_row = jnp.concatenate([up_row, jnp.zeros((hidden_of,), jnp.bfloat16)])
+    ff_blocks = line_gather(with_row(seat_exchange(ff_piece, seat), ff_row), planes, plane)
+    up_half = jnp.concatenate([b[: SEATS * rows_of, :hidden_of] for b in ff_blocks], axis=1)
+    down_half = jnp.concatenate([b[: SEATS * rows_of, hidden_of:] for b in ff_blocks], axis=1)
+    up_full = both_cores(up_half, core, rows_of)
+    down_full = both_cores(down_half, core, rows_of)
+    up_shift = jnp.concatenate([b[SEATS * rows_of, :hidden_of] for b in ff_blocks])
+
+    rows = rows_low.astype(jnp.float32)
+    normed = layer_norm(rows, gain_one, bias_one).astype(jnp.bfloat16)
+    normed_all = plane_gather(normed)
+    seq = normed_all.shape[0]
+    qkv = (
+        dot(normed_all, qkv_full, (1, 0)) + qkv_shift.astype(jnp.float32)
+    ).astype(jnp.bfloat16)
+    block, part, place = (
+        lax.broadcasted_iota(jnp.int32, (SEATS, planes, sub), a) for a in range(3)
+    )
+    position = ((plane ^ part) * quarter + (seat ^ block) * sub + place).reshape(seq)
+    valid = position < length
+    shaped = qkv.reshape(seq, heads, SLOT)
+    queries = shaped[:, :, :HEAD_DIM]
+    keyed = shaped[:, :, HEAD_DIM : 2 * HEAD_DIM]
+    valued = shaped[:, :, 2 * HEAD_DIM : 3 * HEAD_DIM]
+    blocks = 2
+    context, log_total = attend_clip(queries, keyed, valued, valid, blocks)
+    context = context.reshape(SEATS, quarter, wide)
+    context_from = jnp.stack(
+        [context[0]] + [swap(context[r], r << 1) for r in range(1, SEATS)]
+    )
+    context_own = jnp.concatenate([at(context_from, s ^ seat) for s in range(SEATS)], axis=1)
+    attended = dot(context_own, out_full, (1, 1))
+    middle = rows + attended + out_shift
+    normed_two = layer_norm(middle, gain_two, bias_two).astype(jnp.bfloat16)
+    normed_two_all = plane_gather(normed_two)
+    hidden_pre = dot(normed_two_all, up_full, (1, 0)) + up_shift.astype(jnp.float32)
+    cot_all = plane_gather(cot_low)
+    hidden_grad = dot(cot_all, down_full, (1, 0))
+    normal = 0.5 * (1.0 + lax.erf(hidden_pre * (0.5**0.5)))
+    slope = normal + hidden_pre * (jnp.exp(-0.5 * hidden_pre * hidden_pre) * (0.5 / jnp.pi) ** 0.5)
+    hidden = (hidden_pre * normal).astype(jnp.bfloat16)
+    pre_grad = (hidden_grad * slope).astype(jnp.bfloat16)
+
+    normed_two_terms = dot(pre_grad, up_full, (1, 1))
+    normed_two_grad = plane_scatter(normed_two_terms)
+    mixed = plane_scatter(dot(hidden, down_full, (1, 1)))
+    output = (middle + mixed + down_shift).astype(jnp.bfloat16)
+    output_home = from_plane(output, seat, plane, planes)
+    up_grad = dot(normed_two_all, pre_grad, (0, 0)).astype(jnp.bfloat16)
+    down_grad = dot(cot_all, hidden, (0, 0)).astype(jnp.bfloat16)
+    up_shift_grad = jnp.sum(pre_grad, axis=0, dtype=jnp.float32)
+    grad_out = cot_low.astype(jnp.float32)
+    down_shift_grad = jnp.sum(grad_out, axis=0)
+    middle_part, gain_two_grad, bias_two_grad = norm_back(middle, gain_two, normed_two_grad)
+    middle_grad = grad_out + middle_part
+    out_shift_grad = jnp.sum(middle_grad, axis=0)
+    middle_low = middle_grad.astype(jnp.bfloat16)
+
+    context_grad_own = (
+        dot(middle_low, out_full, (1, 0)).astype(jnp.bfloat16).reshape(quarter, SEATS, wide)
+    ).transpose(1, 0, 2)
+    context_grad = jnp.concatenate(
+        [at(context_grad_own, seat)]
+        + [swap(at(context_grad_own, seat ^ r), r << 1) for r in range(1, SEATS)]
+    ).reshape(seq, heads, HEAD_DIM)
+    out_grad = dot(middle_low, context_own, (0, 0)).astype(jnp.bfloat16)
+    query_grad, key_grad, value_grad = attend_back(
+        queries, keyed, valued, context_grad, log_total, valid, blocks
+    )
+    qkv_grad = jnp.concatenate(
+        [
+            query_grad,
+            key_grad,
+            value_grad,
+            jnp.zeros((seq, heads, SLOT - 3 * HEAD_DIM), jnp.bfloat16),
+        ],
+        axis=2,
+    ).reshape(seq, heads * SLOT)
+    normed_grad = plane_scatter(dot(qkv_grad, qkv_full, (1, 1)))
+    qkv_weight_grad = dot(normed_all, qkv_grad, (0, 0)).astype(jnp.bfloat16)
+    qkv_shift_grad = jnp.sum(qkv_grad, axis=0, dtype=jnp.float32).reshape(planes, SLOT)
+    tokens_part, gain_one_grad, bias_one_grad = norm_back(rows, gain_one, normed_grad)
+    tokens_grad = (middle_grad + tokens_part).astype(jnp.bfloat16)
+    tokens_grad_home = from_plane(tokens_grad, seat, plane, planes)
+
+    def lanes(full, t, size):
+        return full[..., t * size : (t + 1) * size]
+
+    ff_grad = [
+        jnp.concatenate([lanes(up_grad, t, hidden_of), lanes(down_grad, t, hidden_of)], axis=1)
+        for t in range(planes)
+    ]
+    ff_home = weights_home(ff_grad, core, seat, rows_of, planes)
+    up_home = jnp.concatenate([at(ff_home, s ^ seat)[:, :hidden_of] for s in range(SEATS)], axis=1)
+    down_home = jnp.concatenate(
+        [at(ff_home, s ^ seat)[:, hidden_of:] for s in range(SEATS)], axis=1
+    )
+    qkv_home = weights_home(
+        [lanes(qkv_weight_grad, t, SLOT) for t in range(planes)], core, seat, rows_of, planes
+    )
+    query_home, key_home, value_home = (
+        jnp.concatenate(
+            [at(qkv_home, s ^ seat)[:, k * HEAD_DIM : (k + 1) * HEAD_DIM] for s in range(SEATS)],
+            axis=1,
+        )
+        for k in range(3)
+    )
+    out_kept = core_scatter(out_grad, core, rows_of).astype(jnp.bfloat16)
+    out_owned = plane_scatter(
+        jnp.concatenate([at(out_kept, seat ^ r) for r in range(SEATS)])
+    ).astype(jnp.bfloat16)
+    out_owned = out_owned.reshape(rows_of, SEATS, planes, HEAD_DIM)
+    out_home = line_scatter(
+        [out_owned[:, :, t].reshape(rows_of, wide) for t in range(planes)], planes
+    )
+
+    def by_block(v):
+        placed = jnp.stack([at(v, (plane - p) % planes) for p in range(planes)])
+        seats = lax.broadcasted_iota(jnp.int32, (1, SEATS, 1), 1)
+        return jnp.where(seats == seat, placed[:, None, :], 0.0).reshape(-1)
+
+    def everywhere(v):
+        for bit in (1, 2, 4):
+            v = v + swap(v, bit)
+        for bit in (1, 2):
+            v = v + plane_swap(v, bit, planes)
+        return v
+
+    early = everywhere(
+        jnp.concatenate(
+            [gain_two_grad, bias_two_grad, out_shift_grad, down_shift_grad]
+            + [by_block(up_shift_grad.reshape(planes, hidden_of))]
+        )
+    )
+    late = everywhere(
+        jnp.concatenate(
+            [gain_one_grad, bias_one_grad]
+            + [by_block(qkv_shift_grad[:, :HEAD_DIM])]
+            + [by_block(qkv_shift_grad[:, 2 * HEAD_DIM : 3 * HEAD_DIM])]
+        )
+    )
+
+    def owned(v, k, size, index):
+        return lax.dynamic_slice_in_dim(v[k * width :], index * size, size)
+
+    return (
+        output_home[None],
+        tokens_grad_home[None].astype(jnp.float32),
+        owned(late, 0, rows_of, mine),
+        owned(late, 1, rows_of, mine),
+        query_home.astype(jnp.float32),
+        owned(late, 2, wide, plane),
+        key_home.astype(jnp.float32),
+        value_home.astype(jnp.float32),
+        owned(late, 3, wide, plane),
+        out_home,
+        owned(early, 2, rows_of, mine),
+        owned(early, 0, rows_of, mine),
+        owned(early, 1, rows_of, mine),
+        up_home.astype(jnp.float32),
+        owned(early, 4, SEATS * hidden_of, plane),
+        down_home.astype(jnp.float32),
+        owned(early, 3, rows_of, mine),
+    )
+
+
 def solution(mesh):
+    one_plane = mesh.shape["dp"] == 2 * SEATS and mesh.shape["tensor"] == SEATS
     placed = (
         P("dp", "tensor", None),
         P("dp"),
@@ -421,7 +821,7 @@
         P("dp"),
     )
     return jax.shard_map(
-        local,
+        plane_local if one_plane else local,
         mesh=mesh,
         in_specs=placed,
         out_specs=(

time: 1140 us -> 788 us (0.69)
  waiting for transfers between devices: 629 us -> 199 us
  starting transfers between devices: 2.3 us -> 231 us
  blocking collectives: 203 us -> 23.1 us
  matrix products: 190 us -> 97.9 us
  local copies, waits for them, and re-layouts: 34.6 us -> 123 us
  other arithmetic: 61 us -> 94.7 us
  between operations: 18.4 us -> 6.37 us
    reduce_scatter x10 -> x0, waiting for transfers between devices: 354 us -> none  [the longest x2 99.9 us: forward_pass(): lax.psum_scatter(attn_terms.astype(jnp.bfloat16), 'tensor', scatter_dimen...]
    all_gather x10 -> x0, waiting for transfers between devices: 272 us -> none  [the longest x2 114 us: forward_pass(): normed_two_all = lax.all_gather(normed_two, 'tensor', axis=1, tiled=True)]
    ppermute x0 -> x149, starting transfers between devices: none -> 231 us  [the longest x97 97.2 us: swap(): return lax.ppermute(values, 'dp', [(k, k ^ bits) for k in range(size)])]
    ppermute x0 -> x149, waiting for transfers between devices: none -> 199 us  [the longest x97 141 us: swap(): return lax.ppermute(values, 'dp', [(k, k ^ bits) for k in range(size)])]
    all_gather x8 -> x0, blocking collectives: 88.5 us -> none  [the longest x2 22.8 us: forward_pass(): lax.all_gather(out_weight, 'dp', axis=0, tiled=True)]
    dot_general x22 -> x12, matrix products: 125 us -> 46.4 us  [dot(): lax.dot_general(left, right, (((dims[0],), (dims[1],)), ((), ())), prefer...]
    unnamed x3 -> x1, blocking collectives: 71.7 us -> 23.1 us
    psum x2 -> x0, blocking collectives: 42.4 us -> none  [the longest x1 24.7 us: local(): shared = lax.psum((query_shift_grad, value_shift_grad, up_shift_grad), 'dp')]
  transfers between devices with their start and end apart: 21 -> 149, of which waited for: 17 -> 58; matrix products, arithmetic and copies ran while one was open for 12% -> 31% of each run, Pallas kernels for 0% -> 0%
where the time goes in v1:
time: 788 us; the launch traced here: 775 us
  starting transfers between devices  231 us (29%)
  waiting for transfers between devices  199 us (25%)
  local copies, waits for them, and re-layouts  123 us (16%)
  matrix products  97.9 us (12%)
  other arithmetic  94.7 us (12%)
  blocking collectives  23.1 us (3%)
    ppermute x97, waiting for transfers between devices, swap(): return lax.ppermute(values, 'dp', [(k, k ^ bits) for k in range(size)])  141 us
    ppermute x97, starting transfers between devices, swap(): return lax.ppermute(values, 'dp', [(k, k ^ bits) for k in range(size)])  97.2 us
    ppermute x9, starting transfers between devices, line_scatter(): lax.ppermute((wide[planes - k] + up).astype(jnp.bfloat16), 'tensor', [(j,...  62.4 us
    dot_general x12, matrix products, dot(): lax.dot_general(left, right, (((dims[0],), (dims[1],)), ((), ())), prefer...  46.4 us
    ppermute x16, starting transfers between devices, plane_swap(): lax.ppermute(values, 'tensor', [(k, k ^ bits) for k in range(planes)])  29.9 us
    unnamed x308, local copies, waits for them, and re-layouts  28.9 us
    ppermute x9, waiting for transfers between devices, line_gather(): lax.ppermute(below, 'tensor', [(j, j - 1) for j in range(1, planes - t +...  23.1 us
    unnamed x1, blocking collectives  23.1 us
  transfers between devices with their start and end apart: 149, of which 58 were waited for; matrix products, arithmetic and copies ran while one was open for 31% of the time, Pallas kernels for 0%

profile of v1, /device:TPU:0, one launch (start us, length us, event | category | flops | bytes accessed | tf_op | source)
XLA Modules:
  0.0 775.5 jit_solution(5328322815377416772)
XLA Ops:
  2.0 6.2 collective-permute-start.25
  29.4 23.1 %all-reduce.1 = f32[7688]{0:T(1024)S(1)} all-reduce(f32[7688]{0:T(1024)S(1)} %dynamic-update-slice), channel_id=2, replica_groups=mesh['dp'=8,'tensor'=4] {'dp'}, use_global_device_ids=true, to_apply=%add.1 | all-reduce | flops 7688 | bytes 61504
  87.3 6.6 collective-permute-start.3
  106.2 4.9 collective-permute-start.5
  144.0 4.9 collective-permute-done.34
  164.8 7.5 collective-permute-done.76
  174.4 5.0 collective-permute-done.7
  189.8 5.9 collective-permute-done.35
  195.7 5.7 collective-permute-done.36
  221.1 6.1 collective-permute-done.18
  230.4 12.4 %collective-permute-done.49 = bf16[656,640]{1,0:T(8,128)(2,1)} collective-permute-done((bf16[656,640]{1,0:T(8,128)(2,1)}, bf16[656,640]{1,0:T(8,128)(2,1)}, u32[]{:S(2)}, u32[]{:S(2)}) %collective-permute-start.49) | collective-permute-done | bytes 839712 | tf_op jit(solution)/shard_map/ppermute | solution.py:111
  261.6 12.9 %while.28 = (s32[]{:T(128)}, bf16[2,512,4,80]{1,3,2,0:T(8,128)(2,1)S(1)}, f32[2,4,512]{2,1,0:T(4,128)S(1)}, bf16[2,512,4,80]{1,3,2,0:T(8,128)(2,1)S(1)}, bf16[10...) while((s32[]{:T(128)}, ...), condition=%wide.region_5.6_spmd.clone, body=%wide.region_2.5_spmd.clone.sunk | while | flops 696419328 | bytes 27203732 | solution.py:199
  338.0 5.7 convert_reduce_fusion
  347.6 5.7 fusion.151
  357.4 6.1 fusion.152
  408.5 11.3 %collective-permute-done.56 = bf16[128,1280]{1,0:T(8,128)(2,1)S(1)} collective-permute-done((bf16[128,1280]{1,0:T(8,128)(2,1)S(1)}, bf16[128,1280]{1,0:T(8,128)(2,1)S(1)}, u32[]{:S(2)}, u32[]{:S(2)}) %collective-permute-start.56) | collective-permute-done | bytes 327712 | tf_op jit(solution)/shard_map/ppermute | solution.py:31
  424.8 5.3 collective-permute-done.81
  466.7 5.5 collective-permute-done.133
  493.6 51.7 %while.29 = (s32[]{:T(128)}, f32[1024,4,80]{0,2,1:T(8,128)S(1)}, f32[1024,4,80]{0,2,1:T(8,128)}, bf16[2,512,4,80]{1,3,2,0:T(8,128)(2,1)}, bf16[2,512,4,80]{1,3,2...) while((s32[]{:T(128)}, f32[1024,4,80]{0,2,1:T(8,128)S(1)}, ...), condition=%wide.region_12.13_spmd.clone, body=%wide.region_10.12_spmd.clone.sunk | while | flops 1711145984 | bytes 133168440 | solution.py:237
  498.3 5.6 multiply_reduce_fusion.7
  511.2 4.7 fusion.217
  523.7 5.6 multiply_reduce_fusion.7
  552.9 5.0 fusion.153
  586.1 4.8 collective-permute-done.90
  620.5 5.7 collective-permute-done.95
  650.4 5.2 collective-permute-done.141
  665.4 5.5 collective-permute-done.122
  673.5 12.3 %collective-permute-done.114 = bf16[4,160,256]{2,1,0:T(8,128)(2,1)S(1)} collective-permute-done((bf16[4,160,256]{2,1,0:T(8,128)(2,1)S(1)}, bf16[4,160,256]{2,1,0:T(8,128)(2,1)S(1)}, u32[]{:S(2)}, u32[]{:S(2)}) %collective-permute-start.114) | collective-permute-done | bytes 327712 | tf_op jit(solution)/shard_map/ppermute | solution.py:129
  696.4 19.6 %collective-permute-start.142 = (bf16[4,160,640]{2,1,0:T(8,128)(2,1)}, bf16[4,160,640]{2,1,0:T(8,128)(2,1)}, u32[]{:S(2)}, u32[]{:S(2)}) collective-permute-start(bf16[4,160,640]{2,1,0:T(8,128)(2,1)} %get-tuple-element.334), channel_id=1, source_target_pairs={{0,1},{1,2},{2,3},{4,5},{5,6},{6,7},{8,9},{9,10},{10,11},{12,13},{... | collective-permute-start | bytes 2457608 | tf_op jit(solution)/shard_map/ppermute | solution.py:124
  726.5 4.7 collective-permute-start.125
  737.4 13.4 %collective-permute-start.126 = (bf16[160,320]{1,0:T(8,128)(2,1)}, bf16[160,320]{1,0:T(8,128)(2,1)}, u32[]{:S(2)}, u32[]{:S(2)}) collective-permute-start(bf16[160,320]{1,0:T(8,128)(2,1)} %get-tuple-element.519), channel_id=1, source_target_pairs={{0,1},{1,2},{4,5},{5,6},{8,9},{9,10},{12,13},{13,14},{16,17},{17,1... | collective-permute-start | bytes 307208 | tf_op jit(solution)/shard_map/ppermute | solution.py:124
  753.9 4.7 collective-permute-start.127
  (910 shorter events, 544.2 us)
Async XLA Ops:
  0.7 79.8 %collective-permute-start.26 = (bf16[160,320]{1,0:T(8,128)(2,1)}, bf16[160,320]{1,0:T(8,128)(2,1)}, u32[]{:S(2)}, u32[]{:S(2)}) collective-permute-start(bf16[160,320]{1,0:T(8,128)(2,1)} %param.32), channel_id=1, source_target_pairs={{1,0},{2,1},{3,2},{5,4},{6,5},{7,6},{9,8},{10,9},{11,10},{13,12},{... | collective-permute-start | bytes 307208 | tf_op jit(solution)/shard_map/ppermute | solution.py:111
  2.0 82.1 %collective-permute-start.25 = (bf16[160,320]{1,0:T(8,128)(2,1)}, bf16[160,320]{1,0:T(8,128)(2,1)}, u32[]{:S(2)}, u32[]{:S(2)}) collective-permute-start(bf16[160,320]{1,0:T(8,128)(2,1)} %param.32), channel_id=1, source_target_pairs={{0,1},{1,2},{2,3},{4,5},{5,6},{6,7},{8,9},{9,10},{10,11},{12,13},{... | collective-permute-start | bytes 307208 | tf_op jit(solution)/shard_map/ppermute | solution.py:110
  14.8 43.1 %collective-permute-start.12 = (bf16[160,256]{1,0:T(8,128)(2,1)S(1)}, bf16[160,256]{1,0:T(8,128)(2,1)S(1)}, u32[]{:S(2)}, u32[]{:S(2)}) collective-permute-start(bf16[160,256]{1,0:T(8,128)(2,1)S(1)} %bitcast.539), channel_id=1, source_target_pairs={{0,8},{4,12},{8,0},{12,4},{16,24},{20,28},{24,16},{28,20},{1,9},{5... | collective-permute-start | bytes 245768 | tf_op jit(solution)/shard_map/ppermute | solution.py:31
  16.8 41.1 %collective-permute-start.13 = (bf16[160,256]{1,0:T(8,128)(2,1)S(1)}, bf16[160,256]{1,0:T(8,128)(2,1)S(1)}, u32[]{:S(2)}, u32[]{:S(2)}) collective-permute-start(bf16[160,256]{1,0:T(8,128)(2,1)S(1)} %bitcast.538), channel_id=1, source_target_pairs={{0,16},{4,20},{8,24},{12,28},{16,0},{20,4},{24,8},{28,12},{1,17},{... | collective-permute-start | bytes 245768 | tf_op jit(solution)/shard_map/ppermute | solution.py:31
  18.4 40.7 %collective-permute-start.14 = (bf16[160,256]{1,0:T(8,128)(2,1)S(1)}, bf16[160,256]{1,0:T(8,128)(2,1)S(1)}, u32[]{:S(2)}, u32[]{:S(2)}) collective-permute-start(bf16[160,256]{1,0:T(8,128)(2,1)S(1)} %bitcast.537), channel_id=1, source_target_pairs={{0,24},{4,28},{8,16},{12,20},{16,8},{20,12},{24,0},{28,4},{1,25},{... | collective-permute-start | bytes 245768 | tf_op jit(solution)/shard_map/ppermute | solution.py:31
  80.5 100.7 %collective-permute-start.15 = (bf16[656,256]{1,0:T(8,128)(2,1)}, bf16[656,256]{1,0:T(8,128)(2,1)}, u32[]{:S(2)}, u32[]{:S(2)}) collective-permute-start(bf16[656,256]{1,0:T(8,128)(2,1)} %constant_dynamic-update-slice_fusion.7), channel_id=1, source_target_pairs={{0,1},{1,2},{2,3},{4,5},{5,6},{6,7},{8,9},{9,10},{10,11},{12,13},{... | collective-permute-start | bytes 1007624 | tf_op jit(solution)/shard_map/ppermute | solution.py:110
  84.0 98.4 %collective-permute-start.16 = (bf16[656,256]{1,0:T(8,128)(2,1)}, bf16[656,256]{1,0:T(8,128)(2,1)}, u32[]{:S(2)}, u32[]{:S(2)}) collective-permute-start(bf16[656,256]{1,0:T(8,128)(2,1)} %constant_dynamic-update-slice_fusion.7), channel_id=1, source_target_pairs={{1,0},{2,1},{3,2},{5,4},{6,5},{7,6},{9,8},{10,9},{11,10},{13,12},{... | collective-permute-start | bytes 1007624 | tf_op jit(solution)/shard_map/ppermute | solution.py:111
  87.3 29.2 %collective-permute-start.3 = (bf16[64,1280]{1,0:T(8,128)(2,1)}, bf16[64,1280]{1,0:T(8,128)(2,1)S(1)}, u32[]{:S(2)}, u32[]{:S(2)}) collective-permute-start(bf16[64,1280]{1,0:T(8,128)(2,1)} %get-tuple-element.500), channel_id=1, source_target_pairs={{0,1},{1,0},{2,3},{3,2},{4,5},{5,4},{6,7},{7,6},{8,9},{9,8},{10,11... | collective-permute-start | bytes 491528 | tf_op jit(solution)/shard_map/ppermute | solution.py:35
  123.5 93.5 %collective-permute-start.47 = (bf16[656,640]{1,0:T(8,128)(2,1)}, bf16[656,640]{1,0:T(8,128)(2,1)}, u32[]{:S(2)}, u32[]{:S(2)}) collective-permute-start(bf16[656,640]{1,0:T(8,128)(2,1)} %constant_dynamic-update-slice_fusion.27), channel_id=1, source_target_pairs={{0,1},{1,2},{2,3},{4,5},{5,6},{6,7},{8,9},{9,10},{10,11},{12,13},{... | collective-permute-start | bytes 2519048 | tf_op jit(solution)/shard_map/ppermute | solution.py:110
  181.2 37.6 %collective-permute-start.48 = (bf16[656,640]{1,0:T(8,128)(2,1)}, bf16[656,640]{1,0:T(8,128)(2,1)}, u32[]{:S(2)}, u32[]{:S(2)}) collective-permute-start(bf16[656,640]{1,0:T(8,128)(2,1)} %constant_dynamic-update-slice_fusion.27), channel_id=1, source_target_pairs={{1,0},{2,1},{3,2},{5,4},{6,5},{7,6},{9,8},{10,9},{11,10},{13,12},{... | collective-permute-start | bytes 2519048 | tf_op jit(solution)/shard_map/ppermute | solution.py:111
  211.7 35.9 %collective-permute-start.37 = (bf16[640,1280]{1,0:T(8,128)(2,1)}, bf16[640,1280]{1,0:T(8,128)(2,1)}, u32[]{:S(2)}, u32[]{:S(2)}) collective-permute-start(bf16[640,1280]{1,0:T(8,128)(2,1)} %pad_maximum_fusion.4), channel_id=1, source_target_pairs={{0,4},{4,0},{8,12},{12,8},{16,20},{20,16},{24,28},{28,24},{1,5},{5... | collective-permute-start | bytes 4915208 | tf_op jit(solution)/shard_map/ppermute | solution.py:31
  218.8 24.0 %collective-permute-start.49 = (bf16[656,640]{1,0:T(8,128)(2,1)}, bf16[656,640]{1,0:T(8,128)(2,1)}, u32[]{:S(2)}, u32[]{:S(2)}) collective-permute-start(bf16[656,640]{1,0:T(8,128)(2,1)} %collective-permute-done.48), channel_id=1, source_target_pairs={{1,0},{2,1},{5,4},{6,5},{9,8},{10,9},{13,12},{14,13},{17,16},{18,1... | collective-permute-start | bytes 2519048 | tf_op jit(solution)/shard_map/ppermute | solution.py:111
  228.6 22.7 %collective-permute-start.21 = (bf16[640,1024]{1,0:T(8,128)(2,1)}, bf16[640,1024]{1,0:T(8,128)(2,1)}, u32[]{:S(2)}, u32[]{:S(2)}) collective-permute-start(bf16[640,1024]{1,0:T(8,128)(2,1)} %pad_maximum_fusion.9), channel_id=1, source_target_pairs={{0,4},{4,0},{8,12},{12,8},{16,20},{20,16},{24,28},{28,24},{1,5},{5... | collective-permute-start | bytes 3932168 | tf_op jit(solution)/shard_map/ppermute | solution.py:31
  228.8 67.0 %collective-permute-start.52 = (bf16[656,640]{1,0:T(8,128)(2,1)}, bf16[656,640]{1,0:T(8,128)(2,1)}, u32[]{:S(2)}, u32[]{:S(2)}) collective-permute-start(bf16[656,640]{1,0:T(8,128)(2,1)} %collective-permute-done.51), channel_id=1, source_target_pairs={{2,3},{6,7},{10,11},{14,15},{18,19},{22,23},{26,27},{30,31}} | collective-permute-start | bytes 2519048 | tf_op jit(solution)/shard_map/ppermute | solution.py:110
  242.8 55.6 %collective-permute-start.50 = (bf16[656,640]{1,0:T(8,128)(2,1)}, bf16[656,640]{1,0:T(8,128)(2,1)}, u32[]{:S(2)}, u32[]{:S(2)}) collective-permute-start(bf16[656,640]{1,0:T(8,128)(2,1)} %collective-permute-done.49), channel_id=1, source_target_pairs={{1,0},{5,4},{9,8},{13,12},{17,16},{21,20},{25,24},{29,28}} | collective-permute-start | bytes 2519048 | tf_op jit(solution)/shard_map/ppermute | solution.py:111
  304.9 24.9 %collective-permute-start.53 = (bf16[640,1280]{1,0:T(8,128)(2,1)}, bf16[640,1280]{1,0:T(8,128)(2,1)}, u32[]{:S(2)}, u32[]{:S(2)}) collective-permute-start(bf16[640,1280]{1,0:T(8,128)(2,1)} %concatenate.202), channel_id=1, source_target_pairs={{0,4},{4,0},{8,12},{12,8},{16,20},{20,16},{24,28},{28,24},{1,5},{5... | collective-permute-start | bytes 4915208 | tf_op jit(solution)/shard_map/ppermute | solution.py:31
  397.1 25.5 %collective-permute-start.79 = (bf16[128,1280]{1,0:T(8,128)(2,1)S(1)}, bf16[128,1280]{1,0:T(8,128)(2,1)}, u32[]{:S(2)}, u32[]{:S(2)}) collective-permute-start(bf16[128,1280]{1,0:T(8,128)(2,1)S(1)} %get-tuple-element.402), channel_id=1, source_target_pairs={{0,8},{4,12},{8,0},{12,4},{16,24},{20,28},{24,16},{28,20},{1,9},{5... | collective-permute-start | bytes 983048 | tf_op jit(solution)/shard_map/ppermute | solution.py:31
  397.1 27.6 %collective-permute-start.82 = (bf16[128,1280]{1,0:T(8,128)(2,1)}, bf16[128,1280]{1,0:T(8,128)(2,1)}, u32[]{:S(2)}, u32[]{:S(2)}) collective-permute-start(bf16[128,1280]{1,0:T(8,128)(2,1)} %get-tuple-element.404), channel_id=1, source_target_pairs={{0,16},{4,20},{8,24},{12,28},{16,0},{20,4},{24,8},{28,12},{1,17},{... | collective-permute-start | bytes 983048 | tf_op jit(solution)/shard_map/ppermute | solution.py:31
  400.6 31.3 %collective-permute-start.55 = (bf16[128,1280]{1,0:T(8,128)(2,1)}, bf16[128,1280]{1,0:T(8,128)(2,1)}, u32[]{:S(2)}, u32[]{:S(2)}) collective-permute-start(bf16[128,1280]{1,0:T(8,128)(2,1)} %get-tuple-element.406), channel_id=1, source_target_pairs={{0,8},{4,12},{8,0},{12,4},{16,24},{20,28},{24,16},{28,20},{1,9},{5... | collective-permute-start | bytes 983048 | tf_op jit(solution)/shard_map/ppermute | solution.py:31
  405.7 26.6 %collective-permute-start.58 = (bf16[128,1280]{1,0:T(8,128)(2,1)}, bf16[128,1280]{1,0:T(8,128)(2,1)}, u32[]{:S(2)}, u32[]{:S(2)}) collective-permute-start(bf16[128,1280]{1,0:T(8,128)(2,1)} %get-tuple-element.408), channel_id=1, source_target_pairs={{0,16},{4,20},{8,24},{12,28},{16,0},{20,4},{24,8},{28,12},{1,17},{... | collective-permute-start | bytes 983048 | tf_op jit(solution)/shard_map/ppermute | solution.py:31
  424.8 205.9 %collective-permute-start.138 = (bf16[4,160,640]{2,1,0:T(8,128)(2,1)}, bf16[4,160,640]{2,1,0:T(8,128)(2,1)}, u32[]{:S(2)}, u32[]{:S(2)}) collective-permute-start(bf16[4,160,640]{2,1,0:T(8,128)(2,1)} %dynamic-slice_bitcast_fusion.3), channel_id=1, source_target_pairs={{0,4},{4,0},{8,12},{12,8},{16,20},{20,16},{24,28},{28,24},{1,5},{5... | collective-permute-start | bytes 2457608 | tf_op jit(solution)/shard_map/ppermute | solution.py:31
  478.0 152.7 %collective-permute-start.140 = (bf16[4,160,640]{2,1,0:T(8,128)(2,1)}, bf16[4,160,640]{2,1,0:T(8,128)(2,1)}, u32[]{:S(2)}, u32[]{:S(2)}) collective-permute-start(bf16[4,160,640]{2,1,0:T(8,128)(2,1)} %fusion.57), channel_id=1, source_target_pairs={{0,1},{4,5},{8,9},{12,13},{16,17},{20,21},{24,25},{28,29}} | collective-permute-start | bytes 2457608 | tf_op jit(solution)/shard_map/ppermute | solution.py:124
  482.1 79.4 %collective-permute-start.61 = (bf16[64,1280]{1,0:T(8,128)(2,1)}, bf16[64,1280]{1,0:T(8,128)(2,1)}, u32[]{:S(2)}, u32[]{:S(2)}) collective-permute-start(bf16[64,1280]{1,0:T(8,128)(2,1)} %get-tuple-element.484), channel_id=1, source_target_pairs={{0,1},{1,0},{2,3},{3,2},{4,5},{5,4},{6,7},{7,6},{8,9},{9,8},{10,11... | collective-permute-start | bytes 491528 | tf_op jit(solution)/shard_map/ppermute | solution.py:35
  482.2 79.3 %collective-permute-start.62 = (bf16[64,1280]{1,0:T(8,128)(2,1)}, bf16[64,1280]{1,0:T(8,128)(2,1)}, u32[]{:S(2)}, u32[]{:S(2)}) collective-permute-start(bf16[64,1280]{1,0:T(8,128)(2,1)} %get-tuple-element.483), channel_id=1, source_target_pairs={{0,2},{1,3},{2,0},{3,1},{4,6},{5,7},{6,4},{7,5},{8,10},{9,11},{10,... | collective-permute-start | bytes 491528 | tf_op jit(solution)/shard_map/ppermute | solution.py:35
  483.0 80.7 %collective-permute-start.63 = (bf16[64,1280]{1,0:T(8,128)(2,1)}, bf16[64,1280]{1,0:T(8,128)(2,1)}, u32[]{:S(2)}, u32[]{:S(2)}) collective-permute-start(bf16[64,1280]{1,0:T(8,128)(2,1)} %get-tuple-element.482), channel_id=1, source_target_pairs={{0,3},{1,2},{2,1},{3,0},{4,7},{5,6},{6,5},{7,4},{8,11},{9,10},{10,... | collective-permute-start | bytes 491528 | tf_op jit(solution)/shard_map/ppermute | solution.py:35
  620.5 42.8 %collective-permute-start.118 = (bf16[4,160,1280]{2,1,0:T(8,128)(2,1)S(1)}, bf16[4,160,1280]{2,1,0:T(8,128)(2,1)S(1)}, u32[]{:S(2)}, u32[]{:S(2)}) collective-permute-start(bf16[4,160,1280]{2,1,0:T(8,128)(2,1)S(1)} %copy-done.45), channel_id=1, source_target_pairs={{0,4},{4,0},{8,12},{12,8},{16,20},{20,16},{24,28},{28,24},{1,5},{5... | collective-permute-start | bytes 4915208 | tf_op jit(solution)/shard_map/ppermute | solution.py:31
  647.8 112.1 %collective-permute-start.136 = (bf16[4,160,640]{2,1,0:T(8,128)(2,1)}, bf16[4,160,640]{2,1,0:T(8,128)(2,1)}, u32[]{:S(2)}, u32[]{:S(2)}) collective-permute-start(bf16[4,160,640]{2,1,0:T(8,128)(2,1)} %dynamic-slice_bitcast_fusion.5), channel_id=1, source_target_pairs={{0,4},{4,0},{8,12},{12,8},{16,20},{20,16},{24,28},{28,24},{1,5},{5... | collective-permute-start | bytes 2457608 | tf_op jit(solution)/shard_map/ppermute | solution.py:31
  661.6 60.3 %collective-permute-start.143 = (bf16[4,160,640]{2,1,0:T(8,128)(2,1)}, bf16[4,160,640]{2,1,0:T(8,128)(2,1)}, u32[]{:S(2)}, u32[]{:S(2)}) collective-permute-start(bf16[4,160,640]{2,1,0:T(8,128)(2,1)} %get-tuple-element.335), channel_id=1, source_target_pairs={{3,2},{7,6},{11,10},{15,14},{19,18},{23,22},{27,26},{31,30}} | collective-permute-start | bytes 2457608 | tf_op jit(solution)/shard_map/ppermute | solution.py:129
  688.8 27.2 %collective-permute-start.116 = (bf16[160,256]{1,0:T(8,128)(2,1)}, bf16[160,256]{1,0:T(8,128)(2,1)}, u32[]{:S(2)}, u32[]{:S(2)}) collective-permute-start(bf16[160,256]{1,0:T(8,128)(2,1)} %get-tuple-element.513), channel_id=1, source_target_pairs={{0,16},{4,20},{8,24},{12,28},{16,0},{20,4},{24,8},{28,12},{1,17},{... | collective-permute-start | bytes 245768 | tf_op jit(solution)/shard_map/ppermute | solution.py:31
  691.9 24.2 %collective-permute-start.117 = (bf16[160,256]{1,0:T(8,128)(2,1)}, bf16[160,256]{1,0:T(8,128)(2,1)}, u32[]{:S(2)}, u32[]{:S(2)}) collective-permute-start(bf16[160,256]{1,0:T(8,128)(2,1)} %get-tuple-element.512), channel_id=1, source_target_pairs={{0,24},{4,28},{8,16},{12,20},{16,8},{20,12},{24,0},{28,4},{1,25},{... | collective-permute-start | bytes 245768 | tf_op jit(solution)/shard_map/ppermute | solution.py:31
  696.4 63.5 %collective-permute-start.142 = (bf16[4,160,640]{2,1,0:T(8,128)(2,1)}, bf16[4,160,640]{2,1,0:T(8,128)(2,1)}, u32[]{:S(2)}, u32[]{:S(2)}) collective-permute-start(bf16[4,160,640]{2,1,0:T(8,128)(2,1)} %get-tuple-element.334), channel_id=1, source_target_pairs={{0,1},{1,2},{2,3},{4,5},{5,6},{6,7},{8,9},{9,10},{10,11},{12,13},{... | collective-permute-start | bytes 2457608 | tf_op jit(solution)/shard_map/ppermute | solution.py:124
  734.3 25.7 %collective-permute-start.145 = (bf16[4,160,640]{2,1,0:T(8,128)(2,1)S(1)}, bf16[4,160,640]{2,1,0:T(8,128)(2,1)}, u32[]{:S(2)}, u32[]{:S(2)}) collective-permute-start(bf16[4,160,640]{2,1,0:T(8,128)(2,1)S(1)} %add_convert_fusion.2), channel_id=1, source_target_pairs={{3,2},{2,1},{1,0},{7,6},{6,5},{5,4},{11,10},{10,9},{9,8},{15,14},{... | collective-permute-start | bytes 2457608 | tf_op jit(solution)/shard_map/ppermute | solution.py:129
  (251 other events, 2384.3 us)

commit v2 on v0

--- a/solution.py
+++ b/solution.py
@@ -1,6 +1,9 @@
 import jax
 import jax.numpy as jnp
 from jax import lax
+from jax.experimental import pallas as pl
+from jax.experimental.pallas import tpu as pltpu
+from jax.sharding import Mesh
 from jax.sharding import PartitionSpec as P
 
 HEAD_DIM = 80
@@ -15,22 +18,355 @@
     return centre * lax.rsqrt(spread + 1e-05) * gain + shift
 
 
-def masked_scores(query_part, key_rows, length, scale):
-    seq = key_rows.shape[0]
-    valid = lax.broadcasted_iota(jnp.int32, (seq,), 0) < length
+SEATS = 4
+SLOT = 256
+EXTRA = 16
+MEGA = 1 << 20
+LOG2E = 1.4426950408889634
+CORES = ((0, 1), (1, 0))
+
+
+def dot(left, right, dims):
+    return lax.dot_general(
+        left, right, (((dims[0],), (dims[1],)), ((), ())), preferred_element_type=jnp.float32
+    )
+
+
+def seat_swap(values, bits):
+    return lax.ppermute(values, "seat", [(k, k ^ bits) for k in range(SEATS)])
+
+
+def core_swap(values):
+    return lax.ppermute(values, "core", CORES)
+
+
+def plane_swap(values, bits, planes):
+    return lax.ppermute(values, "tensor", [(k, k ^ bits) for k in range(planes)])
+
+
+def at_index(stack, index):
+    return lax.dynamic_index_in_dim(stack, index, 0, keepdims=False)
+
+
+def to_plane(rows, seat, plane, planes):
+    parts = rows.reshape(SEATS, -1, rows.shape[1])
+    got = jnp.stack(
+        [at_index(parts, seat)] + [seat_swap(at_index(parts, seat ^ r), r) for r in range(1, SEATS)]
+    )
+    turn = seat ^ plane
+    return jnp.concatenate(
+        [at_index(got, turn)]
+        + [plane_swap(at_index(got, turn ^ k), k, planes) for k in range(1, planes)]
+    )
+
+
+def from_plane(rows, seat, plane, planes):
+    parts = rows.reshape(planes, -1, rows.shape[1])
+    got = jnp.stack([parts[0]] + [plane_swap(parts[k], k, planes) for k in range(1, planes)])
+    turn = seat ^ plane
+    back = jnp.stack(
+        [at_index(got, turn)] + [seat_swap(at_index(got, turn ^ r), r) for r in range(1, SEATS)]
+    )
+    return jnp.concatenate([at_index(back, s ^ seat) for s in range(SEATS)])
+
+
+def plane_gather(own):
+    half = own.shape[0] // 2
+    across, along = seat_swap(own, 1), seat_swap(own, 2)
+    far_a, far_b = seat_swap(across[:half], 2), seat_swap(along[half:], 1)
+    return jnp.concatenate([own, across, along, far_a, far_b])
+
+
+def plane_scatter(terms):
+    rows = terms.shape[0] // SEATS
+    half = rows // 2
+    own, across, along, far = (terms[k * rows : (k + 1) * rows] for k in range(SEATS))
+    far = far.astype(jnp.bfloat16)
+    far_a, far_b = seat_swap(far[:half], 1), seat_swap(far[half:], 2)
+    along = jnp.concatenate([along[:half] + far_a.astype(jnp.float32), along[half:]])
+    across = jnp.concatenate([across[:half], across[half:] + far_b.astype(jnp.float32)])
+    along = seat_swap(along.astype(jnp.bfloat16), 2).astype(jnp.float32)
+    across = seat_swap(across.astype(jnp.bfloat16), 1).astype(jnp.float32)
+    return own + across + along
+
+
+def smem():
+    return pl.BlockSpec(memory_space=pltpu.SMEM)
+
+
+def vmem():
+    return pl.BlockSpec(memory_space=pltpu.VMEM)
+
+
+def pack_weights(plan, columns, sources, extra, seat):
+    rows = sources[0].shape[0]
+
+    def kernel(seat_ref, *refs):
+        inputs, extra_ref = refs[: len(sources)], refs[len(sources)]
+        outs, held = refs[len(sources) + 1 : -1], refs[-1]
+        used = max(lane + size for _, lane, size in plan)
+        for j in range(SEATS):
+            for k, lane, size in plan:
+                held[j, :rows, lane : lane + size] = inputs[k][:, j * size : (j + 1) * size]
+            if used < columns:
+                held[j, :rows, used:] = jnp.zeros((rows, columns - used), jnp.bfloat16)
+            held[j, rows:, :] = extra_ref[j]
+        for r in range(SEATS):
+            outs[r][...] = held[seat_ref[0] ^ r]
+
+    piece = jax.ShapeDtypeStruct((rows + EXTRA, columns), jnp.bfloat16)
+    return pl.pallas_call(
+        kernel,
+        out_shape=[piece] * SEATS,
+        in_specs=[smem()] + [vmem()] * (len(sources) + 1),
+        out_specs=[vmem()] * SEATS,
+        scratch_shapes=[pltpu.VMEM((SEATS, rows + EXTRA, columns), jnp.bfloat16)],
+        compiler_params=pltpu.CompilerParams(vmem_limit_bytes=16 * MEGA),
+        name="pack_weights",
+    )(seat, *sources, extra)
+
+
+def assemble_weights(plan, gathered, seat, planes):
+    groups, _, tall, columns = gathered.shape
+    rows = tall - EXTRA
+
+    def kernel(seat_ref, in_ref, *outs):
+        del seat_ref
+        for c in range(2):
+            for z in range(planes):
+                for k, (lane, size) in enumerate(plan):
+                    outs[k][c * rows : (c + 1) * rows, z * size : (z + 1) * size] = in_ref[
+                        c * planes + z, 0, :rows, lane : lane + size
+                    ]
+        outs[-1][0] = in_ref[:, 0, rows:, :]
+
+    return pl.pallas_call(
+        kernel,
+        out_shape=[
+            jax.ShapeDtypeStruct((SEATS * 2 * rows, planes * size), jnp.bfloat16)
+            for _, size in plan
+        ]
+        + [jax.ShapeDtypeStruct((SEATS, groups, EXTRA, columns), jnp.bfloat16)],
+        grid_spec=pltpu.PrefetchScalarGridSpec(
+            num_scalar_prefetch=1,
+            grid=(SEATS,),
+            in_specs=[
+                pl.BlockSpec((groups, 1, tall, columns), lambda s, seat: (0, s ^ seat[0], 0, 0))
+            ],
+            out_specs=[
+                pl.BlockSpec((2 * rows, planes * size), lambda s, seat: (s, 0)) for _, size in plan
+            ]
+            + [pl.BlockSpec((1, groups, EXTRA, columns), lambda s, seat: (s, 0, 0, 0))],
+        ),
+        compiler_params=pltpu.CompilerParams(vmem_limit_bytes=24 * MEGA),
+        name="assemble_weights",
+    )(seat, gathered)
+
+
+def pack_grads(plan, columns, sources, vectors, shift, core, planes):
+    rows = sources[0].shape[0] // (2 * SEATS)
+    tall = rows + EXTRA
+
+    def kernel(core_ref, *refs):
+        inputs, vec_ref, shift_ref = refs[: len(sources)], refs[len(sources)], refs[-3]
+        for out, c in ((refs[-2], core_ref[0]), (refs[-1], 1 - core_ref[0])):
+            start = pl.multiple_of(c * rows, 16)
+            tile = vec_ref[0, c]
+            line = lax.broadcasted_iota(jnp.int32, tile.shape, 0)
+            for z in range(planes):
+                for k, stride, lane, size in plan:
+                    out[z, 0, :rows, lane : lane + size] = inputs[k][
+                        pl.ds(start, rows), z * stride : z * stride + size
+                    ]
+                out[z, 0, rows:, :] = jnp.where(line == 8, shift_ref[z], tile).astype(jnp.bfloat16)
+
+    chunk = jax.ShapeDtypeStruct((planes, SEATS, tall, columns), jnp.bfloat16)
+    block = pl.BlockSpec((planes, 1, tall, columns), lambda s: (0, s, 0, 0))
+    return pl.pallas_call(
+        kernel,
+        out_shape=[chunk, chunk],
+        grid=(SEATS,),
+        in_specs=[smem()]
+        + [pl.BlockSpec((2 * rows, a.shape[1]), lambda s: (s, 0)) for a in sources]
+        + [
+            pl.BlockSpec((1, 2, EXTRA, columns), lambda s: (s, 0, 0, 0)),
+            pl.BlockSpec((planes, 1, columns), lambda s: (0, 0, 0)),
+        ],
+        out_specs=[block, block],
+        compiler_params=pltpu.CompilerParams(vmem_limit_bytes=32 * MEGA),
+        name="pack_grads",
+    )(core, *sources, vectors, shift)
+
+
+def finish_grads(plan, pieces, seat):
+    tall, columns = pieces[0].shape
+    rows = tall - EXTRA
+
+    def kernel(seat_ref, *refs):
+        outs, held = refs[SEATS:-1], refs[-1]
+        for r in range(SEATS):
+            held[seat_ref[0] ^ r] = refs[r][...]
+        for j in range(SEATS):
+            for k, (lane, size) in enumerate(plan):
+                outs[k][:, j * size : (j + 1) * size] = held[j, :rows, lane : lane + size].astype(
+                    jnp.float32
+                )
+            outs[-1][j] = held[j, rows:, :].astype(jnp.float32)
+
+    return pl.pallas_call(
+        kernel,
+        out_shape=[jax.ShapeDtypeStruct((rows, SEATS * size), jnp.float32) for _, size in plan]
+        + [jax.ShapeDtypeStruct((SEATS, EXTRA, columns), jnp.float32)],
+        in_specs=[smem()] + [vmem()] * SEATS,
+        out_specs=[vmem()] * (len(plan) + 1),
+        scratch_shapes=[pltpu.VMEM((SEATS, tall, columns), jnp.bfloat16)],
+        compiler_params=pltpu.CompilerParams(vmem_limit_bytes=24 * MEGA),
+        name="finish_grads",
+    )(seat, *pieces)
+
+
+def key_shift(facts_ref, shape, planes, quarter):
+    length, seat, plane = facts_ref[0], facts_ref[1], facts_ref[2]
+    row = lax.broadcasted_iota(jnp.int32, shape, 0)
+    sub = quarter // SEATS
+    block, part, place = row // quarter, (row // sub) % planes, row % sub
+    position = (plane ^ part) * quarter + (seat ^ block) * sub + place
+    return jnp.where(position < length, 0.0, masked_score).astype(jnp.float32)
+
+
+def attend(facts, qkv, planes, quarter):
+    seq = qkv.shape[1]
+    scale = HEAD_DIM ** (-0.5) * LOG2E
+
+    def kernel(facts_ref, qkv_ref, all_ref, *refs):
+        outs, log_ref, shift_ref = refs[: SEATS - 1], refs[-2], refs[-1]
+
+        @pl.when(pl.program_id(0) == 0)
+        def _():
+            shift_ref[...] = key_shift(facts_ref, shift_ref.shape, planes, quarter)
+
+        keys = jnp.transpose(qkv_ref[HEAD_DIM : 2 * HEAD_DIM, :])
+        values = qkv_ref[2 * HEAD_DIM : 3 * HEAD_DIM, :]
+        for r in range(SEATS):
+            at = slice(r * quarter, (r + 1) * quarter)
+            scores = dot(keys, qkv_ref[:HEAD_DIM, at], (1, 0)) * scale + shift_ref[...]
+            top = jnp.max(scores, axis=0, keepdims=True)
+            expo = jnp.exp2(scores - top)
+            total = jnp.sum(expo, axis=0, keepdims=True)
+            context = dot(values, expo.astype(jnp.bfloat16), (1, 0)) / total
+            context = context.astype(jnp.bfloat16)
+            all_ref[:, at] = context
+            if r:
+                outs[r - 1][...] = context
+            log_ref[0, :, at] = top + jnp.log2(total)
+
+    head = pl.BlockSpec((HEAD_DIM, quarter), lambda h: (h, 0))
+    return pl.pallas_call(
+        kernel,
+        out_shape=[jax.ShapeDtypeStruct((planes * HEAD_DIM, seq), jnp.bfloat16)]
+        + [jax.ShapeDtypeStruct((planes * HEAD_DIM, quarter), jnp.bfloat16)] * (SEATS - 1)
+        + [jax.ShapeDtypeStruct((planes, 1, seq), jnp.float32)],
+        grid=(planes,),
+        in_specs=[smem(), pl.BlockSpec((SLOT, seq), lambda h: (h, 0))],
+        out_specs=[pl.BlockSpec((HEAD_DIM, seq), lambda h: (h, 0))]
+        + [head] * (SEATS - 1)
+        + [pl.BlockSpec((1, 1, seq), lambda h: (h, 0, 0))],
+        scratch_shapes=[pltpu.VMEM((seq, quarter), jnp.float32)],
+        compiler_params=pltpu.CompilerParams(vmem_limit_bytes=40 * MEGA),
+        name="attend",
+    )(facts, qkv)
+
+
+def attend_grad(facts, qkv, context_grad, logs, planes, quarter):
+    seq = qkv.shape[1]
+    scale = HEAD_DIM ** (-0.5)
+
+    def kernel(facts_ref, qkv_ref, grad_ref, log_ref, out_ref, shift_ref, key_acc, value_acc):
+        @pl.when(pl.program_id(0) == 0)
+        def _():
+            shift_ref[...] = key_shift(facts_ref, shift_ref.shape, planes, quarter)
+
+        keys = jnp.transpose(qkv_ref[HEAD_DIM : 2 * HEAD_DIM, :])
+        values = jnp.transpose(qkv_ref[2 * HEAD_DIM : 3 * HEAD_DIM, :])
+        for r in range(SEATS):
+            at = slice(r * quarter, (r + 1) * quarter)
+            queries, grad = qkv_ref[:HEAD_DIM, at], grad_ref[:, at]
+            scores = dot(keys, queries, (1, 0)) * (scale * LOG2E) + shift_ref[...]
+            probs = jnp.exp2(scores - log_ref[0, :, at])
+            prob_grad = dot(values, grad, (1, 0))
+            mean = jnp.sum(probs * prob_grad, axis=0, keepdims=True)
+            score_grad = (probs * (prob_grad - mean)).astype(jnp.bfloat16)
+            query_grad = dot(qkv_ref[HEAD_DIM : 2 * HEAD_DIM, :], score_grad, (1, 0))
+            out_ref[:HEAD_DIM, at] = (query_grad * scale).astype(jnp.bfloat16)
+            key_part = dot(queries, score_grad, (1, 1))
+            value_part = dot(grad, probs.astype(jnp.bfloat16), (1, 1))
+            if r == 0:
+                key_acc[...] = key_part
+                value_acc[...] = value_part
+            else:
+                key_acc[...] += key_part
+                value_acc[...] += value_part
+        out_ref[HEAD_DIM : 2 * HEAD_DIM, :] = (key_acc[...] * scale).astype(jnp.bfloat16)
+        out_ref[2 * HEAD_DIM : 3 * HEAD_DIM, :] = value_acc[...].astype(jnp.bfloat16)
+        out_ref[3 * HEAD_DIM :, :] = jnp.zeros((SLOT - 3 * HEAD_DIM, seq), jnp.bfloat16)
+
+    return pl.pallas_call(
+        kernel,
+        out_shape=jax.ShapeDtypeStruct((planes * SLOT, seq), jnp.bfloat16),
+        grid=(planes,),
+        in_specs=[
+            smem(),
+            pl.BlockSpec((SLOT, seq), lambda h: (h, 0)),
+            pl.BlockSpec((HEAD_DIM, seq), lambda h: (h, 0)),
+            pl.BlockSpec((1, 1, seq), lambda h: (h, 0, 0)),
+        ],
+        out_specs=pl.BlockSpec((SLOT, seq), lambda h: (h, 0)),
+        scratch_shapes=[
+            pltpu.VMEM((seq, quarter), jnp.float32),
+            pltpu.VMEM((HEAD_DIM, seq), jnp.float32),
+            pltpu.VMEM((HEAD_DIM, seq), jnp.float32),
+        ],
+        compiler_params=pltpu.CompilerParams(vmem_limit_bytes=48 * MEGA),
+        name="attend_grad",
+    )(facts, qkv, context_grad, logs)
+
+
+def norm_back(values, gain, grad):
+    mean = jnp.mean(values, axis=-1, keepdims=True)
+    centre = values - mean
+    root = lax.rsqrt(jnp.mean(centre * centre, axis=-1, keepdims=True) + 1e-05)
+    unit = centre * root
+    scaled = grad * gain
+    part = root * (
+        scaled
+        - jnp.mean(scaled, axis=-1, keepdims=True)
+        - unit * jnp.mean(scaled * unit, axis=-1, keepdims=True)
+    )
+    return part, jnp.sum(grad * unit, axis=0), jnp.sum(grad, axis=0)
+
+
+def weights_home(kept, given, seat):
+    both = (kept.astype(jnp.float32) + core_swap(given).astype(jnp.float32)).astype(jnp.bfloat16)
+    owned = lax.psum_scatter(both, "tensor", scatter_dimension=0, tiled=False)
+    return [at_index(owned, seat)] + [
+        seat_swap(at_index(owned, seat ^ r), r) for r in range(1, SEATS)
+    ]
+
+
+def masked_scores(query_part, key_rows, valid, scale):
     scores = (
         jnp.einsum("qhe,khe->hqk", query_part, key_rows, preferred_element_type=jnp.float32) * scale
     )
     return jnp.where(valid[None, None, :], scores, masked_score)
 
 
-def attend_clip(query_rows, key_rows, value_rows, length, blocks):
+def attend_clip(query_rows, key_rows, value_rows, valid, blocks):
     seq, heads = (query_rows.shape[0], query_rows.shape[1])
     scale = HEAD_DIM ** (-0.5)
     query_blocks = query_rows.reshape(blocks, seq // blocks, heads, HEAD_DIM)
 
     def one_block(query_part):
-        scores = masked_scores(query_part, key_rows, length, scale)
+        scores = masked_scores(query_part, key_rows, valid, scale)
         top = jnp.max(scores, axis=-1, keepdims=True)
         expo = jnp.exp(scores - top)
         total = jnp.sum(expo, axis=-1, keepdims=True)
@@ -44,7 +380,7 @@
     return (context.reshape(seq, heads, HEAD_DIM), log_total)
 
 
-def attend_back(query_rows, key_rows, value_rows, context_grad, log_total, length, blocks):
+def attend_back(query_rows, key_rows, value_rows, context_grad, log_total, valid, blocks):
     seq, heads = (query_rows.shape[0], query_rows.shape[1])
     scale = HEAD_DIM ** (-0.5)
     query_blocks = query_rows.reshape(blocks, seq // blocks, heads, HEAD_DIM)
@@ -53,7 +389,7 @@
     def one_block(carry, inputs):
         key_acc, value_acc = carry
         query_part, grad_part, lse_part = inputs
-        scores = masked_scores(query_part, key_rows, length, scale)
+        scores = masked_scores(query_part, key_rows, valid, scale)
         probs = jnp.exp(scores - lse_part[..., None])
         value_acc = value_acc + jnp.einsum(
             "hqk,qhe->khe",
@@ -147,7 +483,8 @@
     )
 
     def clip_attend(item):
-        return attend_clip(item[0], item[1], item[2], item[3], blocks)
+        valid = lax.broadcasted_iota(jnp.int32, (seq,), 0) < item[3]
+        return attend_clip(item[0], item[1], item[2], valid, blocks)
 
     context, log_total = lax.map(clip_attend, (queries, keyed, valued, lengths))
     context = context.reshape(clips, seq, heads * HEAD_DIM)
@@ -240,11 +577,7 @@
         down_weight,
         down_bias,
     )
-    first = forward_pass(tokens, lengths, weights)
-    fenced_tokens, fenced_lengths, fenced_weights, fenced_output = lax.optimization_barrier(
-        (tokens, lengths, weights, first["output"])
-    )
-    saved = forward_pass(fenced_tokens, fenced_lengths, fenced_weights)
+    saved = forward_pass(tokens, lengths, weights)
     blocks = saved["blocks"]
     grad_out = cotangent.astype(jnp.float32)
     down_shift_grad = jnp.sum(grad_out, axis=(0, 1))
@@ -290,7 +623,8 @@
     clips, seq, heads = (queries.shape[0], queries.shape[1], queries.shape[2])
 
     def clip_back(item):
-        return attend_back(item[0], item[1], item[2], item[3], item[4], item[5], blocks)
+        valid = lax.broadcasted_iota(jnp.int32, (seq,), 0) < item[5]
+        return attend_back(item[0], item[1], item[2], item[3], item[4], valid, blocks)
 
     query_grad, key_grad, value_grad = lax.map(
         clip_back,
@@ -379,7 +713,7 @@
     )
     shared = lax.psum((query_shift_grad, value_shift_grad, up_shift_grad), "dp")
     return (
-        first["output"].astype(jnp.bfloat16),
+        saved["output"].astype(jnp.bfloat16),
         tokens_grad,
         owned[4],
         owned[5],
@@ -399,49 +733,241 @@
     )
 
 
+def plane_local(
+    tokens,
+    lengths,
+    cotangent,
+    ln1_gain,
+    ln1_bias,
+    query_weight,
+    query_bias,
+    key_weight,
+    value_weight,
+    value_bias,
+    out_weight,
+    out_bias,
+    ln2_gain,
+    ln2_bias,
+    up_weight,
+    up_bias,
+    down_weight,
+    down_bias,
+):
+    planes = lax.axis_size("tensor")
+    core, seat = lax.axis_index("core"), lax.axis_index("seat")
+    plane = lax.axis_index("tensor")
+    seat_word, core_word = seat.reshape(1), core.reshape(1)
+    quarter, width = tokens.shape[1], tokens.shape[2]
+    rows_of = query_weight.shape[0]
+    wide = query_weight.shape[1]
+    hidden_of = up_weight.shape[1] // SEATS
+    low, full = jnp.bfloat16, jnp.float32
+    group = ("core", "tensor")
+
+    vectors = jnp.stack([ln1_gain, ln1_bias, out_bias, ln2_gain, ln2_bias, down_bias])
+    sizes = jnp.stack([lengths // 8, lengths % 8], axis=1).astype(low)
+    extra = jnp.concatenate(
+        [
+            jnp.pad(vectors, ((0, 0), (0, SLOT - rows_of))),
+            jnp.pad(sizes, ((0, 0), (0, SLOT - 2))),
+            jnp.zeros((EXTRA - 7, SLOT), low),
+        ]
+    )
+    heads_shift = jnp.concatenate(
+        [
+            query_bias.reshape(SEATS, HEAD_DIM),
+            jnp.zeros((SEATS, HEAD_DIM), low),
+            value_bias.reshape(SEATS, HEAD_DIM),
+            jnp.zeros((SEATS, SLOT - 3 * HEAD_DIM), low),
+        ],
+        axis=1,
+    )
+    line = lax.broadcasted_iota(jnp.int32, (1, EXTRA, 1), 1)
+    extra = jnp.where(line == 8, heads_shift[:, None, :], extra[None])
+    qkv_pieces = pack_weights(
+        [(0, 0, HEAD_DIM), (1, HEAD_DIM, HEAD_DIM), (2, 2 * HEAD_DIM, HEAD_DIM)],
+        SLOT,
+        [query_weight, key_weight, value_weight],
+        extra,
+        seat_word,
+    )
+    qkv_pieces = [qkv_pieces[0]] + [seat_swap(qkv_pieces[r], r) for r in range(1, SEATS)]
+    qkv_around = lax.all_gather(jnp.stack(qkv_pieces), group, axis=0)
+
+    rows_low = to_plane(tokens[0], seat, plane, planes)
+    tokens_all = plane_gather(rows_low)
+    seq = tokens_all.shape[0]
+
+    ff_extra = jnp.pad(
+        up_bias.reshape(SEATS, 1, hidden_of), ((0, 0), (0, EXTRA - 1), (0, hidden_of))
+    )
+    ff_pieces = pack_weights(
+        [(0, 0, hidden_of), (1, hidden_of, hidden_of)],
+        2 * hidden_of,
+        [up_weight, down_weight],
+        ff_extra,
+        seat_word,
+    )
+    ff_pieces = [ff_pieces[0]] + [seat_swap(ff_pieces[r], r) for r in range(1, SEATS)]
+    ff_around = lax.all_gather(jnp.stack(ff_pieces), group, axis=0)
+    out_around = lax.all_gather(out_weight, ("seat", "core", "tensor"), axis=0)
+    out_full = (
+        out_around.reshape(2 * SEATS, planes, rows_of, wide)
+        .transpose(0, 2, 1, 3)
+        .reshape(width, planes * wide)
+    )
+    out_part = lax.dynamic_index_in_dim(
+        out_full.reshape(width, planes, SEATS, HEAD_DIM), seat, 2, keepdims=False
+    ).reshape(width, planes * HEAD_DIM)
+
+    qkv_full, qkv_extra = assemble_weights([(0, SLOT)], qkv_around, seat_word, planes)
+    vectors = qkv_extra[:, ::planes, :6, :rows_of].astype(full)
+    gain_one, bias_one, out_shift, gain_two, bias_two, down_shift = (
+        vectors[:, :, k].reshape(width) for k in range(6)
+    )
+    qkv_shift = qkv_extra[0, :planes, 8].astype(full).reshape(planes * SLOT, 1)
+    size = lax.dynamic_index_in_dim(at_index(qkv_extra, plane), core * planes, 0, keepdims=False)
+    length = (8.0 * size[6, 0].astype(full) + size[6, 1].astype(full)).astype(jnp.int32)
+    facts = jnp.stack([length, seat, plane])
+
+    up_full, down_full, ff_extra = assemble_weights(
+        [(0, hidden_of), (hidden_of, hidden_of)], ff_around, seat_word, planes
+    )
+    up_shift = ff_extra[0, :planes, 0, :hidden_of].astype(full).reshape(planes * hidden_of)
+
+    cot_low = to_plane(cotangent[0], seat, plane, planes)
+    cot_all = plane_gather(cot_low)
+
+    rows = rows_low.astype(full)
+    normed_all = layer_norm(tokens_all.astype(full), gain_one, bias_one).astype(low)
+    qkv = (dot(qkv_full, normed_all, (0, 1)) + qkv_shift).astype(low)
+    context, *context_parts, logs = attend(facts, qkv, planes, quarter)
+    context_own = jnp.zeros((planes, SEATS, HEAD_DIM, quarter), low)
+    for r in range(SEATS):
+        part = seat_swap(context_parts[r - 1], r) if r else context[:, :quarter]
+        context_own = lax.dynamic_update_index_in_dim(
+            context_own, part.reshape(planes, HEAD_DIM, quarter), seat ^ r, 1
+        )
+    context_own = context_own.reshape(planes * wide, quarter)
+    middle = rows + dot(context_own, out_full, (0, 1)) + out_shift
+    normed_two = layer_norm(middle, gain_two, bias_two).astype(low)
+    normed_two_all = plane_gather(normed_two)
+    hidden_grad = dot(cot_all, down_full, (1, 0))
+    hidden_pre = dot(normed_two_all, up_full, (1, 0)) + up_shift
+    normal = 0.5 * (1.0 + lax.erf(hidden_pre * (0.5**0.5)))
+    slope = normal + hidden_pre * (jnp.exp(-0.5 * hidden_pre * hidden_pre) * (0.5 / jnp.pi) ** 0.5)
+    hidden = (hidden_pre * normal).astype(low)
+    pre_grad = (hidden_grad * slope).astype(low)
+
+    normed_two_grad = plane_scatter(dot(pre_grad, up_full, (1, 1)))
+    mixed = plane_scatter(dot(hidden, down_full, (1, 1)))
+    output = (middle + mixed + down_shift).astype(low)
+    output_home = from_plane(output, seat, plane, planes)
+    grad_out = cot_low.astype(full)
+    middle_part, gain_two_grad, bias_two_grad = norm_back(middle, gain_two, normed_two_grad)
+    middle_grad = grad_out + middle_part
+    middle_low = middle_grad.astype(low)
+    middle_all = plane_gather(middle_low)
+
+    def by_owner(sums, columns):
+        placed = jnp.stack(sums).reshape(len(sums), SEATS, 2, rows_of).transpose(1, 2, 0, 3)
+        return jnp.pad(
+            placed, ((0, 0), (0, 0), (0, EXTRA - len(sums)), (0, columns - rows_of))
+        )
+
+    up_grad = dot(normed_two_all, pre_grad, (0, 0)).astype(low)
+    down_grad = dot(cot_all, hidden, (0, 0)).astype(low)
+    up_shift_grad = jnp.sum(pre_grad, axis=0, dtype=full).reshape(planes, 1, hidden_of)
+    ff_kept, ff_given = pack_grads(
+        [(0, hidden_of, 0, hidden_of), (1, hidden_of, hidden_of, hidden_of)],
+        2 * hidden_of,
+        [up_grad, down_grad],
+        by_owner(
+            [gain_two_grad, bias_two_grad, jnp.sum(middle_grad, axis=0), jnp.sum(grad_out, axis=0)],
+            2 * hidden_of,
+        ),
+        jnp.pad(up_shift_grad, ((0, 0), (0, 0), (0, hidden_of))),
+        core_word,
+        planes,
+    )
+    ff_home = weights_home(ff_kept, ff_given, seat)
+    up_home, down_home, ff_rest = finish_grads(
+        [(0, hidden_of), (hidden_of, hidden_of)], ff_home, seat_word
+    )
+    ff_sums = jnp.sum(ff_rest[:, :4, :rows_of], axis=0)
+    up_shift_home = ff_rest[:, 8, :hidden_of].reshape(SEATS * hidden_of)
+
+    context_grad = dot(out_part, middle_all, (0, 1)).astype(low)
+    out_grad = dot(middle_all, context, (0, 1)).astype(low)
+    qkv_grad = attend_grad(facts, qkv, context_grad, logs, planes, quarter)
+    normed_grad = plane_scatter(dot(qkv_grad, qkv_full, (0, 1)))
+    tokens_part, gain_one_grad, bias_one_grad = norm_back(rows, gain_one, normed_grad)
+    tokens_grad = (middle_grad + tokens_part).astype(low)
+    tokens_grad_home = from_plane(tokens_grad, seat, plane, planes)
+    ones = jnp.concatenate([gain_one_grad, bias_one_grad])
+    ones = ones + core_swap(ones)
+    for bits in (1, 2):
+        ones = ones + seat_swap(ones, bits)
+    for bits in (1, 2):
+        ones = ones + plane_swap(ones, bits, planes)
+    ones = lax.dynamic_slice_in_dim(
+        ones.reshape(2, width), (2 * seat + core) * rows_of, rows_of, 1
+    )
+
+    qkv_weight_grad = dot(normed_all, qkv_grad, (0, 1)).astype(low)
+    qkv_shift_grad = jnp.sum(qkv_grad, axis=1, dtype=full).reshape(planes, 1, SLOT)
+    columns = 4 * HEAD_DIM
+    qkv_kept, qkv_given = pack_grads(
+        [(0, SLOT, 0, 3 * HEAD_DIM), (1, HEAD_DIM, 3 * HEAD_DIM, HEAD_DIM)],
+        columns,
+        [qkv_weight_grad, out_grad],
+        jnp.zeros((SEATS, 2, EXTRA, columns), full),
+        jnp.pad(qkv_shift_grad, ((0, 0), (0, 0), (0, columns - SLOT))),
+        core_word,
+        planes,
+    )
+    qkv_home = weights_home(qkv_kept, qkv_given, seat)
+    query_home, key_home, value_home, out_home, qkv_rest = finish_grads(
+        [(k * HEAD_DIM, HEAD_DIM) for k in range(4)], qkv_home, seat_word
+    )
+    query_shift_home = qkv_rest[:, 8, :HEAD_DIM].reshape(wide)
+    value_shift_home = qkv_rest[:, 8, 2 * HEAD_DIM : 3 * HEAD_DIM].reshape(wide)
+
+    return (
+        output_home[None],
+        tokens_grad_home[None].astype(full),
+        ones[0],
+        ones[1],
+        query_home,
+        query_shift_home,
+        key_home,
+        value_home,
+        value_shift_home,
+        out_home,
+        ff_sums[2],
+        ff_sums[0],
+        ff_sums[1],
+        up_home,
+        up_shift_home,
+        down_home,
+        ff_sums[3],
+    )
+
+
+def specs(rows, columns):
+    both = (P(rows, columns, None), P(rows), P(rows, columns), P(columns))
+    cube, first, matrix, second = both
+    ins = (cube, first, cube, first, first, matrix, second, matrix, matrix, second, matrix)
+    ins += (first, first, first, matrix, second, matrix, first)
+    outs = (cube, cube, first, first, matrix, second, matrix, matrix, second, matrix)
+    outs += (first, first, first, matrix, second, matrix, first)
+    return ins, outs
+
+
 def solution(mesh):
-    placed = (
-        P("dp", "tensor", None),
-        P("dp"),
-        P("dp", "tensor", None),
-        P("dp"),
-        P("dp"),
-        P("dp", "tensor"),
-        P("tensor"),
-        P("dp", "tensor"),
-        P("dp", "tensor"),
-        P("tensor"),
-        P("dp", "tensor"),
-        P("dp"),
-        P("dp"),
-        P("dp"),
-        P("dp", "tensor"),
-        P("tensor"),
-        P("dp", "tensor"),
-        P("dp"),
-    )
-    return jax.shard_map(
-        local,
-        mesh=mesh,
-        in_specs=placed,
-        out_specs=(
-            P("dp", "tensor", None),
-            P("dp", "tensor", None),
-            P("dp"),
-            P("dp"),
-            P("dp", "tensor"),
-            P("tensor"),
-            P("dp", "tensor"),
-            P("dp", "tensor"),
-            P("tensor"),
-            P("dp", "tensor"),
-            P("dp"),
-            P("dp"),
-            P("dp"),
-            P("dp", "tensor"),
-            P("tensor"),
-            P("dp", "tensor"),
-            P("dp"),
-        ),
-        check_vma=False,
-    )
+    step, rows = local, "dp"
+    if mesh.shape["dp"] == 2 * SEATS and mesh.shape["tensor"] == SEATS:
+        devices = mesh.devices.reshape(SEATS, 2, SEATS)
+        step, rows, mesh = plane_local, ("seat", "core"), Mesh(devices, ("seat", "core", "tensor"))
+    ins, outs = specs(rows, "tensor")
+    return jax.shard_map(step, mesh=mesh, in_specs=ins, out_specs=outs, check_vma=False)

time: 1140 us -> 562 us (0.49)
  waiting for transfers between devices: 629 us -> 215 us
  blocking collectives: 203 us -> 0 us
  matrix products: 190 us -> 55.4 us
  starting transfers between devices: 2.3 us -> 96.1 us
  local copies, waits for them, and re-layouts: 34.6 us -> 99.4 us
  Pallas kernels: 0 us -> 41.7 us
  other arithmetic: 61 us -> 30.9 us
    reduce_scatter x10 -> x2, waiting for transfers between devices: 354 us -> 24.3 us  [weights_home(): owned = lax.psum_scatter(both, 'tensor', scatter_dimension=0, tiled=False)]
    all_gather x10 -> x3, waiting for transfers between devices: 272 us -> 0.01 us  [the longest x1 0.01 us: plane_local(): qkv_around = lax.all_gather(jnp.stack(qkv_pieces), group, axis=0)]
    ppermute x0 -> x74, waiting for transfers between devices: none -> 190 us  [the longest x57 136 us: seat_swap(): return lax.ppermute(values, 'seat', [(k, k ^ bits) for k in range(SEATS)])]
    dot_general x38 -> x12, matrix products: 175 us -> 55.4 us  [dot(): lax.dot_general(left, right, (((dims[0],), (dims[1],)), ((), ())), prefer...]
    ppermute x0 -> x74, starting transfers between devices: none -> 95.6 us  [the longest x57 67.7 us: seat_swap(): return lax.ppermute(values, 'seat', [(k, k ^ bits) for k in range(SEATS)])]
    all_gather x8 -> x0, blocking collectives: 88.5 us -> none  [the longest x2 22.8 us: forward_pass(): lax.all_gather(out_weight, 'dp', axis=0, tiled=True)]
    unnamed x3 -> x0, blocking collectives: 71.7 us -> none
    psum x2 -> x0, blocking collectives: 42.4 us -> none  [the longest x1 24.7 us: local(): shared = lax.psum((query_shift_grad, value_shift_grad, up_shift_grad), 'dp')]
  transfers between devices with their start and end apart: 21 -> 79, of which waited for: 17 -> 42; matrix products, arithmetic and copies ran while one was open for 12% -> 21% of each run, Pallas kernels for 0% -> 3%
where the time goes in v2:
time: 562 us; the launch traced here: 556 us
  waiting for transfers between devices  215 us (38%)
  local copies, waits for them, and re-layouts  99.4 us (18%)
  starting transfers between devices  96.1 us (17%)
  matrix products  55.4 us (10%)
  Pallas kernels  41.7 us (7%)
  other arithmetic  30.9 us (5%)
  between operations  17.2 us (3%)
    ppermute x57, waiting for transfers between devices, seat_swap(): return lax.ppermute(values, 'seat', [(k, k ^ bits) for k in range(SEATS)])  136 us
    ppermute x57, starting transfers between devices, seat_swap(): return lax.ppermute(values, 'seat', [(k, k ^ bits) for k in range(SEATS)])  67.7 us
    dot_general x12, matrix products, dot(): lax.dot_general(left, right, (((dims[0],), (dims[1],)), ((), ())), prefer...  55.4 us
    ppermute x14, waiting for transfers between devices, plane_swap(): lax.ppermute(values, 'tensor', [(k, k ^ bits) for k in range(planes)])  52.7 us
    unnamed x116, local copies, waits for them, and re-layouts  39.2 us
    ppermute x14, starting transfers between devices, plane_swap(): lax.ppermute(values, 'tensor', [(k, k ^ bits) for k in range(planes)])  27.8 us
    reduce_scatter x2, waiting for transfers between devices, weights_home(): owned = lax.psum_scatter(both, 'tensor', scatter_dimension=0, tiled=False)  24.3 us
    pallas_call x1, Pallas kernels, attend_grad(): pl.pallas_call(kernel, out_shape=jax.ShapeDtypeStruct((planes * SLOT, seq...  16.9 us
  transfers between devices with their start and end apart: 79, of which 42 were waited for; matrix products, arithmetic and copies ran while one was open for 21% of the time, Pallas kernels for 3%

profile of v2, /device:TPU:0, one launch (start us, length us, event | category | flops | bytes accessed | tf_op | source)
XLA Modules:
  0.0 555.5 jit_solution(8244545799906965817)
XLA Ops:
  35.3 4.6 collective-permute-done.20
  64.7 14.0 %collective-permute-done.38 = bf16[64,1280]{1,0:T(8,128)(2,1)S(1)} collective-permute-done((bf16[64,1280]{1,0:T(8,128)(2,1)S(1)}, bf16[64,1280]{1,0:T(8,128)(2,1)S(1)}, u32[]{:S(2)}, u32[]{:S(2)}) %collective-permute-start.38) | collective-permute-done | bytes 163872 | tf_op jit(solution)/shard_map/ppermute | solution.py:44
  78.7 9.6 %collective-permute-start.36 = (bf16[64,1280]{1,0:T(8,128)(2,1)S(1)}, bf16[64,1280]{1,0:T(8,128)(2,1)S(1)}, u32[]{:S(2)}, u32[]{:S(2)}) collective-permute-start(bf16[64,1280]{1,0:T(8,128)(2,1)S(1)} %get-tuple-element.146), channel_id=1, source_target_pairs={{0,1},{1,0},{2,3},{3,2},{4,5},{5,4},{6,7},{7,6},{8,9},{9,8},{10,11... | collective-permute-start | bytes 491528 | tf_op jit(solution)/shard_map/ppermute | solution.py:44
  100.2 11.9 %collective-permute-done.40 = bf16[256,1280]{1,0:T(8,128)(2,1)S(1)} collective-permute-done((bf16[256,1280]{1,0:T(8,128)(2,1)S(1)}, bf16[256,1280]{1,0:T(8,128)(2,1)S(1)}, u32[]{:S(2)}, u32[]{:S(2)}) %collective-permute-start.40) | collective-permute-done | bytes 655392 | tf_op jit(solution)/shard_map/ppermute | solution.py:36
  117.4 9.8 %collective-permute-done.10 = bf16[256,1280]{1,0:T(8,128)(2,1)S(1)} collective-permute-done((bf16[256,1280]{1,0:T(8,128)(2,1)S(1)}, bf16[256,1280]{1,0:T(8,128)(2,1)S(1)}, u32[]{:S(2)}, u32[]{:S(2)}) %collective-permute-start.10) | collective-permute-done | bytes 655392 | tf_op jit(solution)/shard_map/ppermute | solution.py:36
  131.2 15.9 %collective-permute-done.11 = bf16[128,1280]{1,0:T(8,128)(2,1)S(1)} collective-permute-done((bf16[128,1280]{1,0:T(8,128)(2,1)S(1)}, bf16[128,1280]{1,0:T(8,128)(2,1)S(1)}, u32[]{:S(2)}, u32[]{:S(2)}) %collective-permute-start.11) | collective-permute-done | bytes 327712 | tf_op jit(solution)/shard_map/ppermute | solution.py:36
  158.4 6.0 %add_convert_fusion.2.qkv_ref = bf16[1024,1024]{1,0:T(8,128)(2,1)S(1)} fusion(f32[1024]{0:T(1024)S(1)} %bitcast.203, bf16[1280,1024]{1,0:T(8,128)(2,1)} %copy-done.18, bf16[1024,1280]{1,0:T(8,128)(2,1)} %copy-done.23, f32[1280]{0:T(1024)S(1)} %add.287, f32[1280]{0:T(1024)S(1)} %mul.161, f32[1024]{0:T(1024)S(1)} %add_rsqrt_fusion, ...), kind=kOutput, calls=%fused_computation.23 | convolution fusion | flops 2694316032 | bytes 7362560 | tf_op jit(solution)/shard_map/dot_general | solution.py:30
  164.4 12.5 %attend.1 = (bf16[320,1024]{1,0:T(8,128)(2,1)S(1)}, bf16[320,256]{1,0:T(8,128)(2,1)S(1)}, bf16[320,256]{1,0:T(8,128)(2,1)S(1)}, bf16[320,256]{1,0:T(8,128)(2,1)S(1)}, f32[4,1,1024]{2,1,0:T(1,128)S(1)}) custom-call(s32[3]{0:T(128)S(1)} %pad_add_fusion.facts_ref, bf16[1024,1024]{1,0:T(8,128)(2,1)S(1)} %add_convert_fusion.2.qkv_ref), custom_call_target="tpu_custom_call" | custom-call | tf_op jit(solution)/shard_map/attend/pallas_call | solution.py:264
  188.9 6.1 %copy.57 = bf16[8,160,4,320]{3,2,1,0:T(4,128)(2,1)} copy(bf16[8,160,4,320]{3,1,2,0:T(8,128)(2,1)} %bitcast.169) | data formatting | bytes 6553600 | tf_op jit(solution)/shard_map/transpose | solution.py:816
  195.0 8.2 %reshape.304 = bf16[1280,1280]{1,0:T(8,128)(2,1)} reshape(bf16[8,160,4,320]{3,2,1,0:T(4,128)(2,1)} %copy.57) | data formatting | bytes 6553600 | tf_op jit(solution)/shard_map/reshape | solution.py:817
  215.0 7.6 %collective-permute-done.17 = bf16[256,1280]{1,0:T(8,128)(2,1)S(1)} collective-permute-done((bf16[256,1280]{1,0:T(8,128)(2,1)S(1)}, bf16[256,1280]{1,0:T(8,128)(2,1)S(1)}, u32[]{:S(2)}, u32[]{:S(2)}) %collective-permute-start.17) | collective-permute-done | bytes 655392 | tf_op jit(solution)/shard_map/ppermute | solution.py:36
  242.1 7.0 %multiply_convert_fusion = (bf16[1024,1280]{1,0:T(8,128)(2,1)S(1)}, f32[1024,1280]{1,0:T(8,128)S(1)}) fusion(f32[1280]{0:T(1024)S(1)} %reshape.312, bf16[1024,1280]{1,0:T(8,128)(2,1)} %constant_dynamic-update-slice_fusion.8, bf16[1280,1280]{1,0:T(8,128)(2,1)} %copy-done.14), kind=kOutput, calls=%fused_computation.19 | convolution fusion | flops 3363307520 | bytes 13767680 | tf_op jit(solution)/shard_map/dot_general | solution.py:30
  252.7 5.8 %convert_reduce_fusion.1 = (f32[1280]{0:T(1024)S(1)}, bf16[1024,1280]{1,0:T(8,128)(2,1)S(1)}) fusion(f32[1024,1280]{1,0:T(8,128)S(1)} %get-tuple-element.187, f32[1280]{0:T(1024)S(1)} %reshape.312, bf16[1024,1280]{1,0:T(8,128)(2,1)S(1)} %copy-done.42, bf16[1280,1280]{1,0:T(8,128)(2,1)S(1)} %copy-done.17), kind=kOutput, calls=%fused_computation.18 | convolution fusion | flops 3372481280 | bytes 13772800 | tf_op jit(solution)/shard_map/dot_general | solution.py:30
  269.6 5.0 collective-permute-done.43
  286.0 9.6 %collective-permute-done.46 = bf16[256,1280]{1,0:T(8,128)(2,1)} collective-permute-done((bf16[256,1280]{1,0:T(8,128)(2,1)}, bf16[256,1280]{1,0:T(8,128)(2,1)}, u32[]{:S(2)}, u32[]{:S(2)}) %collective-permute-start.46) | collective-permute-done | bytes 655392 | tf_op jit(solution)/shard_map/ppermute | solution.py:36
  298.5 4.1 collective-permute-done.26
  310.4 8.5 %copy.56 = bf16[8,4,160,320]{2,0,3,1:T(8,128)(2,1)} copy(bf16[8,4,160,320]{3,2,1,0:T(8,128)(2,1)} %bitcast.170) | data formatting | bytes 6553600 | tf_op jit(solution)/shard_map/reshape | solution.py:815
  318.9 9.2 %reshape_reshape.3 = bf16[1280,4,4,80]{0,3,2,1:T(8,128)(2,1)} reshape(bf16[8,160,4,320]{1,0,3,2:T(8,128)(2,1)} %bitcast.168) | data formatting | bytes 6553600 | tf_op jit(solution)/shard_map/reshape;reshape | solution.py:820
  346.7 16.9 %attend_grad.1 = bf16[1024,1024]{1,0:T(8,128)(2,1)S(1)} custom-call(s32[3]{0:T(128)S(1)} %pad_add_fusion.facts_ref, bf16[1024,1024]{1,0:T(8,128)(2,1)S(1)} %add_convert_fusion.2.qkv_ref, bf16[320,1024]{1,0:T(8,128)(2,1)S(1)} %convolution_convert_fusion.4.grad_ref, f32[4,1,1024]{2,1,0:T(1,128)S(1)} %get-tuple-element.64.log_ref), custom_call_target="tpu_custom_call" | custom-call | tf_op jit(solution)/shard_map/attend_grad/pallas_call | solution.py:313
  363.7 5.4 convolution_convert_fusion.2.refs_0_
  375.1 6.2 %convolution_convert_fusion.1.refs_0_ = bf16[1280,1280]{1,0:T(8,128)(2,1)S(1)} fusion(bf16[1024,1280]{1,0:T(8,128)(2,1)} %constant_dynamic-update-slice_fusion.8, bf16[1024,1280]{1,0:T(8,128)(2,1)S(1)} %copy-done.47), kind=kOutput, calls=%fused_computation.2 | convolution fusion | flops 3357081600 | bytes 8519680 | tf_op jit(solution)/shard_map/dot_general | solution.py:30
  381.3 5.0 convolution_convert_fusion.refs_1_
  398.5 4.2 collective-permute-start.29
  403.3 6.3 %add_convert_fusion = bf16[4,4,176,640]{3,2,1,0:T(8,128)(2,1)} fusion(bf16[4,4,176,640]{3,2,1,0:T(8,128)(2,1)} %collective-permute-done.70, bf16[4,4,176,640]{3,2,1,0:T(8,128)(2,1)} %copy-done.3), kind=kLoop, calls=%fused_computation.3 | loop fusion | flops 7208960 | bytes 10813440 | tf_op jit(solution)/shard_map/convert_element_type | solution.py:349
  411.2 4.7 fusion.56
  418.3 4.8 collective-permute-done.28
  432.7 16.6 %collective-permute-done.32 = bf16[64,1280]{1,0:T(8,128)(2,1)S(1)} collective-permute-done((bf16[64,1280]{1,0:T(8,128)(2,1)S(1)}, bf16[64,1280]{1,0:T(8,128)(2,1)S(1)}, u32[]{:S(2)}, u32[]{:S(2)}) %collective-permute-start.32) | collective-permute-done | bytes 163872 | tf_op jit(solution)/shard_map/ppermute | solution.py:36
  462.9 19.8 %collective-permute-done.64 = f32[2560]{0:T(1024)S(1)} collective-permute-done((f32[2560]{0:T(1024)S(1)}, f32[2560]{0:T(1024)S(1)}, u32[]{:S(2)}, u32[]{:S(2)}) %collective-permute-start.64) | collective-permute-done | bytes 10272 | tf_op jit(solution)/shard_map/ppermute | solution.py:44
  482.8 8.1 %collective-permute-done.56 = bf16[64,1280]{1,0:T(8,128)(2,1)S(1)} collective-permute-done((bf16[64,1280]{1,0:T(8,128)(2,1)S(1)}, bf16[64,1280]{1,0:T(8,128)(2,1)S(1)}, u32[]{:S(2)}, u32[]{:S(2)}) %collective-permute-start.56) | collective-permute-done | bytes 163872 | tf_op jit(solution)/shard_map/ppermute | solution.py:44
  497.6 4.4 collective-permute-done.59
  506.9 24.3 %reduce-scatter.5.cloned.1.call-done = bf16[1,4,176,640]{3,2,1,0:T(8,128)(2,1)} async-done(((bf16[4,4,176,640]{3,2,1,0:T(8,128)(2,1)}), bf16[1,4,176,640]{3,2,1,0:T(8,128)(2,1)}) %reduce-scatter.5.cloned.1.call-update) | async-done | bytes 901136 | tf_op jit(solution)/shard_map/reduce_scatter | solution.py:350
  541.9 3.9 collective-permute-done.72.refs_2_
  (412 shorter events, 252.2 us)
Async XLA Ops:
  7.2 144.6 %all-gather.7.cloned.1.call-start = ((), (), s32[]{:S(2)}) async-start(), calls=%async_computation.4 | async-start | bytes 3244032 | tf_op jit(solution)/shard_map/all_gather | solution.py:795
  27.8 161.1 %all-gather.9.cloned.1.call-start = ((), (), s32[]{:S(2)}) async-start(), calls=%async_computation.5 | async-start | bytes 4055040 | tf_op jit(solution)/shard_map/all_gather | solution.py:813
  28.5 204.5 %all-gather.11.cloned.1.call-start = ((), (), s32[]{:S(2)}) async-start(), calls=%async_computation.6 | async-start | bytes 8110080 | tf_op jit(solution)/shard_map/all_gather | solution.py:812
  44.1 458.0 %reduce-scatter.3.cloned.1.call-start = ((), (), s32[]{:S(2)}) async-start(), calls=%async_computation.2 | async-start | bytes 2703360 | tf_op jit(solution)/shard_map/reduce_scatter | solution.py:350
  55.7 41.0 %collective-permute-start.5 = (bf16[64,1280]{1,0:T(8,128)(2,1)S(1)}, bf16[64,1280]{1,0:T(8,128)(2,1)S(1)}, u32[]{:S(2)}, u32[]{:S(2)}) collective-permute-start(bf16[64,1280]{1,0:T(8,128)(2,1)S(1)} %get-tuple-element.163), channel_id=1, source_target_pairs={{0,3},{1,2},{2,1},{3,0},{4,7},{5,6},{6,5},{7,4},{8,11},{9,10},{10,... | collective-permute-start | bytes 491528 | tf_op jit(solution)/shard_map/ppermute | solution.py:44
  59.4 37.4 %collective-permute-start.4 = (bf16[64,1280]{1,0:T(8,128)(2,1)S(1)}, bf16[64,1280]{1,0:T(8,128)(2,1)S(1)}, u32[]{:S(2)}, u32[]{:S(2)}) collective-permute-start(bf16[64,1280]{1,0:T(8,128)(2,1)S(1)} %get-tuple-element.164), channel_id=1, source_target_pairs={{0,2},{1,3},{2,0},{3,1},{4,6},{5,7},{6,4},{7,5},{8,10},{9,11},{10,... | collective-permute-start | bytes 491528 | tf_op jit(solution)/shard_map/ppermute | solution.py:44
  59.4 37.4 %collective-permute-start.3 = (bf16[64,1280]{1,0:T(8,128)(2,1)S(1)}, bf16[64,1280]{1,0:T(8,128)(2,1)S(1)}, u32[]{:S(2)}, u32[]{:S(2)}) collective-permute-start(bf16[64,1280]{1,0:T(8,128)(2,1)S(1)} %get-tuple-element.165), channel_id=1, source_target_pairs={{0,1},{1,0},{2,3},{3,2},{4,5},{5,4},{6,7},{7,6},{8,9},{9,8},{10,11... | collective-permute-start | bytes 491528 | tf_op jit(solution)/shard_map/ppermute | solution.py:44
  64.0 26.4 %collective-permute-start.37 = (bf16[64,1280]{1,0:T(8,128)(2,1)S(1)}, bf16[64,1280]{1,0:T(8,128)(2,1)S(1)}, u32[]{:S(2)}, u32[]{:S(2)}) collective-permute-start(bf16[64,1280]{1,0:T(8,128)(2,1)S(1)} %get-tuple-element.145), channel_id=1, source_target_pairs={{0,2},{1,3},{2,0},{3,1},{4,6},{5,7},{6,4},{7,5},{8,10},{9,11},{10,... | collective-permute-start | bytes 491528 | tf_op jit(solution)/shard_map/ppermute | solution.py:44
  95.3 19.7 %collective-permute-start.39 = (bf16[256,1280]{1,0:T(8,128)(2,1)S(1)}, bf16[256,1280]{1,0:T(8,128)(2,1)S(1)}, u32[]{:S(2)}, u32[]{:S(2)}) collective-permute-start(bf16[256,1280]{1,0:T(8,128)(2,1)S(1)} %get-tuple-element.96), channel_id=1, source_target_pairs={{0,8},{8,0},{16,24},{24,16},{1,9},{9,1},{17,25},{25,17},{2,10},{10... | collective-permute-start | bytes 1966088 | tf_op jit(solution)/shard_map/ppermute | solution.py:36
  96.9 30.3 %collective-permute-start.10 = (bf16[256,1280]{1,0:T(8,128)(2,1)S(1)}, bf16[256,1280]{1,0:T(8,128)(2,1)S(1)}, u32[]{:S(2)}, u32[]{:S(2)}) collective-permute-start(bf16[256,1280]{1,0:T(8,128)(2,1)S(1)} %get-tuple-element.99), channel_id=1, source_target_pairs={{0,16},{8,24},{16,0},{24,8},{1,17},{9,25},{17,1},{25,9},{2,18},{10... | collective-permute-start | bytes 1966088 | tf_op jit(solution)/shard_map/ppermute | solution.py:36
  97.6 32.9 %collective-permute-start.9 = (bf16[256,1280]{1,0:T(8,128)(2,1)S(1)}, bf16[256,1280]{1,0:T(8,128)(2,1)S(1)}, u32[]{:S(2)}, u32[]{:S(2)}) collective-permute-start(bf16[256,1280]{1,0:T(8,128)(2,1)S(1)} %get-tuple-element.99), channel_id=1, source_target_pairs={{0,8},{8,0},{16,24},{24,16},{1,9},{9,1},{17,25},{25,17},{2,10},{10... | collective-permute-start | bytes 1966088 | tf_op jit(solution)/shard_map/ppermute | solution.py:36
  112.9 100.3 %collective-permute-start.42 = (bf16[128,1280]{1,0:T(8,128)(2,1)}, bf16[128,1280]{1,0:T(8,128)(2,1)}, u32[]{:S(2)}, u32[]{:S(2)}) collective-permute-start(bf16[128,1280]{1,0:T(8,128)(2,1)} %slice.310), channel_id=1, source_target_pairs={{0,8},{8,0},{16,24},{24,16},{1,9},{9,1},{17,25},{25,17},{2,10},{10... | collective-permute-start | bytes 983048 | tf_op jit(solution)/shard_map/ppermute | solution.py:36
  115.8 95.6 %collective-permute-start.41 = (bf16[128,1280]{1,0:T(8,128)(2,1)}, bf16[128,1280]{1,0:T(8,128)(2,1)}, u32[]{:S(2)}, u32[]{:S(2)}) collective-permute-start(bf16[128,1280]{1,0:T(8,128)(2,1)} %slice.309), channel_id=1, source_target_pairs={{0,16},{8,24},{16,0},{24,8},{1,17},{9,25},{17,1},{25,9},{2,18},{10... | collective-permute-start | bytes 983048 | tf_op jit(solution)/shard_map/ppermute | solution.py:36
  127.3 22.9 %collective-permute-start.12 = (bf16[128,1280]{1,0:T(8,128)(2,1)S(1)}, bf16[128,1280]{1,0:T(8,128)(2,1)S(1)}, u32[]{:S(2)}, u32[]{:S(2)}) collective-permute-start(bf16[128,1280]{1,0:T(8,128)(2,1)S(1)} %slice.289), channel_id=1, source_target_pairs={{0,8},{8,0},{16,24},{24,16},{1,9},{9,1},{17,25},{25,17},{2,10},{10... | collective-permute-start | bytes 983048 | tf_op jit(solution)/shard_map/ppermute | solution.py:36
  275.6 20.0 %collective-permute-start.46 = (bf16[256,1280]{1,0:T(8,128)(2,1)}, bf16[256,1280]{1,0:T(8,128)(2,1)}, u32[]{:S(2)}, u32[]{:S(2)}) collective-permute-start(bf16[256,1280]{1,0:T(8,128)(2,1)} %pad_maximum_fusion.10), channel_id=1, source_target_pairs={{0,16},{8,24},{16,0},{24,8},{1,17},{9,25},{17,1},{25,9},{2,18},{10... | collective-permute-start | bytes 1966088 | tf_op jit(solution)/shard_map/ppermute | solution.py:36
  282.7 19.9 %collective-permute-start.26 = (bf16[256,1280]{1,0:T(8,128)(2,1)}, bf16[256,1280]{1,0:T(8,128)(2,1)S(1)}, u32[]{:S(2)}, u32[]{:S(2)}) collective-permute-start(bf16[256,1280]{1,0:T(8,128)(2,1)} %pad_maximum_fusion.4), channel_id=1, source_target_pairs={{0,16},{8,24},{16,0},{24,8},{1,17},{9,25},{17,1},{25,9},{2,18},{10... | collective-permute-start | bytes 1966088 | tf_op jit(solution)/shard_map/ppermute | solution.py:36
  307.9 22.3 %collective-permute-start.48 = (bf16[256,1280]{1,0:T(8,128)(2,1)}, bf16[256,1280]{1,0:T(8,128)(2,1)}, u32[]{:S(2)}, u32[]{:S(2)}) collective-permute-start(bf16[256,1280]{1,0:T(8,128)(2,1)} %get-tuple-element.101), channel_id=1, source_target_pairs={{0,16},{8,24},{16,0},{24,8},{1,17},{9,25},{17,1},{25,9},{2,18},{10... | collective-permute-start | bytes 1966088 | tf_op jit(solution)/shard_map/ppermute | solution.py:36
  309.1 23.1 %collective-permute-start.47 = (bf16[256,1280]{1,0:T(8,128)(2,1)}, bf16[256,1280]{1,0:T(8,128)(2,1)}, u32[]{:S(2)}, u32[]{:S(2)}) collective-permute-start(bf16[256,1280]{1,0:T(8,128)(2,1)} %get-tuple-element.101), channel_id=1, source_target_pairs={{0,8},{8,0},{16,24},{24,16},{1,9},{9,1},{17,25},{25,17},{2,10},{10... | collective-permute-start | bytes 1966088 | tf_op jit(solution)/shard_map/ppermute | solution.py:36
  397.4 133.8 %reduce-scatter.5.cloned.1.call-start = ((), (), s32[]{:S(2)}) async-start(), calls=%async_computation.3 | async-start | bytes 4505600 | tf_op jit(solution)/shard_map/reduce_scatter | solution.py:350
  398.5 19.8 %collective-permute-start.29 = (bf16[64,1280]{1,0:T(8,128)(2,1)S(1)}, bf16[64,1280]{1,0:T(8,128)(2,1)S(1)}, u32[]{:S(2)}, u32[]{:S(2)}) collective-permute-start(bf16[64,1280]{1,0:T(8,128)(2,1)S(1)} %get-tuple-element.160), channel_id=1, source_target_pairs={{0,3},{1,2},{2,1},{3,0},{4,7},{5,6},{6,5},{7,4},{8,11},{9,10},{10,... | collective-permute-start | bytes 491528 | tf_op jit(solution)/shard_map/ppermute | solution.py:44
  402.7 20.4 %collective-permute-start.28 = (bf16[64,1280]{1,0:T(8,128)(2,1)S(1)}, bf16[64,1280]{1,0:T(8,128)(2,1)S(1)}, u32[]{:S(2)}, u32[]{:S(2)}) collective-permute-start(bf16[64,1280]{1,0:T(8,128)(2,1)S(1)} %get-tuple-element.161), channel_id=1, source_target_pairs={{0,2},{1,3},{2,0},{3,1},{4,6},{5,7},{6,4},{7,5},{8,10},{9,11},{10,... | collective-permute-start | bytes 491528 | tf_op jit(solution)/shard_map/ppermute | solution.py:44
  402.7 21.1 %collective-permute-start.27 = (bf16[64,1280]{1,0:T(8,128)(2,1)S(1)}, bf16[64,1280]{1,0:T(8,128)(2,1)S(1)}, u32[]{:S(2)}, u32[]{:S(2)}) collective-permute-start(bf16[64,1280]{1,0:T(8,128)(2,1)S(1)} %get-tuple-element.162), channel_id=1, source_target_pairs={{0,1},{1,0},{2,3},{3,2},{4,5},{5,4},{6,7},{7,6},{8,9},{9,8},{10,11... | collective-permute-start | bytes 491528 | tf_op jit(solution)/shard_map/ppermute | solution.py:44
  427.1 22.9 %collective-permute-start.54 = (bf16[256,1280]{1,0:T(8,128)(2,1)S(1)}, bf16[256,1280]{1,0:T(8,128)(2,1)S(1)}, u32[]{:S(2)}, u32[]{:S(2)}) collective-permute-start(bf16[256,1280]{1,0:T(8,128)(2,1)S(1)} %pad_maximum_fusion.12), channel_id=1, source_target_pairs={{0,16},{8,24},{16,0},{24,8},{1,17},{9,25},{17,1},{25,9},{2,18},{10... | collective-permute-start | bytes 1966088 | tf_op jit(solution)/shard_map/ppermute | solution.py:36
  427.5 22.5 %collective-permute-start.52 = (bf16[256,1280]{1,0:T(8,128)(2,1)S(1)}, bf16[256,1280]{1,0:T(8,128)(2,1)S(1)}, u32[]{:S(2)}, u32[]{:S(2)}) collective-permute-start(bf16[256,1280]{1,0:T(8,128)(2,1)S(1)} %pad_maximum_fusion.11), channel_id=1, source_target_pairs={{0,8},{8,0},{16,24},{24,16},{1,9},{9,1},{17,25},{25,17},{2,10},{10... | collective-permute-start | bytes 1966088 | tf_op jit(solution)/shard_map/ppermute | solution.py:36
  429.2 20.2 %collective-permute-start.32 = (bf16[64,1280]{1,0:T(8,128)(2,1)S(1)}, bf16[64,1280]{1,0:T(8,128)(2,1)S(1)}, u32[]{:S(2)}, u32[]{:S(2)}) collective-permute-start(bf16[64,1280]{1,0:T(8,128)(2,1)S(1)} %get-tuple-element.156), channel_id=1, source_target_pairs={{0,24},{8,16},{16,8},{24,0},{1,25},{9,17},{17,9},{25,1},{2,26},{10... | collective-permute-start | bytes 491528 | tf_op jit(solution)/shard_map/ppermute | solution.py:36
  457.6 25.2 %collective-permute-start.57 = (bf16[64,1280]{1,0:T(8,128)(2,1)S(1)}, bf16[64,1280]{1,0:T(8,128)(2,1)S(1)}, u32[]{:S(2)}, u32[]{:S(2)}) collective-permute-start(bf16[64,1280]{1,0:T(8,128)(2,1)S(1)} %get-tuple-element.141), channel_id=1, source_target_pairs={{0,3},{1,2},{2,1},{3,0},{4,7},{5,6},{6,5},{7,4},{8,11},{9,10},{10,... | collective-permute-start | bytes 491528 | tf_op jit(solution)/shard_map/ppermute | solution.py:44
  460.8 30.0 %collective-permute-start.56 = (bf16[64,1280]{1,0:T(8,128)(2,1)S(1)}, bf16[64,1280]{1,0:T(8,128)(2,1)S(1)}, u32[]{:S(2)}, u32[]{:S(2)}) collective-permute-start(bf16[64,1280]{1,0:T(8,128)(2,1)S(1)} %get-tuple-element.142), channel_id=1, source_target_pairs={{0,2},{1,3},{2,0},{3,1},{4,6},{5,7},{6,4},{7,5},{8,10},{9,11},{10,... | collective-permute-start | bytes 491528 | tf_op jit(solution)/shard_map/ppermute | solution.py:44
  460.8 30.0 %collective-permute-start.55 = (bf16[64,1280]{1,0:T(8,128)(2,1)S(1)}, bf16[64,1280]{1,0:T(8,128)(2,1)S(1)}, u32[]{:S(2)}, u32[]{:S(2)}) collective-permute-start(bf16[64,1280]{1,0:T(8,128)(2,1)S(1)} %get-tuple-element.143), channel_id=1, source_target_pairs={{0,1},{1,0},{2,3},{3,2},{4,5},{5,4},{6,7},{7,6},{8,9},{9,8},{10,11... | collective-permute-start | bytes 491528 | tf_op jit(solution)/shard_map/ppermute | solution.py:44
  462.0 20.8 %collective-permute-start.64 = (f32[2560]{0:T(1024)S(1)}, f32[2560]{0:T(1024)S(1)}, u32[]{:S(2)}, u32[]{:S(2)}) collective-permute-start(f32[2560]{0:T(1024)S(1)} %add.326), channel_id=1, source_target_pairs={{0,1},{1,0},{2,3},{3,2},{4,5},{5,4},{6,7},{7,6},{8,9},{9,8},{10,11... | collective-permute-start | bytes 30728 | tf_op jit(solution)/shard_map/ppermute | solution.py:44
  503.3 31.3 %collective-permute-start.69 = (bf16[176,320]{1,0:T(8,128)(2,1)S(1)}, bf16[176,320]{1,0:T(8,128)(2,1)S(1)}, u32[]{:S(2)}, u32[]{:S(2)}) collective-permute-start(bf16[176,320]{1,0:T(8,128)(2,1)S(1)} %get-tuple-element.170), channel_id=1, source_target_pairs={{0,24},{8,16},{16,8},{24,0},{1,25},{9,17},{17,9},{25,1},{2,26},{10... | collective-permute-start | bytes 337928 | tf_op jit(solution)/shard_map/ppermute | solution.py:36
  504.6 32.6 %collective-permute-start.68 = (bf16[176,320]{1,0:T(8,128)(2,1)S(1)}, bf16[176,320]{1,0:T(8,128)(2,1)S(1)}, u32[]{:S(2)}, u32[]{:S(2)}) collective-permute-start(bf16[176,320]{1,0:T(8,128)(2,1)S(1)} %get-tuple-element.171), channel_id=1, source_target_pairs={{0,16},{8,24},{16,0},{24,8},{1,17},{9,25},{17,1},{25,9},{2,18},{10... | collective-permute-start | bytes 337928 | tf_op jit(solution)/shard_map/ppermute | solution.py:36
  505.4 31.7 %collective-permute-start.67 = (bf16[176,320]{1,0:T(8,128)(2,1)S(1)}, bf16[176,320]{1,0:T(8,128)(2,1)S(1)}, u32[]{:S(2)}, u32[]{:S(2)}) collective-permute-start(bf16[176,320]{1,0:T(8,128)(2,1)S(1)} %get-tuple-element.172), channel_id=1, source_target_pairs={{0,8},{8,0},{16,24},{24,16},{1,9},{9,1},{17,25},{25,17},{2,10},{10... | collective-permute-start | bytes 337928 | tf_op jit(solution)/shard_map/ppermute | solution.py:36
  (95 other events, 892.6 us)
Sparse Core Ops, SparseCore 0:
  27.9 54.0 all-gather.6
  84.8 69.0 all-gather.8
  155.6 71.0 all-gather.10
  397.5 53.0 reduce-scatter.2
  452.8 78.2 reduce-scatter.4

commit v3 on v2

--- a/solution.py
+++ b/solution.py
@@ -48,11 +48,18 @@
     return lax.dynamic_index_in_dim(stack, index, 0, keepdims=False)
 
 
-def to_plane(rows, seat, plane, planes):
+def after(value, *others):
+    return lax.optimization_barrier((value, others))[0]
+
+
+def leave_seat(rows, seat):
     parts = rows.reshape(SEATS, -1, rows.shape[1])
-    got = jnp.stack(
+    return jnp.stack(
         [at_index(parts, seat)] + [seat_swap(at_index(parts, seat ^ r), r) for r in range(1, SEATS)]
     )
+
+
+def leave_plane(got, seat, plane, planes):
     turn = seat ^ plane
     return jnp.concatenate(
         [at_index(got, turn)]
@@ -70,14 +77,21 @@
     return jnp.concatenate([at_index(back, s ^ seat) for s in range(SEATS)])
 
 
-def plane_gather(own):
+def gather_near(own):
+    return own, seat_swap(own, 1), seat_swap(own, 2)
+
+
+def gather_far(own, across, along):
     half = own.shape[0] // 2
-    across, along = seat_swap(own, 1), seat_swap(own, 2)
     far_a, far_b = seat_swap(across[:half], 2), seat_swap(along[half:], 1)
     return jnp.concatenate([own, across, along, far_a, far_b])
 
 
-def plane_scatter(terms):
+def plane_gather(own):
+    return gather_far(*gather_near(own))
+
+
+def scatter_far(terms):
     rows = terms.shape[0] // SEATS
     half = rows // 2
     own, across, along, far = (terms[k * rows : (k + 1) * rows] for k in range(SEATS))
@@ -85,8 +99,12 @@
     far_a, far_b = seat_swap(far[:half], 1), seat_swap(far[half:], 2)
     along = jnp.concatenate([along[:half] + far_a.astype(jnp.float32), along[half:]])
     across = jnp.concatenate([across[:half], across[half:] + far_b.astype(jnp.float32)])
-    along = seat_swap(along.astype(jnp.bfloat16), 2).astype(jnp.float32)
-    across = seat_swap(across.astype(jnp.bfloat16), 1).astype(jnp.float32)
+    return own, across.astype(jnp.bfloat16), along.astype(jnp.bfloat16)
+
+
+def scatter_near(own, across, along):
+    along = seat_swap(along, 2).astype(jnp.float32)
+    across = seat_swap(across, 1).astype(jnp.float32)
     return own + across + along
 
 
@@ -94,113 +112,166 @@
     return pl.BlockSpec(memory_space=pltpu.SMEM)
 
 
-def vmem():
-    return pl.BlockSpec(memory_space=pltpu.VMEM)
-
-
-def pack_weights(plan, columns, sources, extra, seat):
+def whole(array):
+    return pl.BlockSpec(array.shape, lambda *_: (0,) * len(array.shape))
+
+
+def pack_heads(sources, vectors, shifts, lengths, seat):
     rows = sources[0].shape[0]
-
-    def kernel(seat_ref, *refs):
-        inputs, extra_ref = refs[: len(sources)], refs[len(sources)]
-        outs, held = refs[len(sources) + 1 : -1], refs[-1]
-        used = max(lane + size for _, lane, size in plan)
+    columns = len(sources) * HEAD_DIM
+    query_shift, value_shift, up_shift = shifts
+    hidden_of = up_shift.shape[1] // SEATS
+
+    def kernel(seat_ref, length_ref, *refs):
+        inputs, vector_ref, query_ref, value_ref, up_ref = refs[:4], *refs[4:8]
+        outs, held, tile = refs[8:-2], refs[-2], refs[-1]
+        tile[...] = jnp.zeros_like(tile)
+        tile[:6, :rows] = vector_ref[...].astype(jnp.float32)
+        lane = lax.broadcasted_iota(jnp.int32, (1, columns), 1)
+        high, low = length_ref[0] // 8, length_ref[0] % 8
+        tile[6:7, :] = jnp.where(lane == 0, high, jnp.where(lane == 1, low, 0)).astype(jnp.float32)
         for j in range(SEATS):
-            for k, lane, size in plan:
-                held[j, :rows, lane : lane + size] = inputs[k][:, j * size : (j + 1) * size]
-            if used < columns:
-                held[j, :rows, used:] = jnp.zeros((rows, columns - used), jnp.bfloat16)
-            held[j, rows:, :] = extra_ref[j]
+            of = slice(j * HEAD_DIM, (j + 1) * HEAD_DIM)
+            for k in range(len(sources)):
+                held[j, :rows, k * HEAD_DIM : (k + 1) * HEAD_DIM] = inputs[k][:, of]
+            tile[8:9, :HEAD_DIM] = query_ref[:, of].astype(jnp.float32)
+            tile[8:9, 2 * HEAD_DIM : 3 * HEAD_DIM] = value_ref[:, of].astype(jnp.float32)
+            tile[9:10, :hidden_of] = up_ref[:, j * hidden_of : (j + 1) * hidden_of].astype(
+                jnp.float32
+            )
+            held[j, rows:, :] = tile[...].astype(jnp.bfloat16)
         for r in range(SEATS):
             outs[r][...] = held[seat_ref[0] ^ r]
 
     piece = jax.ShapeDtypeStruct((rows + EXTRA, columns), jnp.bfloat16)
+    arrays = [*sources, vectors, *shifts]
     return pl.pallas_call(
         kernel,
         out_shape=[piece] * SEATS,
-        in_specs=[smem()] + [vmem()] * (len(sources) + 1),
-        out_specs=[vmem()] * SEATS,
-        scratch_shapes=[pltpu.VMEM((SEATS, rows + EXTRA, columns), jnp.bfloat16)],
+        grid=(1,),
+        in_specs=[smem(), smem()] + [whole(a) for a in arrays],
+        out_specs=[whole(piece)] * SEATS,
+        scratch_shapes=[
+            pltpu.VMEM((SEATS, rows + EXTRA, columns), jnp.bfloat16),
+            pltpu.VMEM((EXTRA, columns), jnp.float32),
+        ],
         compiler_params=pltpu.CompilerParams(vmem_limit_bytes=16 * MEGA),
-        name="pack_weights",
-    )(seat, *sources, extra)
-
-
-def assemble_weights(plan, gathered, seat, planes):
+        name="pack_heads",
+    )(seat, lengths, *arrays)
+
+
+def pack_hidden(sources, seat):
+    rows, size = sources[0].shape[0], sources[0].shape[1] // SEATS
+    columns = len(sources) * size
+
+    def kernel(seat_ref, *refs):
+        inputs, outs, held = refs[: len(sources)], refs[len(sources) : -1], refs[-1]
+        for j in range(SEATS):
+            for k in range(len(sources)):
+                held[j, :, k * size : (k + 1) * size] = inputs[k][:, j * size : (j + 1) * size]
+        for r in range(SEATS):
+            outs[r][...] = held[seat_ref[0] ^ r]
+
+    piece = jax.ShapeDtypeStruct((rows, columns), jnp.bfloat16)
+    return pl.pallas_call(
+        kernel,
+        out_shape=[piece] * SEATS,
+        grid=(1,),
+        in_specs=[smem()] + [whole(a) for a in sources],
+        out_specs=[whole(piece)] * SEATS,
+        scratch_shapes=[pltpu.VMEM((SEATS, rows, columns), jnp.bfloat16)],
+        compiler_params=pltpu.CompilerParams(vmem_limit_bytes=16 * MEGA),
+        name="pack_hidden",
+    )(seat, *sources)
+
+
+def assemble_weights(plan, gathered, seat, planes, extra):
     groups, _, tall, columns = gathered.shape
-    rows = tall - EXTRA
+    rows = tall - extra
 
     def kernel(seat_ref, in_ref, *outs):
         del seat_ref
         for c in range(2):
+            of = slice(c * rows, (c + 1) * rows)
             for z in range(planes):
-                for k, (lane, size) in enumerate(plan):
-                    outs[k][c * rows : (c + 1) * rows, z * size : (z + 1) * size] = in_ref[
+                for k, (lane, size, stride) in enumerate(plan):
+                    at = z * stride
+                    outs[k][of, at : at + size] = in_ref[
                         c * planes + z, 0, :rows, lane : lane + size
                     ]
-        outs[-1][0] = in_ref[:, 0, rows:, :]
-
+                    if size < stride:
+                        outs[k][of, at + size : at + stride] = jnp.zeros(
+                            (rows, stride - size), jnp.bfloat16
+                        )
+        if extra:
+            outs[-1][0] = in_ref[:, 0, rows:, :]
+
+    shapes = [
+        jax.ShapeDtypeStruct((SEATS * 2 * rows, planes * stride), jnp.bfloat16)
+        for _, _, stride in plan
+    ]
+    blocks = [pl.BlockSpec((2 * rows, planes * stride), lambda s, seat: (s, 0)) for _, _, stride in plan]
+    if extra:
+        shapes += [jax.ShapeDtypeStruct((SEATS, groups, extra, columns), jnp.bfloat16)]
+        blocks += [pl.BlockSpec((1, groups, extra, columns), lambda s, seat: (s, 0, 0, 0))]
     return pl.pallas_call(
         kernel,
-        out_shape=[
-            jax.ShapeDtypeStruct((SEATS * 2 * rows, planes * size), jnp.bfloat16)
-            for _, size in plan
-        ]
-        + [jax.ShapeDtypeStruct((SEATS, groups, EXTRA, columns), jnp.bfloat16)],
+        out_shape=shapes,
         grid_spec=pltpu.PrefetchScalarGridSpec(
             num_scalar_prefetch=1,
             grid=(SEATS,),
             in_specs=[
                 pl.BlockSpec((groups, 1, tall, columns), lambda s, seat: (0, s ^ seat[0], 0, 0))
             ],
-            out_specs=[
-                pl.BlockSpec((2 * rows, planes * size), lambda s, seat: (s, 0)) for _, size in plan
-            ]
-            + [pl.BlockSpec((1, groups, EXTRA, columns), lambda s, seat: (s, 0, 0, 0))],
+            out_specs=blocks,
         ),
         compiler_params=pltpu.CompilerParams(vmem_limit_bytes=24 * MEGA),
         name="assemble_weights",
     )(seat, gathered)
 
 
-def pack_grads(plan, columns, sources, vectors, shift, core, planes):
+def pack_grads(plan, columns, sources, core, planes, vectors=None, shifts=None):
     rows = sources[0].shape[0] // (2 * SEATS)
-    tall = rows + EXTRA
+    extra = 0 if vectors is None else EXTRA
+    tall = rows + extra
 
     def kernel(core_ref, *refs):
-        inputs, vec_ref, shift_ref = refs[: len(sources)], refs[len(sources)], refs[-3]
+        inputs = refs[: len(sources)]
         for out, c in ((refs[-2], core_ref[0]), (refs[-1], 1 - core_ref[0])):
             start = pl.multiple_of(c * rows, 16)
-            tile = vec_ref[0, c]
-            line = lax.broadcasted_iota(jnp.int32, tile.shape, 0)
             for z in range(planes):
                 for k, stride, lane, size in plan:
                     out[z, 0, :rows, lane : lane + size] = inputs[k][
                         pl.ds(start, rows), z * stride : z * stride + size
                     ]
-                out[z, 0, rows:, :] = jnp.where(line == 8, shift_ref[z], tile).astype(jnp.bfloat16)
+                if extra:
+                    vec_ref, shift_ref = refs[len(sources) : len(sources) + 2]
+                    out[z, 0, rows:, :] = (vec_ref[0, c] + shift_ref[z]).astype(jnp.bfloat16)
 
     chunk = jax.ShapeDtypeStruct((planes, SEATS, tall, columns), jnp.bfloat16)
     block = pl.BlockSpec((planes, 1, tall, columns), lambda s: (0, s, 0, 0))
+    in_specs = [pl.BlockSpec((2 * rows, a.shape[1]), lambda s: (s, 0)) for a in sources]
+    more = []
+    if extra:
+        more = [vectors, shifts]
+        in_specs += [
+            pl.BlockSpec((1, 2, EXTRA, columns), lambda s: (s, 0, 0, 0)),
+            pl.BlockSpec((planes, EXTRA, columns), lambda s: (0, 0, 0)),
+        ]
     return pl.pallas_call(
         kernel,
         out_shape=[chunk, chunk],
         grid=(SEATS,),
-        in_specs=[smem()]
-        + [pl.BlockSpec((2 * rows, a.shape[1]), lambda s: (s, 0)) for a in sources]
-        + [
-            pl.BlockSpec((1, 2, EXTRA, columns), lambda s: (s, 0, 0, 0)),
-            pl.BlockSpec((planes, 1, columns), lambda s: (0, 0, 0)),
-        ],
+        in_specs=[smem()] + in_specs,
         out_specs=[block, block],
         compiler_params=pltpu.CompilerParams(vmem_limit_bytes=32 * MEGA),
         name="pack_grads",
-    )(core, *sources, vectors, shift)
-
-
-def finish_grads(plan, pieces, seat):
+    )(core, *sources, *more)
+
+
+def finish_grads(plan, pieces, seat, extra):
     tall, columns = pieces[0].shape
-    rows = tall - EXTRA
+    rows = tall - extra
 
     def kernel(seat_ref, *refs):
         outs, held = refs[SEATS:-1], refs[-1]
@@ -211,14 +282,18 @@
                 outs[k][:, j * size : (j + 1) * size] = held[j, :rows, lane : lane + size].astype(
                     jnp.float32
                 )
-            outs[-1][j] = held[j, rows:, :].astype(jnp.float32)
-
+            if extra:
+                outs[-1][j] = held[j, rows:, :].astype(jnp.float32)
+
+    shapes = [jax.ShapeDtypeStruct((rows, SEATS * size), jnp.float32) for _, size in plan]
+    if extra:
+        shapes += [jax.ShapeDtypeStruct((SEATS, extra, columns), jnp.float32)]
     return pl.pallas_call(
         kernel,
-        out_shape=[jax.ShapeDtypeStruct((rows, SEATS * size), jnp.float32) for _, size in plan]
-        + [jax.ShapeDtypeStruct((SEATS, EXTRA, columns), jnp.float32)],
-        in_specs=[smem()] + [vmem()] * SEATS,
-        out_specs=[vmem()] * (len(plan) + 1),
+        out_shape=shapes,
+        grid=(1,),
+        in_specs=[smem()] + [whole(p) for p in pieces],
+        out_specs=[whole(s) for s in shapes],
         scratch_shapes=[pltpu.VMEM((SEATS, tall, columns), jnp.bfloat16)],
         compiler_params=pltpu.CompilerParams(vmem_limit_bytes=24 * MEGA),
         name="finish_grads",
@@ -238,8 +313,7 @@
     seq = qkv.shape[1]
     scale = HEAD_DIM ** (-0.5) * LOG2E
 
-    def kernel(facts_ref, qkv_ref, all_ref, *refs):
-        outs, log_ref, shift_ref = refs[: SEATS - 1], refs[-2], refs[-1]
+    def kernel(facts_ref, qkv_ref, out_ref, log_ref, shift_ref):
 
         @pl.when(pl.program_id(0) == 0)
         def _():
@@ -254,22 +328,16 @@
             expo = jnp.exp2(scores - top)
             total = jnp.sum(expo, axis=0, keepdims=True)
             context = dot(values, expo.astype(jnp.bfloat16), (1, 0)) / total
-            context = context.astype(jnp.bfloat16)
-            all_ref[:, at] = context
-            if r:
-                outs[r - 1][...] = context
+            out_ref[:, at] = context.astype(jnp.bfloat16)
             log_ref[0, :, at] = top + jnp.log2(total)
 
-    head = pl.BlockSpec((HEAD_DIM, quarter), lambda h: (h, 0))
     return pl.pallas_call(
         kernel,
         out_shape=[jax.ShapeDtypeStruct((planes * HEAD_DIM, seq), jnp.bfloat16)]
-        + [jax.ShapeDtypeStruct((planes * HEAD_DIM, quarter), jnp.bfloat16)] * (SEATS - 1)
         + [jax.ShapeDtypeStruct((planes, 1, seq), jnp.float32)],
         grid=(planes,),
         in_specs=[smem(), pl.BlockSpec((SLOT, seq), lambda h: (h, 0))],
         out_specs=[pl.BlockSpec((HEAD_DIM, seq), lambda h: (h, 0))]
-        + [head] * (SEATS - 1)
         + [pl.BlockSpec((1, 1, seq), lambda h: (h, 0, 0))],
         scratch_shapes=[pltpu.VMEM((seq, quarter), jnp.float32)],
         compiler_params=pltpu.CompilerParams(vmem_limit_bytes=40 * MEGA),
@@ -345,9 +413,11 @@
     return part, jnp.sum(grad * unit, axis=0), jnp.sum(grad, axis=0)
 
 
-def weights_home(kept, given, seat):
-    both = (kept.astype(jnp.float32) + core_swap(given).astype(jnp.float32)).astype(jnp.bfloat16)
-    owned = lax.psum_scatter(both, "tensor", scatter_dimension=0, tiled=False)
+def over_cores(kept, given):
+    return (kept.astype(jnp.float32) + core_swap(given).astype(jnp.float32)).astype(jnp.bfloat16)
+
+
+def seat_home(owned, seat):
     return [at_index(owned, seat)] + [
         seat_swap(at_index(owned, seat ^ r), r) for r in range(1, SEATS)
     ]
@@ -764,94 +834,72 @@
     low, full = jnp.bfloat16, jnp.float32
     group = ("core", "tensor")
 
-    vectors = jnp.stack([ln1_gain, ln1_bias, out_bias, ln2_gain, ln2_bias, down_bias])
-    sizes = jnp.stack([lengths // 8, lengths % 8], axis=1).astype(low)
-    extra = jnp.concatenate(
-        [
-            jnp.pad(vectors, ((0, 0), (0, SLOT - rows_of))),
-            jnp.pad(sizes, ((0, 0), (0, SLOT - 2))),
-            jnp.zeros((EXTRA - 7, SLOT), low),
-        ]
-    )
-    heads_shift = jnp.concatenate(
-        [
-            query_bias.reshape(SEATS, HEAD_DIM),
-            jnp.zeros((SEATS, HEAD_DIM), low),
-            value_bias.reshape(SEATS, HEAD_DIM),
-            jnp.zeros((SEATS, SLOT - 3 * HEAD_DIM), low),
-        ],
-        axis=1,
-    )
-    line = lax.broadcasted_iota(jnp.int32, (1, EXTRA, 1), 1)
-    extra = jnp.where(line == 8, heads_shift[:, None, :], extra[None])
-    qkv_pieces = pack_weights(
-        [(0, 0, HEAD_DIM), (1, HEAD_DIM, HEAD_DIM), (2, 2 * HEAD_DIM, HEAD_DIM)],
-        SLOT,
-        [query_weight, key_weight, value_weight],
-        extra,
+    vectors = jnp.concatenate([ln1_gain, ln1_bias, out_bias, ln2_gain, ln2_bias, down_bias])
+    head_pieces = pack_heads(
+        [query_weight, key_weight, value_weight, out_weight],
+        vectors.reshape(6, rows_of),
+        [query_bias[None], value_bias[None], up_bias[None]],
+        lengths,
         seat_word,
     )
-    qkv_pieces = [qkv_pieces[0]] + [seat_swap(qkv_pieces[r], r) for r in range(1, SEATS)]
-    qkv_around = lax.all_gather(jnp.stack(qkv_pieces), group, axis=0)
-
-    rows_low = to_plane(tokens[0], seat, plane, planes)
-    tokens_all = plane_gather(rows_low)
+    tokens_got = leave_seat(tokens[0], seat)
+    head_pieces = after(head_pieces, tokens_got)
+    head_pieces = [head_pieces[0]] + [seat_swap(head_pieces[r], r) for r in range(1, SEATS)]
+    head_pieces = jnp.stack(head_pieces)
+    heads_around = lax.all_gather(head_pieces, group, axis=0)
+
+    rows_low = leave_plane(tokens_got, seat, plane, planes)
+    tokens_near = gather_near(rows_low)
+    tokens_all = gather_far(*tokens_near)
     seq = tokens_all.shape[0]
 
-    ff_extra = jnp.pad(
-        up_bias.reshape(SEATS, 1, hidden_of), ((0, 0), (0, EXTRA - 1), (0, hidden_of))
-    )
-    ff_pieces = pack_weights(
-        [(0, 0, hidden_of), (1, hidden_of, hidden_of)],
-        2 * hidden_of,
-        [up_weight, down_weight],
-        ff_extra,
+    ff_pieces = pack_hidden([up_weight, down_weight], seat_word)
+    ff_pieces = after(ff_pieces, head_pieces)
+    ff_pieces = [ff_pieces[0]] + [seat_swap(ff_pieces[r], r) for r in range(1, SEATS)]
+    ff_pieces = jnp.stack(ff_pieces)
+    ff_around = lax.all_gather(ff_pieces, group, axis=0)
+
+    cot_got = leave_seat(after(cotangent[0], tokens_near), seat)
+    cot_low = leave_plane(after(cot_got, tokens_all, heads_around), seat, plane, planes)
+
+    qkv_full, out_part, extra = assemble_weights(
+        [(0, 3 * HEAD_DIM, SLOT), (3 * HEAD_DIM, HEAD_DIM, HEAD_DIM)],
+        heads_around,
         seat_word,
-    )
-    ff_pieces = [ff_pieces[0]] + [seat_swap(ff_pieces[r], r) for r in range(1, SEATS)]
-    ff_around = lax.all_gather(jnp.stack(ff_pieces), group, axis=0)
-    out_around = lax.all_gather(out_weight, ("seat", "core", "tensor"), axis=0)
-    out_full = (
-        out_around.reshape(2 * SEATS, planes, rows_of, wide)
-        .transpose(0, 2, 1, 3)
-        .reshape(width, planes * wide)
-    )
-    out_part = lax.dynamic_index_in_dim(
-        out_full.reshape(width, planes, SEATS, HEAD_DIM), seat, 2, keepdims=False
-    ).reshape(width, planes * HEAD_DIM)
-
-    qkv_full, qkv_extra = assemble_weights([(0, SLOT)], qkv_around, seat_word, planes)
-    vectors = qkv_extra[:, ::planes, :6, :rows_of].astype(full)
+        planes,
+        EXTRA,
+    )
+    vectors = extra[:, ::planes, :6, :rows_of].astype(full)
     gain_one, bias_one, out_shift, gain_two, bias_two, down_shift = (
         vectors[:, :, k].reshape(width) for k in range(6)
     )
-    qkv_shift = qkv_extra[0, :planes, 8].astype(full).reshape(planes * SLOT, 1)
-    size = lax.dynamic_index_in_dim(at_index(qkv_extra, plane), core * planes, 0, keepdims=False)
+    qkv_shift = jnp.pad(
+        extra[0, :planes, 8, : 3 * HEAD_DIM].astype(full), ((0, 0), (0, SLOT - 3 * HEAD_DIM))
+    ).reshape(planes * SLOT, 1)
+    up_shift = extra[0, :planes, 9, :hidden_of].astype(full).reshape(planes * hidden_of)
+    size = lax.dynamic_index_in_dim(at_index(extra, plane), core * planes, 0, keepdims=False)
     length = (8.0 * size[6, 0].astype(full) + size[6, 1].astype(full)).astype(jnp.int32)
     facts = jnp.stack([length, seat, plane])
-
-    up_full, down_full, ff_extra = assemble_weights(
-        [(0, hidden_of), (hidden_of, hidden_of)], ff_around, seat_word, planes
-    )
-    up_shift = ff_extra[0, :planes, 0, :hidden_of].astype(full).reshape(planes * hidden_of)
-
-    cot_low = to_plane(cotangent[0], seat, plane, planes)
-    cot_all = plane_gather(cot_low)
 
     rows = rows_low.astype(full)
     normed_all = layer_norm(tokens_all.astype(full), gain_one, bias_one).astype(low)
     qkv = (dot(qkv_full, normed_all, (0, 1)) + qkv_shift).astype(low)
-    context, *context_parts, logs = attend(facts, qkv, planes, quarter)
-    context_own = jnp.zeros((planes, SEATS, HEAD_DIM, quarter), low)
-    for r in range(SEATS):
-        part = seat_swap(context_parts[r - 1], r) if r else context[:, :quarter]
-        context_own = lax.dynamic_update_index_in_dim(
-            context_own, part.reshape(planes, HEAD_DIM, quarter), seat ^ r, 1
-        )
-    context_own = context_own.reshape(planes * wide, quarter)
-    middle = rows + dot(context_own, out_full, (0, 1)) + out_shift
+    qkv, cot_low = lax.optimization_barrier((qkv, cot_low))
+    cot_near = gather_near(cot_low)
+    context, logs = attend(facts, qkv, planes, quarter)
+    context, cot_near = lax.optimization_barrier((context, cot_near))
+    cot_all = gather_far(*cot_near)
+    attended = scatter_near(*scatter_far(dot(context, out_part, (0, 1))))
+    middle = rows + attended + out_shift
     normed_two = layer_norm(middle, gain_two, bias_two).astype(low)
     normed_two_all = plane_gather(normed_two)
+    up_full, down_full = assemble_weights(
+        [(0, hidden_of, hidden_of), (hidden_of, hidden_of, hidden_of)],
+        ff_around,
+        seat_word,
+        planes,
+        0,
+    )
     hidden_grad = dot(cot_all, down_full, (1, 0))
     hidden_pre = dot(normed_two_all, up_full, (1, 0)) + up_shift
     normal = 0.5 * (1.0 + lax.erf(hidden_pre * (0.5**0.5)))
@@ -859,51 +907,70 @@
     hidden = (hidden_pre * normal).astype(low)
     pre_grad = (hidden_grad * slope).astype(low)
 
-    normed_two_grad = plane_scatter(dot(pre_grad, up_full, (1, 1)))
-    mixed = plane_scatter(dot(hidden, down_full, (1, 1)))
-    output = (middle + mixed + down_shift).astype(low)
-    output_home = from_plane(output, seat, plane, planes)
+    terms = dot(pre_grad, up_full, (1, 1))
+    pre_grad_later = after(pre_grad, terms)
+    own, across, along = scatter_far(terms)
+    up_grad = dot(normed_two_all, pre_grad_later, (0, 0)).astype(low)
+    up_shift_grad = jnp.sum(pre_grad_later, axis=0, dtype=full).reshape(planes, hidden_of)
+    hidden_later = after(hidden, up_grad, across, along)
+    down_grad = dot(cot_all, hidden_later, (0, 0)).astype(low)
     grad_out = cot_low.astype(full)
+
+    ff_kept, ff_given = pack_grads(
+        [(0, hidden_of, 0, hidden_of), (1, hidden_of, hidden_of, hidden_of)],
+        2 * hidden_of,
+        [up_grad, down_grad],
+        core_word,
+        planes,
+    )
+    normed_two_grad = after(scatter_near(own, across, along), ff_given)
     middle_part, gain_two_grad, bias_two_grad = norm_back(middle, gain_two, normed_two_grad)
     middle_grad = grad_out + middle_part
     middle_low = middle_grad.astype(low)
     middle_all = plane_gather(middle_low)
-
-    def by_owner(sums, columns):
-        placed = jnp.stack(sums).reshape(len(sums), SEATS, 2, rows_of).transpose(1, 2, 0, 3)
-        return jnp.pad(
-            placed, ((0, 0), (0, 0), (0, EXTRA - len(sums)), (0, columns - rows_of))
-        )
-
-    up_grad = dot(normed_two_all, pre_grad, (0, 0)).astype(low)
-    down_grad = dot(cot_all, hidden, (0, 0)).astype(low)
-    up_shift_grad = jnp.sum(pre_grad, axis=0, dtype=full).reshape(planes, 1, hidden_of)
-    ff_kept, ff_given = pack_grads(
-        [(0, hidden_of, 0, hidden_of), (1, hidden_of, hidden_of, hidden_of)],
-        2 * hidden_of,
-        [up_grad, down_grad],
-        by_owner(
-            [gain_two_grad, bias_two_grad, jnp.sum(middle_grad, axis=0), jnp.sum(grad_out, axis=0)],
-            2 * hidden_of,
-        ),
-        jnp.pad(up_shift_grad, ((0, 0), (0, 0), (0, hidden_of))),
+    ff_both = over_cores(ff_kept, ff_given)
+    ff_owned = lax.psum_scatter(ff_both, "tensor", scatter_dimension=0, tiled=False)
+    mixed_terms = dot(after(hidden, middle_low, ff_both), down_full, (1, 1))
+    middle_all, context, mixed_terms = lax.optimization_barrier(
+        (middle_all, context, mixed_terms)
+    )
+    mixed = scatter_far(mixed_terms)
+
+    context_grad = dot(out_part, middle_all, (0, 1)).astype(low)
+    qkv_grad = attend_grad(facts, qkv, context_grad, logs, planes, quarter)
+    qkv_grad, mixed = lax.optimization_barrier((qkv_grad, mixed))
+    terms = dot(qkv_grad, qkv_full, (0, 1))
+    qkv_grad_later, middle_later = after((qkv_grad, middle_all), terms)
+    normed_grad = scatter_near(*scatter_far(terms))
+    qkv_weight_grad = dot(normed_all, qkv_grad_later, (0, 1)).astype(low)
+    out_grad = dot(middle_later, context, (0, 1)).astype(low)
+    qkv_shift_grad = jnp.sum(qkv_grad_later, axis=1, dtype=full).reshape(planes, SLOT)
+    columns = 4 * HEAD_DIM
+    sums = [gain_two_grad, bias_two_grad, jnp.sum(middle_grad, axis=0), jnp.sum(grad_out, axis=0)]
+    by_owner = jnp.stack(sums).reshape(len(sums), SEATS, 2, rows_of).transpose(1, 2, 0, 3)
+    shifts = jnp.stack(
+        [jnp.pad(qkv_shift_grad, ((0, 0), (0, columns - SLOT))), up_shift_grad], axis=1
+    )
+    heads_kept, heads_given = pack_grads(
+        [(0, SLOT, 0, 3 * HEAD_DIM), (1, HEAD_DIM, 3 * HEAD_DIM, HEAD_DIM)],
+        columns,
+        [qkv_weight_grad, out_grad],
         core_word,
         planes,
-    )
-    ff_home = weights_home(ff_kept, ff_given, seat)
-    up_home, down_home, ff_rest = finish_grads(
-        [(0, hidden_of), (hidden_of, hidden_of)], ff_home, seat_word
-    )
-    ff_sums = jnp.sum(ff_rest[:, :4, :rows_of], axis=0)
-    up_shift_home = ff_rest[:, 8, :hidden_of].reshape(SEATS * hidden_of)
-
-    context_grad = dot(out_part, middle_all, (0, 1)).astype(low)
-    out_grad = dot(middle_all, context, (0, 1)).astype(low)
-    qkv_grad = attend_grad(facts, qkv, context_grad, logs, planes, quarter)
-    normed_grad = plane_scatter(dot(qkv_grad, qkv_full, (0, 1)))
+        jnp.pad(by_owner, ((0, 0), (0, 0), (0, EXTRA - len(sums)), (0, columns - rows_of))),
+        jnp.pad(shifts, ((0, 0), (8, EXTRA - 10), (0, 0))),
+    )
+    heads_both, ff_owned = lax.optimization_barrier(
+        (over_cores(heads_kept, heads_given), ff_owned)
+    )
+    heads_owned = lax.psum_scatter(heads_both, "tensor", scatter_dimension=0, tiled=False)
+    normed_grad = after(normed_grad, heads_given)
+    mixed = scatter_near(*after(mixed, normed_grad))
+    output = (middle + mixed + down_shift).astype(low)
     tokens_part, gain_one_grad, bias_one_grad = norm_back(rows, gain_one, normed_grad)
     tokens_grad = (middle_grad + tokens_part).astype(low)
     tokens_grad_home = from_plane(tokens_grad, seat, plane, planes)
+    output_home = from_plane(output, seat, plane, planes)
     ones = jnp.concatenate([gain_one_grad, bias_one_grad])
     ones = ones + core_swap(ones)
     for bits in (1, 2):
@@ -914,24 +981,19 @@
         ones.reshape(2, width), (2 * seat + core) * rows_of, rows_of, 1
     )
 
-    qkv_weight_grad = dot(normed_all, qkv_grad, (0, 1)).astype(low)
-    qkv_shift_grad = jnp.sum(qkv_grad, axis=1, dtype=full).reshape(planes, 1, SLOT)
-    columns = 4 * HEAD_DIM
-    qkv_kept, qkv_given = pack_grads(
-        [(0, SLOT, 0, 3 * HEAD_DIM), (1, HEAD_DIM, 3 * HEAD_DIM, HEAD_DIM)],
-        columns,
-        [qkv_weight_grad, out_grad],
-        jnp.zeros((SEATS, 2, EXTRA, columns), full),
-        jnp.pad(qkv_shift_grad, ((0, 0), (0, 0), (0, columns - SLOT))),
-        core_word,
-        planes,
-    )
-    qkv_home = weights_home(qkv_kept, qkv_given, seat)
-    query_home, key_home, value_home, out_home, qkv_rest = finish_grads(
-        [(k * HEAD_DIM, HEAD_DIM) for k in range(4)], qkv_home, seat_word
-    )
-    query_shift_home = qkv_rest[:, 8, :HEAD_DIM].reshape(wide)
-    value_shift_home = qkv_rest[:, 8, 2 * HEAD_DIM : 3 * HEAD_DIM].reshape(wide)
+    up_home, down_home = finish_grads(
+        [(0, hidden_of), (hidden_of, hidden_of)], seat_home(ff_owned, seat), seat_word, 0
+    )
+    query_home, key_home, value_home, out_home, rest = finish_grads(
+        [(k * HEAD_DIM, HEAD_DIM) for k in range(4)],
+        seat_home(heads_owned, seat),
+        seat_word,
+        EXTRA,
+    )
+    sums = jnp.sum(rest[:, :4, :rows_of], axis=0)
+    query_shift_home = rest[:, 8, :HEAD_DIM].reshape(wide)
+    value_shift_home = rest[:, 8, 2 * HEAD_DIM : 3 * HEAD_DIM].reshape(wide)
+    up_shift_home = rest[:, 9, :hidden_of].reshape(SEATS * hidden_of)
 
     return (
         output_home[None],
@@ -944,13 +1006,13 @@
         value_home,
         value_shift_home,
         out_home,
-        ff_sums[2],
-        ff_sums[0],
-        ff_sums[1],
+        sums[2],
+        sums[0],
+        sums[1],
         up_home,
         up_shift_home,
         down_home,
-        ff_sums[3],
+        sums[3],
     )
 
 

time: 562 us -> 477 us (0.85)
  waiting for transfers between devices: 215 us -> 160 us
  local copies, waits for them, and re-layouts: 99.4 us -> 58.7 us
  starting transfers between devices: 96.1 us -> 103 us
  other arithmetic: 30.9 us -> 36.9 us
    ppermute x57 -> x58, waiting for transfers between devices: 136 us -> 99.6 us  [seat_swap(): return lax.ppermute(values, 'seat', [(k, k ^ bits) for k in range(SEATS)])]
    reduce_scatter x2, waiting for transfers between devices: 24.3 us -> 0.01 us  [the longest x1 0.01 us: plane_local(): lax.psum_scatter(ff_both, 'tensor', scatter_dimension=0, tiled=False)]
    reshape x6 -> x2, local copies, waits for them, and re-layouts: 19.1 us -> 0.1 us  [the longest x1 0.09 us: plane_local(): vectors.reshape(6, rows_of)]
    another operation x15 -> x9, local copies, waits for them, and re-layouts: 15.5 us -> 2.41 us  [the longest x1 0.67 us: plane_local(): up_shift_home = rest[:, 9, :hidden_of].reshape(SEATS * hidden_of)]
    unnamed x116 -> x101, local copies, waits for them, and re-layouts: 39.2 us -> 28.4 us
    ppermute x14, starting transfers between devices: 27.8 us -> 35.1 us  [plane_swap(): lax.ppermute(values, 'tensor', [(k, k ^ bits) for k in range(planes)])]
    ppermute x14, waiting for transfers between devices: 52.7 us -> 59.4 us  [plane_swap(): lax.ppermute(values, 'tensor', [(k, k ^ bits) for k in range(planes)])]
    transpose x1 -> x0, local copies, waits for them, and re-layouts: 6.06 us -> none  [plane_local(): out_full = out_around.reshape(2 * SEATS, planes, rows_of, wide).transpose...]
  transfers between devices with their start and end apart: 79 -> 79, of which waited for: 42 -> 39; matrix products, arithmetic and copies ran while one was open for 21% -> 21% of each run, Pallas kernels for 3% -> 8%
where the time goes in v3:
time: 477 us; the launch traced here: 470 us
  waiting for transfers between devices  160 us (34%)
  starting transfers between devices  103 us (22%)
  local copies, waits for them, and re-layouts  58.7 us (12%)
  matrix products  52.2 us (11%)
  Pallas kernels  42.3 us (9%)
  other arithmetic  36.9 us (8%)
  between operations  17.2 us (4%)
    ppermute x58, waiting for transfers between devices, seat_swap(): return lax.ppermute(values, 'seat', [(k, k ^ bits) for k in range(SEATS)])  99.6 us
    ppermute x58, starting transfers between devices, seat_swap(): return lax.ppermute(values, 'seat', [(k, k ^ bits) for k in range(SEATS)])  67.4 us
    ppermute x14, waiting for transfers between devices, plane_swap(): lax.ppermute(values, 'tensor', [(k, k ^ bits) for k in range(planes)])  59.4 us
    dot_general x12, matrix products, dot(): lax.dot_general(left, right, (((dims[0],), (dims[1],)), ((), ())), prefer...  52.2 us
    ppermute x14, starting transfers between devices, plane_swap(): lax.ppermute(values, 'tensor', [(k, k ^ bits) for k in range(planes)])  35.1 us
    unnamed x101, local copies, waits for them, and re-layouts  28.4 us
    pallas_call x1, Pallas kernels, attend_grad(): pl.pallas_call(kernel, out_shape=jax.ShapeDtypeStruct((planes * SLOT, seq...  17.1 us
    pallas_call x1, Pallas kernels, attend(): pl.pallas_call(kernel, out_shape=[jax.ShapeDtypeStruct((planes * HEAD_DIM...  12.5 us
  transfers between devices with their start and end apart: 79, of which 39 were waited for; matrix products, arithmetic and copies ran while one was open for 21% of the time, Pallas kernels for 8%

profile of v3, /device:TPU:0, one launch (start us, length us, event | category | flops | bytes accessed | tf_op | source)
XLA Modules:
  0.0 470.4 jit_solution(9870060674161228070)
XLA Ops:
  8.5 4.0 collective-permute-start.2
  13.8 4.1 concatenate.72
  43.4 13.3 %collective-permute-done.4 = bf16[64,1280]{1,0:T(8,128)(2,1)S(1)} collective-permute-done((bf16[64,1280]{1,0:T(8,128)(2,1)S(1)}, bf16[64,1280]{1,0:T(8,128)(2,1)S(1)}, u32[]{:S(2)}, u32[]{:S(2)}) %collective-permute-start.4) | collective-permute-done | bytes 163872 | tf_op jit(solution)/shard_map/ppermute | solution.py:44
  60.5 13.1 %collective-permute-done.9 = bf16[256,1280]{1,0:T(8,128)(2,1)} collective-permute-done((bf16[256,1280]{1,0:T(8,128)(2,1)S(1)}, bf16[256,1280]{1,0:T(8,128)(2,1)}, u32[]{:S(2)}, u32[]{:S(2)}) %collective-permute-start.9) | collective-permute-done | bytes 655392 | tf_op jit(solution)/shard_map/ppermute | solution.py:36
  98.5 5.5 %collective-permute-start.18 = (bf16[64,1280]{1,0:T(8,128)(2,1)S(1)}, bf16[64,1280]{1,0:T(8,128)(2,1)S(1)}, u32[]{:S(2)}, u32[]{:S(2)}) collective-permute-start(bf16[64,1280]{1,0:T(8,128)(2,1)S(1)} %get-tuple-element.222), channel_id=1, source_target_pairs={{0,3},{1,2},{2,1},{3,0},{4,7},{5,6},{6,5},{7,4},{8,11},{9,10},{10,... | collective-permute-start | bytes 491528 | tf_op jit(solution)/shard_map/ppermute | solution.py:44
  104.0 8.2 %collective-permute-start.17 = (bf16[64,1280]{1,0:T(8,128)(2,1)S(1)}, bf16[64,1280]{1,0:T(8,128)(2,1)S(1)}, u32[]{:S(2)}, u32[]{:S(2)}) collective-permute-start(bf16[64,1280]{1,0:T(8,128)(2,1)S(1)} %get-tuple-element.223), channel_id=1, source_target_pairs={{0,2},{1,3},{2,0},{3,1},{4,6},{5,7},{6,4},{7,5},{8,10},{9,11},{10,... | collective-permute-start | bytes 491528 | tf_op jit(solution)/shard_map/ppermute | solution.py:44
  112.7 6.0 %add_convert_fusion.2.qkv_ref = bf16[1024,1024]{1,0:T(8,128)(2,1)S(1)} fusion(f32[1024]{0:T(1024)S(1)} %bitcast.173, bf16[1280,1024]{1,0:T(8,128)(2,1)} %copy-done.15, bf16[1024,1280]{1,0:T(8,128)(2,1)} %copy-done.24, f32[1280]{0:T(1024)S(1)} %add.285, f32[1280]{0:T(1024)S(1)} %mul.161, f32[1024]{0:T(1024)S(1)} %add_rsqrt_fusion, ...), kind=kOutput, calls=%fused_computation.23 | convolution fusion | flops 2694316032 | bytes 7362560 | tf_op jit(solution)/shard_map/dot_general | solution.py:30
  118.6 18.5 %collective-permute-done.17 = bf16[64,1280]{1,0:T(8,128)(2,1)S(1)} collective-permute-done((bf16[64,1280]{1,0:T(8,128)(2,1)S(1)}, bf16[64,1280]{1,0:T(8,128)(2,1)S(1)}, u32[]{:S(2)}, u32[]{:S(2)}) %collective-permute-start.17) | collective-permute-done | bytes 163872 | tf_op jit(solution)/shard_map/ppermute | solution.py:44
  142.1 12.5 %attend.1 = (bf16[320,1024]{1,0:T(8,128)(2,1)S(1)}, f32[4,1,1024]{2,1,0:T(1,128)S(1)}) custom-call(s32[3]{0:T(128)S(1)} %pad_add_fusion.facts_ref, bf16[1024,1024]{1,0:T(8,128)(2,1)S(1)} %add_convert_fusion.2.qkv_ref), custom_call_target="tpu_custom_call" | custom-call | tf_op jit(solution)/shard_map/attend/pallas_call | solution.py:334
  158.4 8.6 %collective-permute-done.21 = bf16[128,1280]{1,0:T(8,128)(2,1)S(1)} collective-permute-done((bf16[128,1280]{1,0:T(8,128)(2,1)S(1)}, bf16[128,1280]{1,0:T(8,128)(2,1)S(1)}, u32[]{:S(2)}, u32[]{:S(2)}) %collective-permute-start.21) | collective-permute-done | bytes 327712 | tf_op jit(solution)/shard_map/ppermute | solution.py:36
  178.4 4.1 collective-permute-done.24
  182.5 5.0 %collective-permute-done.22 = bf16[256,1280]{1,0:T(8,128)(2,1)} collective-permute-done((bf16[256,1280]{1,0:T(8,128)(2,1)}, bf16[256,1280]{1,0:T(8,128)(2,1)}, u32[]{:S(2)}, u32[]{:S(2)}) %collective-permute-start.22) | collective-permute-done | bytes 655392 | tf_op jit(solution)/shard_map/ppermute | solution.py:36
  194.7 9.2 %collective-permute-done.30 = bf16[256,1280]{1,0:T(8,128)(2,1)S(1)} collective-permute-done((bf16[256,1280]{1,0:T(8,128)(2,1)S(1)}, bf16[256,1280]{1,0:T(8,128)(2,1)S(1)}, u32[]{:S(2)}, u32[]{:S(2)}) %collective-permute-start.30) | collective-permute-done | bytes 655392 | tf_op jit(solution)/shard_map/ppermute | solution.py:36
  207.9 3.1 collective-permute-done.32
  218.7 6.2 %multiply_convert_fusion = (bf16[1024,1280]{1,0:T(8,128)(2,1)S(1)}, f32[1024,1280]{1,0:T(8,128)S(1)}) fusion(f32[1280]{0:T(1024)S(1)} %reshape.218, bf16[1024,1280]{1,0:T(8,128)(2,1)} %constant_dynamic-update-slice_fusion.13, bf16[1280,1280]{1,0:T(8,128)(2,1)S(1)} %get-tuple-element.107), kind=kOutput, calls=%fused_computation.19 | convolution fusion | flops 3363307520 | bytes 13767680 | tf_op jit(solution)/shard_map/dot_general | solution.py:30
  224.9 5.6 %fusion.11 = bf16[1024,1280]{1,0:T(8,128)(2,1)S(1)} fusion(bf16[1024,1280]{1,0:T(8,128)(2,1)S(1)} %copy-done.34, bf16[1280,1280]{1,0:T(8,128)(2,1)S(1)} %get-tuple-element.106, f32[1024,1280]{1,0:T(8,128)S(1)} %get-tuple-element.253, f32[1280]{0:T(1024)S(1)} %reshape.218), kind=kOutput, calls=%fused_computation.17 | convolution fusion | flops 3369861120 | bytes 13767680 | tf_op jit(solution)/shard_map/dot_general | solution.py:30
  230.5 3.6 fusion.48
  236.3 5.4 %convolution_convert_fusion.1.refs_0_ = bf16[1280,1280]{1,0:T(8,128)(2,1)S(1)} fusion(bf16[1024,1280]{1,0:T(8,128)(2,1)} %constant_dynamic-update-slice_fusion.13, bf16[1024,1280]{1,0:T(8,128)(2,1)S(1)} %fusion.11), kind=kOutput, calls=%fused_computation.2 | convolution fusion | flops 3357081600 | bytes 8519680 | tf_op jit(solution)/shard_map/dot_general | solution.py:30
  245.3 3.9 convolution_convert_fusion.refs_1_
  249.2 3.7 pack_grads.2
  262.9 12.5 %collective-permute-done.38 = bf16[256,1280]{1,0:T(8,128)(2,1)} collective-permute-done((bf16[256,1280]{1,0:T(8,128)(2,1)}, bf16[256,1280]{1,0:T(8,128)(2,1)}, u32[]{:S(2)}, u32[]{:S(2)}) %collective-permute-start.38) | collective-permute-done | bytes 655392 | tf_op jit(solution)/shard_map/ppermute | solution.py:36
  286.2 4.6 add_convert_fusion
  290.7 6.3 %fusion.50 = f32[1024,1280]{1,0:T(8,128)S(1)} fusion(bf16[1024,1280]{1,0:T(8,128)(2,1)} %copy-done.38, bf16[1280,1280]{1,0:T(8,128)(2,1)} %copy-done.14), kind=kOutput, calls=%fused_computation.203 | convolution fusion | flops 3355443200 | bytes 11141120 | tf_op jit(solution)/shard_map/dot_general | solution.py:30
  308.0 17.1 %attend_grad.1 = bf16[1024,1024]{1,0:T(8,128)(2,1)S(1)} custom-call(s32[3]{0:T(128)S(1)} %pad_add_fusion.facts_ref, bf16[1024,1024]{1,0:T(8,128)(2,1)S(1)} %add_convert_fusion.2.qkv_ref, bf16[320,1024]{1,0:T(8,128)(2,1)S(1)} %convolution_convert_fusion.4.grad_ref, f32[4,1,1024]{2,1,0:T(1,128)S(1)} %get-tuple-element.115.log_ref), custom_call_target="tpu_custom_call" | custom-call | tf_op jit(solution)/shard_map/attend_grad/pallas_call | solution.py:381
  328.0 4.7 fusion.49
  346.5 4.1 convolution_convert_fusion.2.refs_0_
  352.1 3.4 collective-permute-done.48
  362.9 8.7 %collective-permute-done.64 = f32[2560]{0:T(1024)S(1)} collective-permute-done((f32[2560]{0:T(1024)S(1)}, f32[2560]{0:T(1024)S(1)}, u32[]{:S(2)}, u32[]{:S(2)}) %collective-permute-start.64) | collective-permute-done | bytes 10272 | tf_op jit(solution)/shard_map/ppermute | solution.py:36
  385.8 4.4 collective-permute-start.67
  408.8 8.2 %collective-permute-done.53 = bf16[64,1280]{1,0:T(8,128)(2,1)S(1)} collective-permute-done((bf16[64,1280]{1,0:T(8,128)(2,1)S(1)}, bf16[64,1280]{1,0:T(8,128)(2,1)S(1)}, u32[]{:S(2)}, u32[]{:S(2)}) %collective-permute-start.53) | collective-permute-done | bytes 163872 | tf_op jit(solution)/shard_map/ppermute | solution.py:44
  417.0 19.3 %collective-permute-done.52 = bf16[64,1280]{1,0:T(8,128)(2,1)S(1)} collective-permute-done((bf16[64,1280]{1,0:T(8,128)(2,1)S(1)}, bf16[64,1280]{1,0:T(8,128)(2,1)S(1)}, u32[]{:S(2)}, u32[]{:S(2)}) %collective-permute-start.52) | collective-permute-done | bytes 163872 | tf_op jit(solution)/shard_map/ppermute | solution.py:44
  442.9 3.1 collective-permute-done.55
  (382 shorter events, 213.5 us)
Async XLA Ops:
  7.2 84.2 %all-gather.5.cloned.1.call-start = ((), (), s32[]{:S(2)}) async-start(), calls=%async_computation.4 | async-start | bytes 4866048 | tf_op jit(solution)/shard_map/all_gather | solution.py:849
  8.5 15.5 %collective-permute-start.2 = (bf16[64,1280]{1,0:T(8,128)(2,1)S(1)}, bf16[64,1280]{1,0:T(8,128)(2,1)S(1)}, u32[]{:S(2)}, u32[]{:S(2)}) collective-permute-start(bf16[64,1280]{1,0:T(8,128)(2,1)S(1)} %get-tuple-element.233), channel_id=1, source_target_pairs={{0,24},{8,16},{16,8},{24,0},{1,25},{9,17},{17,9},{25,1},{2,26},{10... | collective-permute-start | bytes 491528 | tf_op jit(solution)/shard_map/ppermute | solution.py:36
  33.9 179.4 %all-gather.7.cloned.1.call-start = ((), (), s32[]{:S(2)}) async-start(), calls=%async_computation.5 | async-start | bytes 7372800 | tf_op jit(solution)/shard_map/all_gather | solution.py:860
  36.0 20.7 %collective-permute-start.4 = (bf16[64,1280]{1,0:T(8,128)(2,1)S(1)}, bf16[64,1280]{1,0:T(8,128)(2,1)S(1)}, u32[]{:S(2)}, u32[]{:S(2)}) collective-permute-start(bf16[64,1280]{1,0:T(8,128)(2,1)S(1)} %get-tuple-element.230), channel_id=1, source_target_pairs={{0,2},{1,3},{2,0},{3,1},{4,6},{5,7},{6,4},{7,5},{8,10},{9,11},{10,... | collective-permute-start | bytes 491528 | tf_op jit(solution)/shard_map/ppermute | solution.py:44
  38.6 18.1 %collective-permute-start.5 = (bf16[64,1280]{1,0:T(8,128)(2,1)S(1)}, bf16[64,1280]{1,0:T(8,128)(2,1)S(1)}, u32[]{:S(2)}, u32[]{:S(2)}) collective-permute-start(bf16[64,1280]{1,0:T(8,128)(2,1)S(1)} %get-tuple-element.229), channel_id=1, source_target_pairs={{0,3},{1,2},{2,1},{3,0},{4,7},{5,6},{6,5},{7,4},{8,11},{9,10},{10,... | collective-permute-start | bytes 491528 | tf_op jit(solution)/shard_map/ppermute | solution.py:44
  38.9 20.5 %collective-permute-start.29 = (bf16[160,640]{1,0:T(8,128)(2,1)S(1)}, bf16[160,640]{1,0:T(8,128)(2,1)S(1)}, u32[]{:S(2)}, u32[]{:S(2)}) collective-permute-start(bf16[160,640]{1,0:T(8,128)(2,1)S(1)} %get-tuple-element.105), channel_id=1, source_target_pairs={{0,24},{8,16},{16,8},{24,0},{1,25},{9,17},{17,9},{25,1},{2,26},{10... | collective-permute-start | bytes 614408 | tf_op jit(solution)/shard_map/ppermute | solution.py:36
  40.5 18.9 %collective-permute-start.28 = (bf16[160,640]{1,0:T(8,128)(2,1)S(1)}, bf16[160,640]{1,0:T(8,128)(2,1)S(1)}, u32[]{:S(2)}, u32[]{:S(2)}) collective-permute-start(bf16[160,640]{1,0:T(8,128)(2,1)S(1)} %get-tuple-element.104), channel_id=1, source_target_pairs={{0,16},{8,24},{16,0},{24,8},{1,17},{9,25},{17,1},{25,9},{2,18},{10... | collective-permute-start | bytes 614408 | tf_op jit(solution)/shard_map/ppermute | solution.py:36
  41.9 17.5 %collective-permute-start.27 = (bf16[160,640]{1,0:T(8,128)(2,1)S(1)}, bf16[160,640]{1,0:T(8,128)(2,1)S(1)}, u32[]{:S(2)}, u32[]{:S(2)}) collective-permute-start(bf16[160,640]{1,0:T(8,128)(2,1)S(1)} %get-tuple-element.103), channel_id=1, source_target_pairs={{0,8},{8,0},{16,24},{24,16},{1,9},{9,1},{17,25},{25,17},{2,10},{10... | collective-permute-start | bytes 614408 | tf_op jit(solution)/shard_map/ppermute | solution.py:36
  57.4 16.2 %collective-permute-start.9 = (bf16[256,1280]{1,0:T(8,128)(2,1)S(1)}, bf16[256,1280]{1,0:T(8,128)(2,1)}, u32[]{:S(2)}, u32[]{:S(2)}) collective-permute-start(bf16[256,1280]{1,0:T(8,128)(2,1)S(1)} %get-tuple-element.156), channel_id=1, source_target_pairs={{0,8},{8,0},{16,24},{24,16},{1,9},{9,1},{17,25},{25,17},{2,10},{10... | collective-permute-start | bytes 1966088 | tf_op jit(solution)/shard_map/ppermute | solution.py:36
  59.3 18.0 %collective-permute-start.10 = (bf16[256,1280]{1,0:T(8,128)(2,1)S(1)}, bf16[256,1280]{1,0:T(8,128)(2,1)}, u32[]{:S(2)}, u32[]{:S(2)}) collective-permute-start(bf16[256,1280]{1,0:T(8,128)(2,1)S(1)} %get-tuple-element.156), channel_id=1, source_target_pairs={{0,16},{8,24},{16,0},{24,8},{1,17},{9,25},{17,1},{25,9},{2,18},{10... | collective-permute-start | bytes 1966088 | tf_op jit(solution)/shard_map/ppermute | solution.py:36
  60.5 325.3 %reduce-scatter.3.cloned.1.call-start = ((), (), s32[]{:S(2)}) async-start(), calls=%async_computation.2 | async-start | bytes 4096000 | tf_op jit(solution)/shard_map/reduce_scatter | solution.py:932
  74.6 15.2 %collective-permute-start.11 = (bf16[128,1280]{1,0:T(8,128)(2,1)S(1)}, bf16[128,1280]{1,0:T(8,128)(2,1)S(1)}, u32[]{:S(2)}, u32[]{:S(2)}) collective-permute-start(bf16[128,1280]{1,0:T(8,128)(2,1)S(1)} %slice.324), channel_id=1, source_target_pairs={{0,16},{8,24},{16,0},{24,8},{1,17},{9,25},{17,1},{25,9},{2,18},{10... | collective-permute-start | bytes 983048 | tf_op jit(solution)/shard_map/ppermute | solution.py:36
  98.5 20.1 %collective-permute-start.18 = (bf16[64,1280]{1,0:T(8,128)(2,1)S(1)}, bf16[64,1280]{1,0:T(8,128)(2,1)S(1)}, u32[]{:S(2)}, u32[]{:S(2)}) collective-permute-start(bf16[64,1280]{1,0:T(8,128)(2,1)S(1)} %get-tuple-element.222), channel_id=1, source_target_pairs={{0,3},{1,2},{2,1},{3,0},{4,7},{5,6},{6,5},{7,4},{8,11},{9,10},{10,... | collective-permute-start | bytes 491528 | tf_op jit(solution)/shard_map/ppermute | solution.py:44
  104.0 33.1 %collective-permute-start.17 = (bf16[64,1280]{1,0:T(8,128)(2,1)S(1)}, bf16[64,1280]{1,0:T(8,128)(2,1)S(1)}, u32[]{:S(2)}, u32[]{:S(2)}) collective-permute-start(bf16[64,1280]{1,0:T(8,128)(2,1)S(1)} %get-tuple-element.223), channel_id=1, source_target_pairs={{0,2},{1,3},{2,0},{3,1},{4,6},{5,7},{6,4},{7,5},{8,10},{9,11},{10,... | collective-permute-start | bytes 491528 | tf_op jit(solution)/shard_map/ppermute | solution.py:44
  112.2 25.0 %collective-permute-start.16 = (bf16[64,1280]{1,0:T(8,128)(2,1)S(1)}, bf16[64,1280]{1,0:T(8,128)(2,1)S(1)}, u32[]{:S(2)}, u32[]{:S(2)}) collective-permute-start(bf16[64,1280]{1,0:T(8,128)(2,1)S(1)} %get-tuple-element.224), channel_id=1, source_target_pairs={{0,1},{1,0},{2,3},{3,2},{4,5},{5,4},{6,7},{7,6},{8,9},{9,8},{10,11... | collective-permute-start | bytes 491528 | tf_op jit(solution)/shard_map/ppermute | solution.py:44
  138.1 16.5 %collective-permute-start.19 = (bf16[256,1280]{1,0:T(8,128)(2,1)}, bf16[256,1280]{1,0:T(8,128)(2,1)}, u32[]{:S(2)}, u32[]{:S(2)}) collective-permute-start(bf16[256,1280]{1,0:T(8,128)(2,1)} %pad_maximum_fusion.4), channel_id=1, source_target_pairs={{0,8},{8,0},{16,24},{24,16},{1,9},{9,1},{17,25},{25,17},{2,10},{10... | collective-permute-start | bytes 1966088 | tf_op jit(solution)/shard_map/ppermute | solution.py:36
  138.7 15.9 %collective-permute-start.20 = (bf16[256,1280]{1,0:T(8,128)(2,1)}, bf16[256,1280]{1,0:T(8,128)(2,1)}, u32[]{:S(2)}, u32[]{:S(2)}) collective-permute-start(bf16[256,1280]{1,0:T(8,128)(2,1)} %pad_maximum_fusion.4), channel_id=1, source_target_pairs={{0,16},{8,24},{16,0},{24,8},{1,17},{9,25},{17,1},{25,9},{2,18},{10... | collective-permute-start | bytes 1966088 | tf_op jit(solution)/shard_map/ppermute | solution.py:36
  168.6 13.9 %collective-permute-start.24 = (bf16[256,1280]{1,0:T(8,128)(2,1)}, bf16[256,1280]{1,0:T(8,128)(2,1)}, u32[]{:S(2)}, u32[]{:S(2)}) collective-permute-start(bf16[256,1280]{1,0:T(8,128)(2,1)} %pad_maximum_fusion.6), channel_id=1, source_target_pairs={{0,16},{8,24},{16,0},{24,8},{1,17},{9,25},{17,1},{25,9},{2,18},{10... | collective-permute-start | bytes 1966088 | tf_op jit(solution)/shard_map/ppermute | solution.py:36
  170.9 16.6 %collective-permute-start.22 = (bf16[256,1280]{1,0:T(8,128)(2,1)}, bf16[256,1280]{1,0:T(8,128)(2,1)}, u32[]{:S(2)}, u32[]{:S(2)}) collective-permute-start(bf16[256,1280]{1,0:T(8,128)(2,1)} %pad_maximum_fusion.5), channel_id=1, source_target_pairs={{0,8},{8,0},{16,24},{24,16},{1,9},{9,1},{17,25},{25,17},{2,10},{10... | collective-permute-start | bytes 1966088 | tf_op jit(solution)/shard_map/ppermute | solution.py:36
  173.0 21.6 %collective-permute-start.25 = (bf16[128,1280]{1,0:T(8,128)(2,1)S(1)}, bf16[128,1280]{1,0:T(8,128)(2,1)S(1)}, u32[]{:S(2)}, u32[]{:S(2)}) collective-permute-start(bf16[128,1280]{1,0:T(8,128)(2,1)S(1)} %slice.271), channel_id=1, source_target_pairs={{0,16},{8,24},{16,0},{24,8},{1,17},{9,25},{17,1},{25,9},{2,18},{10... | collective-permute-start | bytes 983048 | tf_op jit(solution)/shard_map/ppermute | solution.py:36
  175.5 19.2 %collective-permute-start.26 = (bf16[128,1280]{1,0:T(8,128)(2,1)S(1)}, bf16[128,1280]{1,0:T(8,128)(2,1)S(1)}, u32[]{:S(2)}, u32[]{:S(2)}) collective-permute-start(bf16[128,1280]{1,0:T(8,128)(2,1)S(1)} %slice.272), channel_id=1, source_target_pairs={{0,8},{8,0},{16,24},{24,16},{1,9},{9,1},{17,25},{25,17},{2,10},{10... | collective-permute-start | bytes 983048 | tf_op jit(solution)/shard_map/ppermute | solution.py:36
  253.0 33.2 %collective-permute-start.42 = (bf16[4,4,160,640]{3,2,1,0:T(8,128)(2,1)}, bf16[4,4,160,640]{3,2,1,0:T(8,128)(2,1)}, u32[]{:S(2)}, u32[]{:S(2)}) collective-permute-start(bf16[4,4,160,640]{3,2,1,0:T(8,128)(2,1)} %get-tuple-element.110), channel_id=1, source_target_pairs={{0,4},{4,0},{1,5},{5,1},{2,6},{6,2},{3,7},{7,3},{8,12},{12,8},{9,1... | collective-permute-start | bytes 9830408 | tf_op jit(solution)/shard_map/ppermute | solution.py:40
  259.9 15.5 %collective-permute-start.38 = (bf16[256,1280]{1,0:T(8,128)(2,1)}, bf16[256,1280]{1,0:T(8,128)(2,1)}, u32[]{:S(2)}, u32[]{:S(2)}) collective-permute-start(bf16[256,1280]{1,0:T(8,128)(2,1)} %get-tuple-element.160), channel_id=1, source_target_pairs={{0,8},{8,0},{16,24},{24,16},{1,9},{9,1},{17,25},{25,17},{2,10},{10... | collective-permute-start | bytes 1966088 | tf_op jit(solution)/shard_map/ppermute | solution.py:36
  260.8 16.5 %collective-permute-start.39 = (bf16[256,1280]{1,0:T(8,128)(2,1)}, bf16[256,1280]{1,0:T(8,128)(2,1)}, u32[]{:S(2)}, u32[]{:S(2)}) collective-permute-start(bf16[256,1280]{1,0:T(8,128)(2,1)} %get-tuple-element.160), channel_id=1, source_target_pairs={{0,16},{8,24},{16,0},{24,8},{1,17},{9,25},{17,1},{25,9},{2,18},{10... | collective-permute-start | bytes 1966088 | tf_op jit(solution)/shard_map/ppermute | solution.py:36
  301.2 148.7 %reduce-scatter.5.cloned.1.call-start = ((), (), s32[]{:S(2)}) async-start(), calls=%async_computation.3 | async-start | bytes 2703360 | tf_op jit(solution)/shard_map/reduce_scatter | solution.py:966
  302.7 22.3 %collective-permute-start.44 = (bf16[128,1280]{1,0:T(8,128)(2,1)S(1)}, bf16[128,1280]{1,0:T(8,128)(2,1)S(1)}, u32[]{:S(2)}, u32[]{:S(2)}) collective-permute-start(bf16[128,1280]{1,0:T(8,128)(2,1)S(1)} %get-tuple-element.179), channel_id=1, source_target_pairs={{0,8},{8,0},{16,24},{24,16},{1,9},{9,1},{17,25},{25,17},{2,10},{10... | collective-permute-start | bytes 983048 | tf_op jit(solution)/shard_map/ppermute | solution.py:36
  304.0 21.0 %collective-permute-start.43 = (bf16[128,1280]{1,0:T(8,128)(2,1)S(1)}, bf16[128,1280]{1,0:T(8,128)(2,1)S(1)}, u32[]{:S(2)}, u32[]{:S(2)}) collective-permute-start(bf16[128,1280]{1,0:T(8,128)(2,1)S(1)} %get-tuple-element.181), channel_id=1, source_target_pairs={{0,16},{8,24},{16,0},{24,8},{1,17},{9,25},{17,1},{25,9},{2,18},{10... | collective-permute-start | bytes 983048 | tf_op jit(solution)/shard_map/ppermute | solution.py:36
  352.0 29.9 %collective-permute-start.68 = (bf16[4,4,176,320]{3,2,1,0:T(8,128)(2,1)S(1)}, bf16[4,4,176,320]{3,2,1,0:T(8,128)(2,1)S(1)}, u32[]{:S(2)}, u32[]{:S(2)}) collective-permute-start(bf16[4,4,176,320]{3,2,1,0:T(8,128)(2,1)S(1)} %get-tuple-element.124), channel_id=1, source_target_pairs={{0,4},{4,0},{1,5},{5,1},{2,6},{6,2},{3,7},{7,3},{8,12},{12,8},{9,1... | collective-permute-start | bytes 5406728 | tf_op jit(solution)/shard_map/ppermute | solution.py:40
  357.9 45.0 %collective-permute-start.50 = (bf16[256,1280]{1,0:T(8,128)(2,1)}, bf16[256,1280]{1,0:T(8,128)(2,1)S(1)}, u32[]{:S(2)}, u32[]{:S(2)}) collective-permute-start(bf16[256,1280]{1,0:T(8,128)(2,1)} %pad_maximum_fusion.10), channel_id=1, source_target_pairs={{0,16},{8,24},{16,0},{24,8},{1,17},{9,25},{17,1},{25,9},{2,18},{10... | collective-permute-start | bytes 1966088 | tf_op jit(solution)/shard_map/ppermute | solution.py:36
  359.0 43.9 %collective-permute-start.49 = (bf16[256,1280]{1,0:T(8,128)(2,1)}, bf16[256,1280]{1,0:T(8,128)(2,1)}, u32[]{:S(2)}, u32[]{:S(2)}) collective-permute-start(bf16[256,1280]{1,0:T(8,128)(2,1)} %pad_maximum_fusion.9), channel_id=1, source_target_pairs={{0,8},{8,0},{16,24},{24,16},{1,9},{9,1},{17,25},{25,17},{2,10},{10... | collective-permute-start | bytes 1966088 | tf_op jit(solution)/shard_map/ppermute | solution.py:36
  407.0 29.3 %collective-permute-start.52 = (bf16[64,1280]{1,0:T(8,128)(2,1)S(1)}, bf16[64,1280]{1,0:T(8,128)(2,1)S(1)}, u32[]{:S(2)}, u32[]{:S(2)}) collective-permute-start(bf16[64,1280]{1,0:T(8,128)(2,1)S(1)} %get-tuple-element.218), channel_id=1, source_target_pairs={{0,2},{1,3},{2,0},{3,1},{4,6},{5,7},{6,4},{7,5},{8,10},{9,11},{10,... | collective-permute-start | bytes 491528 | tf_op jit(solution)/shard_map/ppermute | solution.py:44
  407.0 29.3 %collective-permute-start.51 = (bf16[64,1280]{1,0:T(8,128)(2,1)S(1)}, bf16[64,1280]{1,0:T(8,128)(2,1)S(1)}, u32[]{:S(2)}, u32[]{:S(2)}) collective-permute-start(bf16[64,1280]{1,0:T(8,128)(2,1)S(1)} %get-tuple-element.219), channel_id=1, source_target_pairs={{0,1},{1,0},{2,3},{3,2},{4,5},{5,4},{6,7},{7,6},{8,9},{9,8},{10,11... | collective-permute-start | bytes 491528 | tf_op jit(solution)/shard_map/ppermute | solution.py:44
  (89 other events, 773.2 us)
Sparse Core Ops, SparseCore 0:
  34.1 54.5 all-gather.4
  90.8 78.0 all-gather.6
  301.3 62.9 reduce-scatter.2
  385.9 53.0 reduce-scatter.4

commit v4 on v3

--- a/solution.py
+++ b/solution.py
@@ -21,6 +21,7 @@
 SEATS = 4
 SLOT = 256
 EXTRA = 16
+FOLD = 2
 MEGA = 1 << 20
 LOG2E = 1.4426950408889634
 CORES = ((0, 1), (1, 0))
@@ -52,8 +53,7 @@
     return lax.optimization_barrier((value, others))[0]
 
 
-def leave_seat(rows, seat):
-    parts = rows.reshape(SEATS, -1, rows.shape[1])
+def leave_seat(parts, seat):
     return jnp.stack(
         [at_index(parts, seat)] + [seat_swap(at_index(parts, seat ^ r), r) for r in range(1, SEATS)]
     )
@@ -61,20 +61,22 @@
 
 def leave_plane(got, seat, plane, planes):
     turn = seat ^ plane
-    return jnp.concatenate(
+    return jnp.stack(
         [at_index(got, turn)]
         + [plane_swap(at_index(got, turn ^ k), k, planes) for k in range(1, planes)]
     )
 
 
-def from_plane(rows, seat, plane, planes):
-    parts = rows.reshape(planes, -1, rows.shape[1])
-    got = jnp.stack([parts[0]] + [plane_swap(parts[k], k, planes) for k in range(1, planes)])
+def enter_plane(parts, planes):
+    return jnp.stack([parts[0]] + [plane_swap(parts[k], k, planes) for k in range(1, planes)])
+
+
+def enter_seat(got, seat, plane):
     turn = seat ^ plane
     back = jnp.stack(
         [at_index(got, turn)] + [seat_swap(at_index(got, turn ^ r), r) for r in range(1, SEATS)]
     )
-    return jnp.concatenate([at_index(back, s ^ seat) for s in range(SEATS)])
+    return jnp.stack([at_index(back, s ^ seat) for s in range(SEATS)])
 
 
 def gather_near(own):
@@ -83,12 +85,7 @@
 
 def gather_far(own, across, along):
     half = own.shape[0] // 2
-    far_a, far_b = seat_swap(across[:half], 2), seat_swap(along[half:], 1)
-    return jnp.concatenate([own, across, along, far_a, far_b])
-
-
-def plane_gather(own):
-    return gather_far(*gather_near(own))
+    return own, across, along, seat_swap(across[:half], 2), seat_swap(along[half:], 1)
 
 
 def scatter_far(terms):
@@ -119,6 +116,7 @@
 def pack_heads(sources, vectors, shifts, lengths, seat):
     rows = sources[0].shape[0]
     columns = len(sources) * HEAD_DIM
+    short, few = rows // FOLD, EXTRA // FOLD
     query_shift, value_shift, up_shift = shifts
     hidden_of = up_shift.shape[1] // SEATS
 
@@ -133,17 +131,24 @@
         for j in range(SEATS):
             of = slice(j * HEAD_DIM, (j + 1) * HEAD_DIM)
             for k in range(len(sources)):
-                held[j, :rows, k * HEAD_DIM : (k + 1) * HEAD_DIM] = inputs[k][:, of]
+                for f in range(FOLD):
+                    at = f * columns + k * HEAD_DIM
+                    held[j, :short, at : at + HEAD_DIM] = inputs[k][
+                        f * short : (f + 1) * short, of
+                    ]
             tile[8:9, :HEAD_DIM] = query_ref[:, of].astype(jnp.float32)
             tile[8:9, 2 * HEAD_DIM : 3 * HEAD_DIM] = value_ref[:, of].astype(jnp.float32)
             tile[9:10, :hidden_of] = up_ref[:, j * hidden_of : (j + 1) * hidden_of].astype(
                 jnp.float32
             )
-            held[j, rows:, :] = tile[...].astype(jnp.bfloat16)
+            for f in range(FOLD):
+                held[j, short:, f * columns : (f + 1) * columns] = tile[
+                    f * few : (f + 1) * few, :
+                ].astype(jnp.bfloat16)
         for r in range(SEATS):
             outs[r][...] = held[seat_ref[0] ^ r]
 
-    piece = jax.ShapeDtypeStruct((rows + EXTRA, columns), jnp.bfloat16)
+    piece = jax.ShapeDtypeStruct((short + few, FOLD * columns), jnp.bfloat16)
     arrays = [*sources, vectors, *shifts]
     return pl.pallas_call(
         kernel,
@@ -152,10 +157,10 @@
         in_specs=[smem(), smem()] + [whole(a) for a in arrays],
         out_specs=[whole(piece)] * SEATS,
         scratch_shapes=[
-            pltpu.VMEM((SEATS, rows + EXTRA, columns), jnp.bfloat16),
+            pltpu.VMEM((SEATS, short + few, FOLD * columns), jnp.bfloat16),
             pltpu.VMEM((EXTRA, columns), jnp.float32),
         ],
-        compiler_params=pltpu.CompilerParams(vmem_limit_bytes=16 * MEGA),
+        compiler_params=pltpu.CompilerParams(vmem_limit_bytes=4 * MEGA),
         name="pack_heads",
     )(seat, lengths, *arrays)
 
@@ -180,14 +185,16 @@
         in_specs=[smem()] + [whole(a) for a in sources],
         out_specs=[whole(piece)] * SEATS,
         scratch_shapes=[pltpu.VMEM((SEATS, rows, columns), jnp.bfloat16)],
-        compiler_params=pltpu.CompilerParams(vmem_limit_bytes=16 * MEGA),
+        compiler_params=pltpu.CompilerParams(vmem_limit_bytes=6 * MEGA),
         name="pack_hidden",
     )(seat, *sources)
 
 
-def assemble_weights(plan, gathered, seat, planes, extra):
+def assemble_weights(plan, gathered, seat, planes, extra, fold):
     groups, _, tall, columns = gathered.shape
-    rows = tall - extra
+    columns, few = columns // fold, extra // fold
+    short = tall - few
+    rows = short * fold
 
     def kernel(seat_ref, in_ref, *outs):
         del seat_ref
@@ -196,15 +203,20 @@
             for z in range(planes):
                 for k, (lane, size, stride) in enumerate(plan):
                     at = z * stride
-                    outs[k][of, at : at + size] = in_ref[
-                        c * planes + z, 0, :rows, lane : lane + size
-                    ]
+                    for f in range(fold):
+                        start = f * columns + lane
+                        outs[k][c * rows + f * short : c * rows + (f + 1) * short, at : at + size] = (
+                            in_ref[c * planes + z, 0, :short, start : start + size]
+                        )
                     if size < stride:
                         outs[k][of, at + size : at + stride] = jnp.zeros(
                             (rows, stride - size), jnp.bfloat16
                         )
         if extra:
-            outs[-1][0] = in_ref[:, 0, rows:, :]
+            for f in range(fold):
+                outs[-1][0, :, f * few : (f + 1) * few, :] = in_ref[
+                    :, 0, short:, f * columns : (f + 1) * columns
+                ].astype(jnp.float32)
 
     shapes = [
         jax.ShapeDtypeStruct((SEATS * 2 * rows, planes * stride), jnp.bfloat16)
@@ -212,7 +224,7 @@
     ]
     blocks = [pl.BlockSpec((2 * rows, planes * stride), lambda s, seat: (s, 0)) for _, _, stride in plan]
     if extra:
-        shapes += [jax.ShapeDtypeStruct((SEATS, groups, extra, columns), jnp.bfloat16)]
+        shapes += [jax.ShapeDtypeStruct((SEATS, groups, extra, columns), jnp.float32)]
         blocks += [pl.BlockSpec((1, groups, extra, columns), lambda s, seat: (s, 0, 0, 0))]
     return pl.pallas_call(
         kernel,
@@ -221,35 +233,41 @@
             num_scalar_prefetch=1,
             grid=(SEATS,),
             in_specs=[
-                pl.BlockSpec((groups, 1, tall, columns), lambda s, seat: (0, s ^ seat[0], 0, 0))
+                pl.BlockSpec((groups, 1, tall, fold * columns), lambda s, seat: (0, s ^ seat[0], 0, 0))
             ],
             out_specs=blocks,
         ),
-        compiler_params=pltpu.CompilerParams(vmem_limit_bytes=24 * MEGA),
+        compiler_params=pltpu.CompilerParams(vmem_limit_bytes=12 * MEGA),
         name="assemble_weights",
     )(seat, gathered)
 
 
-def pack_grads(plan, columns, sources, core, planes, vectors=None, shifts=None):
+def pack_grads(plan, columns, sources, core, planes, fold=1, vectors=None, shifts=None):
     rows = sources[0].shape[0] // (2 * SEATS)
     extra = 0 if vectors is None else EXTRA
-    tall = rows + extra
+    short, few = rows // fold, extra // fold
+    tall = short + few
 
     def kernel(core_ref, *refs):
         inputs = refs[: len(sources)]
         for out, c in ((refs[-2], core_ref[0]), (refs[-1], 1 - core_ref[0])):
-            start = pl.multiple_of(c * rows, 16)
             for z in range(planes):
-                for k, stride, lane, size in plan:
-                    out[z, 0, :rows, lane : lane + size] = inputs[k][
-                        pl.ds(start, rows), z * stride : z * stride + size
-                    ]
-                if extra:
-                    vec_ref, shift_ref = refs[len(sources) : len(sources) + 2]
-                    out[z, 0, rows:, :] = (vec_ref[0, c] + shift_ref[z]).astype(jnp.bfloat16)
-
-    chunk = jax.ShapeDtypeStruct((planes, SEATS, tall, columns), jnp.bfloat16)
-    block = pl.BlockSpec((planes, 1, tall, columns), lambda s: (0, s, 0, 0))
+                for f in range(fold):
+                    start = pl.multiple_of(c * rows + f * short, 16)
+                    for k, stride, lane, size in plan:
+                        at = f * columns + lane
+                        out[z, 0, :short, at : at + size] = inputs[k][
+                            pl.ds(start, short), z * stride : z * stride + size
+                        ]
+                    if extra:
+                        vec_ref, shift_ref = refs[len(sources) : len(sources) + 2]
+                        of = slice(f * few, (f + 1) * few)
+                        out[z, 0, short:, f * columns : (f + 1) * columns] = (
+                            vec_ref[0, c, of, :] + shift_ref[z, of, :]
+                        ).astype(jnp.bfloat16)
+
+    chunk = jax.ShapeDtypeStruct((planes, SEATS, tall, fold * columns), jnp.bfloat16)
+    block = pl.BlockSpec((planes, 1, tall, fold * columns), lambda s: (0, s, 0, 0))
     in_specs = [pl.BlockSpec((2 * rows, a.shape[1]), lambda s: (s, 0)) for a in sources]
     more = []
     if extra:
@@ -264,14 +282,16 @@
         grid=(SEATS,),
         in_specs=[smem()] + in_specs,
         out_specs=[block, block],
-        compiler_params=pltpu.CompilerParams(vmem_limit_bytes=32 * MEGA),
+        compiler_params=pltpu.CompilerParams(vmem_limit_bytes=12 * MEGA),
         name="pack_grads",
     )(core, *sources, *more)
 
 
-def finish_grads(plan, pieces, seat, extra):
+def finish_grads(plan, pieces, seat, extra, fold):
     tall, columns = pieces[0].shape
-    rows = tall - extra
+    columns, few = columns // fold, extra // fold
+    short = tall - few
+    rows = short * fold
 
     def kernel(seat_ref, *refs):
         outs, held = refs[SEATS:-1], refs[-1]
@@ -279,11 +299,15 @@
             held[seat_ref[0] ^ r] = refs[r][...]
         for j in range(SEATS):
             for k, (lane, size) in enumerate(plan):
-                outs[k][:, j * size : (j + 1) * size] = held[j, :rows, lane : lane + size].astype(
-                    jnp.float32
-                )
-            if extra:
-                outs[-1][j] = held[j, rows:, :].astype(jnp.float32)
+                for f in range(fold):
+                    at = f * columns + lane
+                    outs[k][f * short : (f + 1) * short, j * size : (j + 1) * size] = held[
+                        j, :short, at : at + size
+                    ].astype(jnp.float32)
+            for f in range(fold if extra else 0):
+                outs[-1][j, f * few : (f + 1) * few, :] = held[
+                    j, short:, f * columns : (f + 1) * columns
+                ].astype(jnp.float32)
 
     shapes = [jax.ShapeDtypeStruct((rows, SEATS * size), jnp.float32) for _, size in plan]
     if extra:
@@ -294,8 +318,8 @@
         grid=(1,),
         in_specs=[smem()] + [whole(p) for p in pieces],
         out_specs=[whole(s) for s in shapes],
-        scratch_shapes=[pltpu.VMEM((SEATS, tall, columns), jnp.bfloat16)],
-        compiler_params=pltpu.CompilerParams(vmem_limit_bytes=24 * MEGA),
+        scratch_shapes=[pltpu.VMEM((SEATS, tall, fold * columns), jnp.bfloat16)],
+        compiler_params=pltpu.CompilerParams(vmem_limit_bytes=8 * MEGA),
         name="finish_grads",
     )(seat, *pieces)
 
@@ -340,16 +364,18 @@
         out_specs=[pl.BlockSpec((HEAD_DIM, seq), lambda h: (h, 0))]
         + [pl.BlockSpec((1, 1, seq), lambda h: (h, 0, 0))],
         scratch_shapes=[pltpu.VMEM((seq, quarter), jnp.float32)],
-        compiler_params=pltpu.CompilerParams(vmem_limit_bytes=40 * MEGA),
+        compiler_params=pltpu.CompilerParams(vmem_limit_bytes=24 * MEGA),
         name="attend",
     )(facts, qkv)
 
 
-def attend_grad(facts, qkv, context_grad, logs, planes, quarter):
+def attend_grad(facts, qkv, context_grad, logs, planes, quarter, first, heads, begun=None):
     seq = qkv.shape[1]
     scale = HEAD_DIM ** (-0.5)
 
-    def kernel(facts_ref, qkv_ref, grad_ref, log_ref, out_ref, shift_ref, key_acc, value_acc):
+    def kernel(facts_ref, qkv_ref, grad_ref, log_ref, *refs):
+        out_ref, shift_ref, key_acc, value_acc = refs[-4:]
+
         @pl.when(pl.program_id(0) == 0)
         def _():
             shift_ref[...] = key_shift(facts_ref, shift_ref.shape, planes, quarter)
@@ -378,25 +404,29 @@
         out_ref[2 * HEAD_DIM : 3 * HEAD_DIM, :] = value_acc[...].astype(jnp.bfloat16)
         out_ref[3 * HEAD_DIM :, :] = jnp.zeros((SLOT - 3 * HEAD_DIM, seq), jnp.bfloat16)
 
+    more = [] if begun is None else [begun]
+    more_specs = [pl.BlockSpec(memory_space=pl.ANY) for _ in more]
     return pl.pallas_call(
         kernel,
         out_shape=jax.ShapeDtypeStruct((planes * SLOT, seq), jnp.bfloat16),
-        grid=(planes,),
+        grid=(heads,),
         in_specs=[
             smem(),
-            pl.BlockSpec((SLOT, seq), lambda h: (h, 0)),
-            pl.BlockSpec((HEAD_DIM, seq), lambda h: (h, 0)),
-            pl.BlockSpec((1, 1, seq), lambda h: (h, 0, 0)),
+            pl.BlockSpec((SLOT, seq), lambda h: (first + h, 0)),
+            pl.BlockSpec((HEAD_DIM, seq), lambda h: (first + h, 0)),
+            pl.BlockSpec((1, 1, seq), lambda h: (first + h, 0, 0)),
+            *more_specs,
         ],
-        out_specs=pl.BlockSpec((SLOT, seq), lambda h: (h, 0)),
+        out_specs=pl.BlockSpec((SLOT, seq), lambda h: (first + h, 0)),
         scratch_shapes=[
             pltpu.VMEM((seq, quarter), jnp.float32),
             pltpu.VMEM((HEAD_DIM, seq), jnp.float32),
             pltpu.VMEM((HEAD_DIM, seq), jnp.float32),
         ],
-        compiler_params=pltpu.CompilerParams(vmem_limit_bytes=48 * MEGA),
+        compiler_params=pltpu.CompilerParams(vmem_limit_bytes=32 * MEGA),
         name="attend_grad",
-    )(facts, qkv, context_grad, logs)
+        input_output_aliases={4: 0} if more else {},
+    )(facts, qkv, context_grad, logs, *more)
 
 
 def norm_back(values, gain, grad):
@@ -842,25 +872,29 @@
         lengths,
         seat_word,
     )
-    tokens_got = leave_seat(tokens[0], seat)
+    def split(rows):
+        return rows.reshape(SEATS, -1, width)
+
+    tokens_got = leave_seat(split(tokens[0]), seat)
+    sub = tokens_got.shape[1]
     head_pieces = after(head_pieces, tokens_got)
     head_pieces = [head_pieces[0]] + [seat_swap(head_pieces[r], r) for r in range(1, SEATS)]
-    head_pieces = jnp.stack(head_pieces)
+    rows_low = leave_plane(tokens_got, seat, plane, planes).reshape(quarter, width)
+    head_pieces, rows_low = lax.optimization_barrier((jnp.stack(head_pieces), rows_low))
     heads_around = lax.all_gather(head_pieces, group, axis=0)
-
-    rows_low = leave_plane(tokens_got, seat, plane, planes)
     tokens_near = gather_near(rows_low)
-    tokens_all = gather_far(*tokens_near)
+    ff_pieces = pack_hidden([up_weight, down_weight], seat_word)
+    ff_pieces, tokens_near, cot_in = lax.optimization_barrier(
+        (ff_pieces, tokens_near, split(cotangent[0]))
+    )
+    tokens_all = jnp.concatenate(gather_far(*tokens_near))
     seq = tokens_all.shape[0]
-
-    ff_pieces = pack_hidden([up_weight, down_weight], seat_word)
-    ff_pieces = after(ff_pieces, head_pieces)
     ff_pieces = [ff_pieces[0]] + [seat_swap(ff_pieces[r], r) for r in range(1, SEATS)]
-    ff_pieces = jnp.stack(ff_pieces)
-    ff_around = lax.all_gather(ff_pieces, group, axis=0)
-
-    cot_got = leave_seat(after(cotangent[0], tokens_near), seat)
-    cot_low = leave_plane(after(cot_got, tokens_all, heads_around), seat, plane, planes)
+    cot_got = leave_seat(cot_in, seat)
+    cot_got, heads_around, tokens_all = lax.optimization_barrier(
+        (cot_got, heads_around, tokens_all)
+    )
+    cot_low = leave_plane(cot_got, seat, plane, planes).reshape(quarter, width)
 
     qkv_full, out_part, extra = assemble_weights(
         [(0, 3 * HEAD_DIM, SLOT), (3 * HEAD_DIM, HEAD_DIM, HEAD_DIM)],
@@ -868,6 +902,7 @@
         seat_word,
         planes,
         EXTRA,
+        FOLD,
     )
     vectors = extra[:, ::planes, :6, :rows_of].astype(full)
     gain_one, bias_one, out_shift, gain_two, bias_two, down_shift = (
@@ -884,23 +919,29 @@
     rows = rows_low.astype(full)
     normed_all = layer_norm(tokens_all.astype(full), gain_one, bias_one).astype(low)
     qkv = (dot(qkv_full, normed_all, (0, 1)) + qkv_shift).astype(low)
-    qkv, cot_low = lax.optimization_barrier((qkv, cot_low))
+    qkv, cot_low, ff_pieces = lax.optimization_barrier((qkv, cot_low, jnp.stack(ff_pieces)))
+    ff_around = lax.all_gather(ff_pieces, group, axis=0)
     cot_near = gather_near(cot_low)
     context, logs = attend(facts, qkv, planes, quarter)
     context, cot_near = lax.optimization_barrier((context, cot_near))
-    cot_all = gather_far(*cot_near)
+    cot_all = jnp.concatenate(gather_far(*cot_near))
     attended = scatter_near(*scatter_far(dot(context, out_part, (0, 1))))
     middle = rows + attended + out_shift
     normed_two = layer_norm(middle, gain_two, bias_two).astype(low)
-    normed_two_all = plane_gather(normed_two)
+    normed_two_near = gather_near(normed_two)
     up_full, down_full = assemble_weights(
         [(0, hidden_of, hidden_of), (hidden_of, hidden_of, hidden_of)],
         ff_around,
         seat_word,
         planes,
         0,
+        1,
     )
     hidden_grad = dot(cot_all, down_full, (1, 0))
+    normed_two_near, hidden_grad, up_full = lax.optimization_barrier(
+        (normed_two_near, hidden_grad, up_full)
+    )
+    normed_two_all = jnp.concatenate(gather_far(*normed_two_near))
     hidden_pre = dot(normed_two_all, up_full, (1, 0)) + up_shift
     normal = 0.5 * (1.0 + lax.erf(hidden_pre * (0.5**0.5)))
     slope = normal + hidden_pre * (jnp.exp(-0.5 * hidden_pre * hidden_pre) * (0.5 / jnp.pi) ** 0.5)
@@ -923,27 +964,42 @@
         core_word,
         planes,
     )
-    normed_two_grad = after(scatter_near(own, across, along), ff_given)
+    ff_both = over_cores(ff_kept, ff_given)
+    normed_two_grad, ff_both = lax.optimization_barrier(
+        (scatter_near(own, across, along), ff_both)
+    )
+    ff_owned = lax.psum_scatter(ff_both, "tensor", scatter_dimension=0, tiled=False)
     middle_part, gain_two_grad, bias_two_grad = norm_back(middle, gain_two, normed_two_grad)
     middle_grad = grad_out + middle_part
     middle_low = middle_grad.astype(low)
-    middle_all = plane_gather(middle_low)
-    ff_both = over_cores(ff_kept, ff_given)
-    ff_owned = lax.psum_scatter(ff_both, "tensor", scatter_dimension=0, tiled=False)
-    mixed_terms = dot(after(hidden, middle_low, ff_both), down_full, (1, 1))
-    middle_all, context, mixed_terms = lax.optimization_barrier(
-        (middle_all, context, mixed_terms)
-    )
+    middle_near = gather_near(middle_low)
+    mixed_terms = dot(after(hidden, middle_low), down_full, (1, 1))
+    middle_near, mixed_terms = lax.optimization_barrier((middle_near, mixed_terms))
+    middle_pieces = gather_far(*middle_near)
+    middle_pieces, mixed_terms = lax.optimization_barrier((middle_pieces, mixed_terms))
     mixed = scatter_far(mixed_terms)
 
-    context_grad = dot(out_part, middle_all, (0, 1)).astype(low)
-    qkv_grad = attend_grad(facts, qkv, context_grad, logs, planes, quarter)
-    qkv_grad, mixed = lax.optimization_barrier((qkv_grad, mixed))
+    context_grad = jnp.concatenate(
+        [dot(out_part, piece, (0, 1)).astype(low) for piece in middle_pieces], axis=1
+    )
+    begun = attend_grad(facts, qkv, context_grad, logs, planes, quarter, 0, planes // 2)
+    begun, mixed = lax.optimization_barrier((begun, mixed))
+    mixed = scatter_near(*mixed)
+    qkv_grad = attend_grad(
+        facts, qkv, context_grad, logs, planes, quarter, planes // 2, planes - planes // 2, begun
+    )
+    qkv_grad, ff_owned = lax.optimization_barrier((qkv_grad, ff_owned))
     terms = dot(qkv_grad, qkv_full, (0, 1))
-    qkv_grad_later, middle_later = after((qkv_grad, middle_all), terms)
-    normed_grad = scatter_near(*scatter_far(terms))
+    qkv_grad_later, middle_pieces = after((qkv_grad, middle_pieces), terms)
+    terms = scatter_far(terms)
     qkv_weight_grad = dot(normed_all, qkv_grad_later, (0, 1)).astype(low)
-    out_grad = dot(middle_later, context, (0, 1)).astype(low)
+    out_grad = dot(jnp.concatenate(middle_pieces), context, (0, 1)).astype(low)
+    output = (middle + mixed + down_shift).astype(low)
+    terms, qkv_weight_grad, out_grad, output = lax.optimization_barrier(
+        (terms, qkv_weight_grad, out_grad, output)
+    )
+    normed_grad = scatter_near(*terms)
+    output_got = enter_plane(split(output), planes)
     qkv_shift_grad = jnp.sum(qkv_grad_later, axis=1, dtype=full).reshape(planes, SLOT)
     columns = 4 * HEAD_DIM
     sums = [gain_two_grad, bias_two_grad, jnp.sum(middle_grad, axis=0), jnp.sum(grad_out, axis=0)]
@@ -957,21 +1013,24 @@
         [qkv_weight_grad, out_grad],
         core_word,
         planes,
+        FOLD,
         jnp.pad(by_owner, ((0, 0), (0, 0), (0, EXTRA - len(sums)), (0, columns - rows_of))),
         jnp.pad(shifts, ((0, 0), (8, EXTRA - 10), (0, 0))),
     )
     heads_both, ff_owned = lax.optimization_barrier(
         (over_cores(heads_kept, heads_given), ff_owned)
     )
-    heads_owned = lax.psum_scatter(heads_both, "tensor", scatter_dimension=0, tiled=False)
-    normed_grad = after(normed_grad, heads_given)
-    mixed = scatter_near(*after(mixed, normed_grad))
-    output = (middle + mixed + down_shift).astype(low)
     tokens_part, gain_one_grad, bias_one_grad = norm_back(rows, gain_one, normed_grad)
     tokens_grad = (middle_grad + tokens_part).astype(low)
-    tokens_grad_home = from_plane(tokens_grad, seat, plane, planes)
-    output_home = from_plane(output, seat, plane, planes)
+    tokens_grad, heads_both, output_got = lax.optimization_barrier(
+        (tokens_grad, heads_both, output_got)
+    )
+    heads_owned = lax.psum_scatter(heads_both, "tensor", scatter_dimension=0, tiled=False)
+    tokens_grad_got = enter_plane(split(tokens_grad), planes)
     ones = jnp.concatenate([gain_one_grad, bias_one_grad])
+    tokens_grad_got, ones = lax.optimization_barrier((tokens_grad_got, ones))
+    output_home = enter_seat(output_got, seat, plane).reshape(quarter, width)
+    tokens_grad_home = enter_seat(tokens_grad_got, seat, plane).reshape(quarter, width)
     ones = ones + core_swap(ones)
     for bits in (1, 2):
         ones = ones + seat_swap(ones, bits)
@@ -982,13 +1041,14 @@
     )
 
     up_home, down_home = finish_grads(
-        [(0, hidden_of), (hidden_of, hidden_of)], seat_home(ff_owned, seat), seat_word, 0
+        [(0, hidden_of), (hidden_of, hidden_of)], seat_home(ff_owned, seat), seat_word, 0, 1
     )
     query_home, key_home, value_home, out_home, rest = finish_grads(
         [(k * HEAD_DIM, HEAD_DIM) for k in range(4)],
         seat_home(heads_owned, seat),
         seat_word,
         EXTRA,
+        FOLD,
     )
     sums = jnp.sum(rest[:, :4, :rows_of], axis=0)
     query_shift_home = rest[:, 8, :HEAD_DIM].reshape(wide)

time: 477 us -> 453 us (0.950)
  starting transfers between devices: 103 us -> 91.8 us
  local copies, waits for them, and re-layouts: 58.7 us -> 47.7 us
  matrix products: 52.2 us -> 44.5 us
  waiting for transfers between devices: 160 us -> 167 us
    ppermute x14, starting transfers between devices: 35.1 us -> 20.2 us  [plane_swap(): lax.ppermute(values, 'tensor', [(k, k ^ bits) for k in range(planes)])]
    all_gather x1, waiting for transfers between devices: 0.01 us -> 9.59 us  [plane_local(): ff_around = lax.all_gather(ff_pieces, group, axis=0)]
    ppermute x14, waiting for transfers between devices: 59.4 us -> 51.2 us  [plane_swap(): lax.ppermute(values, 'tensor', [(k, k ^ bits) for k in range(planes)])]
    dot_general x12 -> x16, matrix products: 52.2 us -> 44.5 us  [dot(): lax.dot_general(left, right, (((dims[0],), (dims[1],)), ((), ())), prefer...]
    ppermute x58, waiting for transfers between devices: 99.6 us -> 105 us  [seat_swap(): return lax.ppermute(values, 'seat', [(k, k ^ bits) for k in range(SEATS)])]
    unnamed x101 -> x125, local copies, waits for them, and re-layouts: 28.4 us -> 24.8 us
    pallas_call x1 -> x2, Pallas kernels: 17.1 us -> 17.8 us  [attend_grad(): pl.pallas_call(kernel, out_shape=jax.ShapeDtypeStruct((planes * SLOT, seq...]
  transfers between devices with their start and end apart: 79 -> 79, of which waited for: 39 -> 42; matrix products, arithmetic and copies ran while one was open for 21% -> 16% of each run, Pallas kernels for 8% -> 8%
where the time goes in v4:
time: 453 us; the launch traced here: 446 us
  waiting for transfers between devices  167 us (37%)
  starting transfers between devices  91.8 us (20%)
  local copies, waits for them, and re-layouts  47.7 us (11%)
  matrix products  44.5 us (10%)
  Pallas kernels  42.1 us (9%)
  other arithmetic  35.4 us (8%)
  between operations  17.3 us (4%)
    ppermute x58, waiting for transfers between devices, seat_swap(): return lax.ppermute(values, 'seat', [(k, k ^ bits) for k in range(SEATS)])  105 us
    ppermute x58, starting transfers between devices, seat_swap(): return lax.ppermute(values, 'seat', [(k, k ^ bits) for k in range(SEATS)])  71.1 us
    ppermute x14, waiting for transfers between devices, plane_swap(): lax.ppermute(values, 'tensor', [(k, k ^ bits) for k in range(planes)])  51.2 us
    dot_general x16, matrix products, dot(): lax.dot_general(left, right, (((dims[0],), (dims[1],)), ((), ())), prefer...  44.5 us
    unnamed x125, local copies, waits for them, and re-layouts  24.8 us
    ppermute x14, starting transfers between devices, plane_swap(): lax.ppermute(values, 'tensor', [(k, k ^ bits) for k in range(planes)])  20.2 us
    pallas_call x2, Pallas kernels, attend_grad(): pl.pallas_call(kernel, out_shape=jax.ShapeDtypeStruct((planes * SLOT, seq...  17.8 us
    pallas_call x1, Pallas kernels, attend(): pl.pallas_call(kernel, out_shape=[jax.ShapeDtypeStruct((planes * HEAD_DIM...  12.5 us
  transfers between devices with their start and end apart: 79, of which 42 were waited for; matrix products, arithmetic and copies ran while one was open for 16% of the time, Pallas kernels for 8%

profile of v4, /device:TPU:0, one launch (start us, length us, event | category | flops | bytes accessed | tf_op | source)
XLA Modules:
  0.0 445.9 jit_solution(2080557440991519957)
XLA Ops:
  8.5 4.0 collective-permute-start.2
  13.7 4.1 concatenate.54
  28.0 4.1 collective-permute-start.8
  33.7 3.4 collective-permute-done.8
  37.2 7.1 %collective-permute-done.7 = bf16[64,1280]{1,0:T(8,128)(2,1)S(1)} collective-permute-done((bf16[64,1280]{1,0:T(8,128)(2,1)S(1)}, bf16[64,1280]{1,0:T(8,128)(2,1)S(1)}, u32[]{:S(2)}, u32[]{:S(2)}) %collective-permute-start.7) | collective-permute-done | bytes 163872 | tf_op jit(solution)/shard_map/ppermute | solution.py:45
  47.8 12.4 %collective-permute-done.9 = bf16[256,1280]{1,0:T(8,128)(2,1)S(1)} collective-permute-done((bf16[256,1280]{1,0:T(8,128)(2,1)S(1)}, bf16[256,1280]{1,0:T(8,128)(2,1)S(1)}, u32[]{:S(2)}, u32[]{:S(2)}) %collective-permute-start.9) | collective-permute-done | bytes 655392 | tf_op jit(solution)/shard_map/ppermute | solution.py:37
  73.8 10.0 %collective-permute-done.21 = bf16[160,640]{1,0:T(8,128)(2,1)S(1)} collective-permute-done((bf16[160,640]{1,0:T(8,128)(2,1)S(1)}, bf16[160,640]{1,0:T(8,128)(2,1)S(1)}, u32[]{:S(2)}, u32[]{:S(2)}) %collective-permute-start.21) | collective-permute-done | bytes 204832 | tf_op jit(solution)/shard_map/ppermute | solution.py:37
  99.1 4.3 collective-permute-start.16
  103.4 4.0 add_convert_fusion.1.qkv_ref
  107.9 6.0 %collective-permute-done.17 = bf16[64,1280]{1,0:T(8,128)(2,1)S(1)} collective-permute-done((bf16[64,1280]{1,0:T(8,128)(2,1)S(1)}, bf16[64,1280]{1,0:T(8,128)(2,1)S(1)}, u32[]{:S(2)}, u32[]{:S(2)}) %collective-permute-start.17) | collective-permute-done | bytes 163872 | tf_op jit(solution)/shard_map/ppermute | solution.py:45
  123.2 12.5 %attend.1 = (bf16[320,1024]{1,0:T(8,128)(2,1)S(1)}, f32[4,1,1024]{2,1,0:T(1,128)S(1)}) custom-call(s32[3]{0:T(128)S(1)} %pad_add_fusion.facts_ref, bf16[1024,1024]{1,0:T(8,128)(2,1)S(1)} %add_convert_fusion.1.qkv_ref), custom_call_target="tpu_custom_call" | custom-call | tf_op jit(solution)/shard_map/attend/pallas_call | solution.py:358
  155.7 11.3 %collective-permute-done.27 = bf16[256,1280]{1,0:T(8,128)(2,1)S(1)} collective-permute-done((bf16[256,1280]{1,0:T(8,128)(2,1)S(1)}, bf16[256,1280]{1,0:T(8,128)(2,1)S(1)}, u32[]{:S(2)}, u32[]{:S(2)}) %collective-permute-start.27) | collective-permute-done | bytes 655392 | tf_op jit(solution)/shard_map/ppermute | solution.py:37
  172.3 9.6 %all-gather.7.cloned.1.call-done = bf16[32,160,640]{2,1,0:T(8,128)(2,1)} async-done(((bf16[4,160,640]{2,1,0:T(8,128)(2,1)}), bf16[32,160,640]{2,1,0:T(8,128)(2,1)}) %all-gather.7.cloned.1.call-update) | async-done | bytes 6553616 | tf_op jit(solution)/shard_map/all_gather | solution.py:923
  187.0 3.6 fusion.54
  199.1 3.6 collective-permute-done.32
  206.1 6.5 %multiply_convert_fusion = (bf16[1024,1280]{1,0:T(8,128)(2,1)S(1)}, bf16[1024,1280]{1,0:T(8,128)(2,1)S(1)}) fusion(f32[1280]{0:T(1024)S(1)} %add.302, f32[1024,1280]{1,0:T(8,128)S(1)} %fusion.54, bf16[1024,1280]{1,0:T(8,128)(2,1)S(1)} %constant_dynamic-update-slice_fusion.10, bf16[1280,1280]{1,0:T(8,128)(2,1)S(1)} %get-tuple-element.154), kind=kOutput, calls=%fused_computation.19 | convolution fusion | flops 3372482560 | bytes 16389120 | tf_op jit(solution)/shard_map/dot_general | solution.py:31
  212.6 3.6 fusion.52
  218.4 3.9 convolution_convert_fusion.1.refs_0_
  225.7 3.9 convolution_convert_fusion.refs_1_
  234.9 14.2 %collective-permute-done.37 = bf16[256,1280]{1,0:T(8,128)(2,1)S(1)} collective-permute-done((bf16[256,1280]{1,0:T(8,128)(2,1)S(1)}, bf16[256,1280]{1,0:T(8,128)(2,1)S(1)}, u32[]{:S(2)}, u32[]{:S(2)}) %collective-permute-start.37) | collective-permute-done | bytes 655392 | tf_op jit(solution)/shard_map/ppermute | solution.py:37
  260.9 3.6 fusion.55
  264.5 10.2 %collective-permute-done.39 = bf16[256,1280]{1,0:T(8,128)(2,1)S(1)} collective-permute-done((bf16[256,1280]{1,0:T(8,128)(2,1)S(1)}, bf16[256,1280]{1,0:T(8,128)(2,1)S(1)}, u32[]{:S(2)}, u32[]{:S(2)}) %collective-permute-start.39) | collective-permute-done | bytes 655392 | tf_op jit(solution)/shard_map/ppermute | solution.py:37
  277.9 6.0 %collective-permute-done.41 = bf16[128,1280]{1,0:T(8,128)(2,1)S(1)} collective-permute-done((bf16[128,1280]{1,0:T(8,128)(2,1)S(1)}, bf16[128,1280]{1,0:T(8,128)(2,1)S(1)}, u32[]{:S(2)}, u32[]{:S(2)}) %collective-permute-start.41) | collective-permute-done | bytes 327712 | tf_op jit(solution)/shard_map/ppermute | solution.py:37
  290.1 9.0 %attend_grad.2.refs_0_ = bf16[1024,1024]{1,0:T(8,128)(2,1)S(1)} custom-call(s32[3]{0:T(128)S(1)} %pad_add_fusion.facts_ref, bf16[1024,1024]{1,0:T(8,128)(2,1)S(1)} %add_convert_fusion.1.qkv_ref, bf16[320,1024]{1,0:T(8,128)(2,1)S(1)} %fusion.31.grad_ref, f32[4,1,1024]{2,1,0:T(1,128)S(1)} %get-tuple-element.170.log_ref), custom_call_target="tpu_custom_call" | custom-call | tf_op jit(solution)/shard_map/attend_grad/pallas_call | solution.py:409
  306.7 8.8 %attend_grad.3 = bf16[1024,1024]{1,0:T(8,128)(2,1)S(1)} custom-call(s32[3]{0:T(128)S(1)} %pad_add_fusion.facts_ref, bf16[1024,1024]{1,0:T(8,128)(2,1)S(1)} %add_convert_fusion.1.qkv_ref, bf16[320,1024]{1,0:T(8,128)(2,1)S(1)} %copy-done.8, f32[4,1,1024]{2,1,0:T(1,128)S(1)} %get-tuple-element.170.log_ref, ...), custom_call_target="tpu_custom_call", output_to_operand_aliasing={{}: (4, {})} | custom-call | tf_op jit(solution)/shard_map/attend_grad/pallas_call | solution.py:409
  319.4 4.7 %fusion.53 = (bf16[1024,1280]{1,0:T(8,128)(2,1)S(1)}, f32[1024,1280]{1,0:T(8,128)S(1)}) fusion(bf16[1024,1024]{1,0:T(8,128)(2,1)S(1)} %copy-done.3, bf16[1280,1024]{1,0:T(8,128)(2,1)} %copy-done.20), kind=kOutput, calls=%fused_computation.207 | convolution fusion | flops 2685665280 | bytes 12582912 | tf_op jit(solution)/shard_map/dot_general | solution.py:31
  328.2 5.3 %convolution_convert_fusion.2.refs_0_ = bf16[1280,1024]{1,0:T(8,128)(2,1)} fusion(bf16[1024,1024]{1,0:T(8,128)(2,1)S(1)} %copy-done.3, bf16[1024,1280]{1,0:T(8,128)(2,1)S(1)} %copy-done.30, f32[1280]{0:T(1024)S(1)} %add.281, f32[1280]{0:T(1024)S(1)} %mul.160, f32[1024]{0:T(1024)S(1)} %add_rsqrt_fusion, f32[1024]{0:T(1024)S(1)} %broadcast_multiply_fusion), kind=kOutput, calls=%fused_computation.23 | convolution fusion | flops 2693529600 | bytes 7358464 | tf_op jit(solution)/shard_map/dot_general | solution.py:31
  348.7 7.8 %collective-permute-done.53 = bf16[64,1280]{1,0:T(8,128)(2,1)S(1)} collective-permute-done((bf16[64,1280]{1,0:T(8,128)(2,1)}, bf16[64,1280]{1,0:T(8,128)(2,1)S(1)}, u32[]{:S(2)}, u32[]{:S(2)}) %collective-permute-start.53) | collective-permute-done | bytes 163872 | tf_op jit(solution)/shard_map/ppermute | solution.py:45
  366.6 4.6 %collective-permute-done.60 = bf16[64,1280]{1,0:T(8,128)(2,1)S(1)} collective-permute-done((bf16[64,1280]{1,0:T(8,128)(2,1)S(1)}, bf16[64,1280]{1,0:T(8,128)(2,1)S(1)}, u32[]{:S(2)}, u32[]{:S(2)}) %collective-permute-start.60) | collective-permute-done | bytes 163872 | tf_op jit(solution)/shard_map/ppermute | solution.py:45
  371.2 17.2 %collective-permute-done.59 = bf16[64,1280]{1,0:T(8,128)(2,1)S(1)} collective-permute-done((bf16[64,1280]{1,0:T(8,128)(2,1)S(1)}, bf16[64,1280]{1,0:T(8,128)(2,1)S(1)}, u32[]{:S(2)}, u32[]{:S(2)}) %collective-permute-start.59) | collective-permute-done | bytes 163872 | tf_op jit(solution)/shard_map/ppermute | solution.py:45
  403.4 3.4 collective-permute-start.73
  411.5 8.0 %collective-permute-done.73.refs_2_ = bf16[160,640]{1,0:T(8,128)(2,1)S(1)} collective-permute-done((bf16[160,640]{1,0:T(8,128)(2,1)S(1)}, bf16[160,640]{1,0:T(8,128)(2,1)S(1)}, u32[]{:S(2)}, u32[]{:S(2)}) %collective-permute-start.73) | collective-permute-done | bytes 204832 | tf_op jit(solution)/shard_map/ppermute | solution.py:37
  (410 shorter events, 208.2 us)
Async XLA Ops:
  7.2 81.3 %all-gather.5.cloned.1.call-start = ((), (), s32[]{:S(2)}) async-start(), calls=%async_computation.4 | async-start | bytes 4055040 | tf_op jit(solution)/shard_map/all_gather | solution.py:884
  8.5 15.8 %collective-permute-start.2 = (bf16[64,1280]{1,0:T(8,128)(2,1)S(1)}, bf16[64,1280]{1,0:T(8,128)(2,1)S(1)}, u32[]{:S(2)}, u32[]{:S(2)}) collective-permute-start(bf16[64,1280]{1,0:T(8,128)(2,1)S(1)} %get-tuple-element.297), channel_id=1, source_target_pairs={{0,24},{8,16},{16,8},{24,0},{1,25},{9,17},{17,9},{25,1},{2,26},{10... | collective-permute-start | bytes 491528 | tf_op jit(solution)/shard_map/ppermute | solution.py:37
  44.4 137.5 %all-gather.7.cloned.1.call-start = ((), (), s32[]{:S(2)}) async-start(), calls=%async_computation.5 | async-start | bytes 7372800 | tf_op jit(solution)/shard_map/all_gather | solution.py:923
  44.4 15.8 %collective-permute-start.9 = (bf16[256,1280]{1,0:T(8,128)(2,1)S(1)}, bf16[256,1280]{1,0:T(8,128)(2,1)S(1)}, u32[]{:S(2)}, u32[]{:S(2)}) collective-permute-start(bf16[256,1280]{1,0:T(8,128)(2,1)S(1)} %bitcast.154), channel_id=1, source_target_pairs={{0,8},{8,0},{16,24},{24,16},{1,9},{9,1},{17,25},{25,17},{2,10},{10... | collective-permute-start | bytes 1966088 | tf_op jit(solution)/shard_map/ppermute | solution.py:37
  46.0 15.5 %collective-permute-start.10 = (bf16[256,1280]{1,0:T(8,128)(2,1)S(1)}, bf16[256,1280]{1,0:T(8,128)(2,1)S(1)}, u32[]{:S(2)}, u32[]{:S(2)}) collective-permute-start(bf16[256,1280]{1,0:T(8,128)(2,1)S(1)} %bitcast.155), channel_id=1, source_target_pairs={{0,16},{8,24},{16,0},{24,8},{1,17},{9,25},{17,1},{25,9},{2,18},{10... | collective-permute-start | bytes 1966088 | tf_op jit(solution)/shard_map/ppermute | solution.py:37
  65.1 22.0 %collective-permute-start.14 = (bf16[128,1280]{1,0:T(8,128)(2,1)S(1)}, bf16[128,1280]{1,0:T(8,128)(2,1)S(1)}, u32[]{:S(2)}, u32[]{:S(2)}) collective-permute-start(bf16[128,1280]{1,0:T(8,128)(2,1)S(1)} %slice.255), channel_id=1, source_target_pairs={{0,16},{8,24},{16,0},{24,8},{1,17},{9,25},{17,1},{25,9},{2,18},{10... | collective-permute-start | bytes 983048 | tf_op jit(solution)/shard_map/ppermute | solution.py:37
  66.7 21.1 %collective-permute-start.15 = (bf16[128,1280]{1,0:T(8,128)(2,1)S(1)}, bf16[128,1280]{1,0:T(8,128)(2,1)S(1)}, u32[]{:S(2)}, u32[]{:S(2)}) collective-permute-start(bf16[128,1280]{1,0:T(8,128)(2,1)S(1)} %slice.256), channel_id=1, source_target_pairs={{0,8},{8,0},{16,24},{24,16},{1,9},{9,1},{17,25},{25,17},{2,10},{10... | collective-permute-start | bytes 983048 | tf_op jit(solution)/shard_map/ppermute | solution.py:37
  114.8 204.5 %reduce-scatter.3.cloned.1.call-start = ((), (), s32[]{:S(2)}) async-start(), calls=%async_computation.2 | async-start | bytes 4096000 | tf_op jit(solution)/shard_map/reduce_scatter | solution.py:971
  116.3 19.4 %collective-permute-start.22 = (bf16[256,1280]{1,0:T(8,128)(2,1)}, bf16[256,1280]{1,0:T(8,128)(2,1)}, u32[]{:S(2)}, u32[]{:S(2)}) collective-permute-start(bf16[256,1280]{1,0:T(8,128)(2,1)} %bitcast.161), channel_id=1, source_target_pairs={{0,8},{8,0},{16,24},{24,16},{1,9},{9,1},{17,25},{25,17},{2,10},{10... | collective-permute-start | bytes 1966088 | tf_op jit(solution)/shard_map/ppermute | solution.py:37
  117.9 17.9 %collective-permute-start.23 = (bf16[256,1280]{1,0:T(8,128)(2,1)}, bf16[256,1280]{1,0:T(8,128)(2,1)}, u32[]{:S(2)}, u32[]{:S(2)}) collective-permute-start(bf16[256,1280]{1,0:T(8,128)(2,1)} %bitcast.162), channel_id=1, source_target_pairs={{0,16},{8,24},{16,0},{24,8},{1,17},{9,25},{17,1},{25,9},{2,18},{10... | collective-permute-start | bytes 1966088 | tf_op jit(solution)/shard_map/ppermute | solution.py:37
  139.6 15.5 %collective-permute-start.30 = (bf16[128,1280]{1,0:T(8,128)(2,1)S(1)}, bf16[128,1280]{1,0:T(8,128)(2,1)S(1)}, u32[]{:S(2)}, u32[]{:S(2)}) collective-permute-start(bf16[128,1280]{1,0:T(8,128)(2,1)S(1)} %slice.273), channel_id=1, source_target_pairs={{0,16},{8,24},{16,0},{24,8},{1,17},{9,25},{17,1},{25,9},{2,18},{10... | collective-permute-start | bytes 983048 | tf_op jit(solution)/shard_map/ppermute | solution.py:37
  148.9 18.1 %collective-permute-start.27 = (bf16[256,1280]{1,0:T(8,128)(2,1)S(1)}, bf16[256,1280]{1,0:T(8,128)(2,1)S(1)}, u32[]{:S(2)}, u32[]{:S(2)}) collective-permute-start(bf16[256,1280]{1,0:T(8,128)(2,1)S(1)} %pad_maximum_fusion.6), channel_id=1, source_target_pairs={{0,16},{8,24},{16,0},{24,8},{1,17},{9,25},{17,1},{25,9},{2,18},{10... | collective-permute-start | bytes 1966088 | tf_op jit(solution)/shard_map/ppermute | solution.py:37
  150.5 16.8 %collective-permute-start.25 = (bf16[256,1280]{1,0:T(8,128)(2,1)S(1)}, bf16[256,1280]{1,0:T(8,128)(2,1)S(1)}, u32[]{:S(2)}, u32[]{:S(2)}) collective-permute-start(bf16[256,1280]{1,0:T(8,128)(2,1)S(1)} %pad_maximum_fusion.5), channel_id=1, source_target_pairs={{0,8},{8,0},{16,24},{24,16},{1,9},{9,1},{17,25},{25,17},{2,10},{10... | collective-permute-start | bytes 1966088 | tf_op jit(solution)/shard_map/ppermute | solution.py:37
  170.2 20.4 %collective-permute-start.28 = (bf16[256,1280]{1,0:T(8,128)(2,1)}, bf16[256,1280]{1,0:T(8,128)(2,1)}, u32[]{:S(2)}, u32[]{:S(2)}) collective-permute-start(bf16[256,1280]{1,0:T(8,128)(2,1)} %add_convert_fusion.4), channel_id=1, source_target_pairs={{0,8},{8,0},{16,24},{24,16},{1,9},{9,1},{17,25},{25,17},{2,10},{10... | collective-permute-start | bytes 1966088 | tf_op jit(solution)/shard_map/ppermute | solution.py:37
  170.8 19.8 %collective-permute-start.29 = (bf16[256,1280]{1,0:T(8,128)(2,1)}, bf16[256,1280]{1,0:T(8,128)(2,1)}, u32[]{:S(2)}, u32[]{:S(2)}) collective-permute-start(bf16[256,1280]{1,0:T(8,128)(2,1)} %add_convert_fusion.4), channel_id=1, source_target_pairs={{0,16},{8,24},{16,0},{24,8},{1,17},{9,25},{17,1},{25,9},{2,18},{10... | collective-permute-start | bytes 1966088 | tf_op jit(solution)/shard_map/ppermute | solution.py:37
  231.8 19.6 %collective-permute-start.38 = (bf16[4,4,160,640]{3,2,1,0:T(8,128)(2,1)S(1)}, bf16[4,4,160,640]{3,2,1,0:T(8,128)(2,1)S(1)}, u32[]{:S(2)}, u32[]{:S(2)}) collective-permute-start(bf16[4,4,160,640]{3,2,1,0:T(8,128)(2,1)S(1)} %get-tuple-element.158), channel_id=1, source_target_pairs={{0,4},{4,0},{1,5},{5,1},{2,6},{6,2},{3,7},{7,3},{8,12},{12,8},{9,1... | collective-permute-start | bytes 9830408 | tf_op jit(solution)/shard_map/ppermute | solution.py:41
  231.9 17.1 %collective-permute-start.37 = (bf16[256,1280]{1,0:T(8,128)(2,1)S(1)}, bf16[256,1280]{1,0:T(8,128)(2,1)S(1)}, u32[]{:S(2)}, u32[]{:S(2)}) collective-permute-start(bf16[256,1280]{1,0:T(8,128)(2,1)S(1)} %pad_maximum_fusion.8), channel_id=1, source_target_pairs={{0,16},{8,24},{16,0},{24,8},{1,17},{9,25},{17,1},{25,9},{2,18},{10... | collective-permute-start | bytes 1966088 | tf_op jit(solution)/shard_map/ppermute | solution.py:37
  233.4 16.8 %collective-permute-start.35 = (bf16[256,1280]{1,0:T(8,128)(2,1)S(1)}, bf16[256,1280]{1,0:T(8,128)(2,1)S(1)}, u32[]{:S(2)}, u32[]{:S(2)}) collective-permute-start(bf16[256,1280]{1,0:T(8,128)(2,1)S(1)} %pad_maximum_fusion.7), channel_id=1, source_target_pairs={{0,8},{8,0},{16,24},{24,16},{1,9},{9,1},{17,25},{25,17},{2,10},{10... | collective-permute-start | bytes 1966088 | tf_op jit(solution)/shard_map/ppermute | solution.py:37
  254.1 172.1 %reduce-scatter.5.cloned.1.call-start = ((), (), s32[]{:S(2)}) async-start(), calls=%async_computation.3 | async-start | bytes 2252800 | tf_op jit(solution)/shard_map/reduce_scatter | solution.py:1028
  258.8 16.0 %collective-permute-start.39 = (bf16[256,1280]{1,0:T(8,128)(2,1)S(1)}, bf16[256,1280]{1,0:T(8,128)(2,1)S(1)}, u32[]{:S(2)}, u32[]{:S(2)}) collective-permute-start(bf16[256,1280]{1,0:T(8,128)(2,1)S(1)} %convert_element_type.192), channel_id=1, source_target_pairs={{0,8},{8,0},{16,24},{24,16},{1,9},{9,1},{17,25},{25,17},{2,10},{10... | collective-permute-start | bytes 1966088 | tf_op jit(solution)/shard_map/ppermute | solution.py:37
  260.2 15.7 %collective-permute-start.40 = (bf16[256,1280]{1,0:T(8,128)(2,1)S(1)}, bf16[256,1280]{1,0:T(8,128)(2,1)S(1)}, u32[]{:S(2)}, u32[]{:S(2)}) collective-permute-start(bf16[256,1280]{1,0:T(8,128)(2,1)S(1)} %convert_element_type.192), channel_id=1, source_target_pairs={{0,16},{8,24},{16,0},{24,8},{1,17},{9,25},{17,1},{25,9},{2,18},{10... | collective-permute-start | bytes 1966088 | tf_op jit(solution)/shard_map/ppermute | solution.py:37
  301.1 15.7 %collective-permute-start.48 = (bf16[256,1280]{1,0:T(8,128)(2,1)}, bf16[256,1280]{1,0:T(8,128)(2,1)}, u32[]{:S(2)}, u32[]{:S(2)}) collective-permute-start(bf16[256,1280]{1,0:T(8,128)(2,1)} %pad_maximum_fusion.10), channel_id=1, source_target_pairs={{0,16},{8,24},{16,0},{24,8},{1,17},{9,25},{17,1},{25,9},{2,18},{10... | collective-permute-start | bytes 1966088 | tf_op jit(solution)/shard_map/ppermute | solution.py:37
  301.7 15.1 %collective-permute-start.47 = (bf16[256,1280]{1,0:T(8,128)(2,1)}, bf16[256,1280]{1,0:T(8,128)(2,1)}, u32[]{:S(2)}, u32[]{:S(2)}) collective-permute-start(bf16[256,1280]{1,0:T(8,128)(2,1)} %pad_maximum_fusion.9), channel_id=1, source_target_pairs={{0,8},{8,0},{16,24},{24,16},{1,9},{9,1},{17,25},{25,17},{2,10},{10... | collective-permute-start | bytes 1966088 | tf_op jit(solution)/shard_map/ppermute | solution.py:37
  338.4 19.2 %collective-permute-start.50 = (bf16[256,1280]{1,0:T(8,128)(2,1)}, bf16[256,1280]{1,0:T(8,128)(2,1)}, u32[]{:S(2)}, u32[]{:S(2)}) collective-permute-start(bf16[256,1280]{1,0:T(8,128)(2,1)} %pad_maximum_fusion.12), channel_id=1, source_target_pairs={{0,16},{8,24},{16,0},{24,8},{1,17},{9,25},{17,1},{25,9},{2,18},{10... | collective-permute-start | bytes 1966088 | tf_op jit(solution)/shard_map/ppermute | solution.py:37
  339.1 18.5 %collective-permute-start.49 = (bf16[256,1280]{1,0:T(8,128)(2,1)}, bf16[256,1280]{1,0:T(8,128)(2,1)}, u32[]{:S(2)}, u32[]{:S(2)}) collective-permute-start(bf16[256,1280]{1,0:T(8,128)(2,1)} %pad_maximum_fusion.11), channel_id=1, source_target_pairs={{0,8},{8,0},{16,24},{24,16},{1,9},{9,1},{17,25},{25,17},{2,10},{10... | collective-permute-start | bytes 1966088 | tf_op jit(solution)/shard_map/ppermute | solution.py:37
  345.0 15.3 %collective-permute-start.51 = (bf16[4,4,88,640]{3,2,1,0:T(8,128)(2,1)S(1)}, bf16[4,4,88,640]{3,2,1,0:T(8,128)(2,1)S(1)}, u32[]{:S(2)}, u32[]{:S(2)}) collective-permute-start(bf16[4,4,88,640]{3,2,1,0:T(8,128)(2,1)S(1)} %get-tuple-element.190), channel_id=1, source_target_pairs={{0,4},{4,0},{1,5},{5,1},{2,6},{6,2},{3,7},{7,3},{8,12},{12,8},{9,1... | collective-permute-start | bytes 5406728 | tf_op jit(solution)/shard_map/ppermute | solution.py:41
  364.1 24.4 %collective-permute-start.59 = (bf16[64,1280]{1,0:T(8,128)(2,1)S(1)}, bf16[64,1280]{1,0:T(8,128)(2,1)S(1)}, u32[]{:S(2)}, u32[]{:S(2)}) collective-permute-start(bf16[64,1280]{1,0:T(8,128)(2,1)S(1)} %get-tuple-element.268), channel_id=1, source_target_pairs={{0,2},{1,3},{2,0},{3,1},{4,6},{5,7},{6,4},{7,5},{8,10},{9,11},{10,... | collective-permute-start | bytes 491528 | tf_op jit(solution)/shard_map/ppermute | solution.py:45
  364.1 24.4 %collective-permute-start.58 = (bf16[64,1280]{1,0:T(8,128)(2,1)S(1)}, bf16[64,1280]{1,0:T(8,128)(2,1)S(1)}, u32[]{:S(2)}, u32[]{:S(2)}) collective-permute-start(bf16[64,1280]{1,0:T(8,128)(2,1)S(1)} %get-tuple-element.269), channel_id=1, source_target_pairs={{0,1},{1,0},{2,3},{3,2},{4,5},{5,4},{6,7},{7,6},{8,9},{9,8},{10,11... | collective-permute-start | bytes 491528 | tf_op jit(solution)/shard_map/ppermute | solution.py:45
  403.4 16.1 %collective-permute-start.73 = (bf16[160,640]{1,0:T(8,128)(2,1)S(1)}, bf16[160,640]{1,0:T(8,128)(2,1)S(1)}, u32[]{:S(2)}, u32[]{:S(2)}) collective-permute-start(bf16[160,640]{1,0:T(8,128)(2,1)S(1)} %get-tuple-element.255), channel_id=1, source_target_pairs={{0,16},{8,24},{16,0},{24,8},{1,17},{9,25},{17,1},{25,9},{2,18},{10... | collective-permute-start | bytes 614408 | tf_op jit(solution)/shard_map/ppermute | solution.py:37
  406.9 17.8 %collective-permute-start.63 = (bf16[64,1280]{1,0:T(8,128)(2,1)S(1)}, bf16[64,1280]{1,0:T(8,128)(2,1)S(1)}, u32[]{:S(2)}, u32[]{:S(2)}) collective-permute-start(bf16[64,1280]{1,0:T(8,128)(2,1)S(1)} %get-tuple-element.263), channel_id=1, source_target_pairs={{0,24},{8,16},{16,8},{24,0},{1,25},{9,17},{17,9},{25,1},{2,26},{10... | collective-permute-start | bytes 491528 | tf_op jit(solution)/shard_map/ppermute | solution.py:37
  409.8 14.9 %collective-permute-start.62 = (bf16[64,1280]{1,0:T(8,128)(2,1)S(1)}, bf16[64,1280]{1,0:T(8,128)(2,1)S(1)}, u32[]{:S(2)}, u32[]{:S(2)}) collective-permute-start(bf16[64,1280]{1,0:T(8,128)(2,1)S(1)} %get-tuple-element.264), channel_id=1, source_target_pairs={{0,16},{8,24},{16,0},{24,8},{1,17},{9,25},{17,1},{25,9},{2,18},{10... | collective-permute-start | bytes 491528 | tf_op jit(solution)/shard_map/ppermute | solution.py:37
  409.8 14.9 %collective-permute-start.61 = (bf16[64,1280]{1,0:T(8,128)(2,1)S(1)}, bf16[64,1280]{1,0:T(8,128)(2,1)S(1)}, u32[]{:S(2)}, u32[]{:S(2)}) collective-permute-start(bf16[64,1280]{1,0:T(8,128)(2,1)S(1)} %get-tuple-element.265), channel_id=1, source_target_pairs={{0,8},{8,0},{16,24},{24,16},{1,9},{9,1},{17,25},{25,17},{2,10},{10... | collective-permute-start | bytes 491528 | tf_op jit(solution)/shard_map/ppermute | solution.py:37
  (101 other events, 896.3 us)
Sparse Core Ops, SparseCore 0:
  44.5 42.1 all-gather.4
  115.0 66.8 all-gather.6
  254.2 60.0 reduce-scatter.2
  362.2 44.9 reduce-scatter.4
